TPU v7x, 512 devices: a whole 4x8x8 slice. The times are simulated.
512 devices in a mesh: seq: 32 (over y, z_lo, core), row: 4 (over x), col: 4 (over z_hi).
Axes of the slice: x: 4, y: 8, z: 8 (z_hi: 4, z_lo: 2; z = z_hi * 2 + z_lo), core: 2. Of those that a mesh axis runs over, the one named last changes fastest.
Arguments:
- hidden_in: bfloat16 [4, 16384, 1024], P('row', 'seq')
- qkv_weight: bfloat16 [1024, 16, 192], P(None, 'col'), may hold values from -0.1875 to 0.1875
- qkv_global_weight: bfloat16 [1024, 16, 192], P('row', 'col'), may hold values from -0.1875 to 0.1875
- out_weight: bfloat16 [1024, 1024], P('col'), may hold values from -0.75 to 0.75
- ln_gain: float32 [1024], replicated, may hold values from 0.1 to 1.9
- ln_bias: float32 [1024], replicated, may hold values from -3 to 3
- ffn_in: bfloat16 [1024, 4096], P('row', 'col'), may hold values from -0.1875 to 0.1875
- ffn_out: bfloat16 [4096, 1024], P('col', 'row'), may hold values from -0.09375 to 0.09375
- ln2_gain: float32 [1024], replicated, may hold values from 0.1 to 1.9
- ln2_bias: float32 [1024], replicated, may hold values from -3 to 3
- segment_ids: int32 [4, 16384], P('row'), may hold values from 0 to 63, never falling along the last dimension, each value on 1 to 9216 neighbouring positions
- global_pos: int32 [4, 128], P('row'), may hold values from 0 to 16383, as said below
- page_owner: int32 [4, 1024, 1], P('row', 'seq'), may hold values from 0 to 31; in each aligned block of 32 rows (0 to 31, 32 to 63, ..., all dimensions but the last counted through in order) at most 2 rows name the same one
Outputs:
- hidden_out: bfloat16 [4, 16384, 1024], P('row', ('seq', 'col'))
- page_pool: bfloat16 [4, 32, 32, 2, 16, 16, 128], P('row', 'seq', None, None, None, 'col')
Inputs may be any that keep to these rules, and one draw needn't show every extreme that they name: `segment_ids`: in each stream, prompt numbers never fall along positions and every prompt has 1 to 9216 tokens, one exactly 9216. `global_pos`: in each stream, exactly 4 distinct global positions lie in each block of 512 consecutive tokens, listed in increasing order. `page_owner`: among the 32 pages of one shard of a stream, at most 2 have the same owner.
All inputs are finite; a program needn't handle non-finite values.
Results may differ from a plain program's by a relative error of at most 0.014.
The roundings to bfloat16 on the way count: a program that leaves them out, or rounds other values in their place, can miss the bound.
Values may be sent and summed in bfloat16 or wider, within the bound.
A program may use at most 64 MiB of HBM per device.

v0:
```python
import math

import jax
import jax.numpy as jnp
from jax import lax
from jax.sharding import PartitionSpec as P

HALF = 256


def padded(block, sides, width):
    for axis, dim in sides:
        count = lax.axis_size(axis)
        forward = [(i, i + 1) for i in range(count - 1)]
        backward = [(target, source) for source, target in forward]
        low = lax.ppermute(
            lax.slice_in_dim(block, block.shape[dim] - width, None, axis=dim), axis, forward
        )
        high = lax.ppermute(lax.slice_in_dim(block, 0, width, axis=dim), axis, backward)
        block = jnp.concatenate([low, block, high], axis=dim)
    return block


def combined_all(array, axis, combine):
    everything = jax.tree.map(lambda part: lax.all_gather(part, axis), array)
    initial = jax.tree.map(lambda part: part[0], everything)

    def lap(k, so_far):
        return combine(so_far, jax.tree.map(lambda part: part[k], everything))

    return lax.fori_loop(1, lax.axis_size(axis), lap, initial)


def combine_parts(first, second):
    top = jnp.maximum(first[0], second[0])
    left = jnp.exp(first[0] - top)
    right = jnp.exp(second[0] - top)
    return (
        top,
        first[1] * left + second[1] * right,
        first[2] * left[:, :, None] + second[2] * right[:, :, None],
    )


def layer_norm(values, gain, bias):
    center = values - jnp.mean(values, axis=1, keepdims=True)
    spread = jnp.mean(center * center, axis=1, keepdims=True)
    return center * lax.rsqrt(spread + 1e-05) * gain + bias


def per_device(
    hidden_in,
    qkv_weight,
    qkv_global_weight,
    out_weight,
    ln_gain,
    ln_bias,
    ffn_in,
    ffn_out,
    ln2_gain,
    ln2_bias,
    segment_ids,
    global_pos,
    page_owner,
):
    neg = -1e30
    tokens = hidden_in[0]
    shard_len, width = tokens.shape
    heads_here = qkv_weight.shape[1]
    triple = qkv_weight.shape[2]
    head_dim = triple // 3
    n_seq = lax.axis_size("seq")
    n_col = lax.axis_size("col")
    seq_index = lax.axis_index("seq")
    col_index = lax.axis_index("col")
    base = seq_index * shard_len
    scale = 1.0 / math.sqrt(head_dim)
    qkv = jnp.dot(
        tokens, qkv_weight.reshape(width, heads_here * triple), preferred_element_type=jnp.float32
    ).astype(jnp.bfloat16)
    qkv_heads = qkv.reshape(shard_len, heads_here, triple)
    queries = qkv_heads[:, :, :head_dim]
    kv_local = qkv_heads[:, :, head_dim:]
    piece = lax.all_gather(qkv_global_weight, "row", axis=0, tiled=True)
    cols = tokens
    global_proj = jnp.dot(
        cols, piece.reshape(piece.shape[0], heads_here * triple), preferred_element_type=jnp.float32
    )
    global_heads = global_proj.astype(jnp.bfloat16).reshape(shard_len, heads_here, triple)
    global_query_local = global_heads[:, :, :head_dim]
    global_kv_local = global_heads[:, :, head_dim:]
    owners = page_owner[0, :, 0]
    n_pages = owners.shape[0]
    page_len = shard_len // n_pages
    capacity = max(2, n_pages // n_seq)
    page_order = jnp.arange(n_pages, dtype=jnp.int32)
    slot = jnp.sum(
        ((owners[:, None] == owners[None, :]) & (page_order[None, :] < page_order[:, None])).astype(
            jnp.int32
        ),
        axis=1,
    )
    target = owners * capacity + slot
    placing = (target[None, :] == jnp.arange(n_seq * capacity, dtype=jnp.int32)[:, None]).astype(
        jnp.bfloat16
    )
    outgoing = jnp.dot(
        placing,
        kv_local.reshape(n_pages, page_len * heads_here * 2 * head_dim),
        preferred_element_type=jnp.float32,
    ).astype(jnp.bfloat16)
    outgoing = outgoing.reshape(n_seq, capacity, page_len, heads_here, 2 * head_dim)
    arrived = lax.all_to_all(outgoing, "seq", split_axis=0, concat_axis=0, tiled=True)
    page_pool = arrived[None, None]
    kv_ext = padded(kv_local, (("seq", 0),), HALF)
    all_pos = global_pos[0]
    n_glob = all_pos.shape[0]
    per_shard = n_glob // n_seq
    own_pos = lax.dynamic_slice_in_dim(all_pos, seq_index * per_shard, per_shard, 0)
    local_order = jnp.arange(shard_len, dtype=jnp.int32)
    own_match = (own_pos - base)[:, None] == local_order[None, :]
    picker = own_match.astype(jnp.bfloat16)
    own_kv = jnp.dot(
        picker,
        kv_local.reshape(shard_len, heads_here * 2 * head_dim),
        preferred_element_type=jnp.float32,
    ).astype(jnp.bfloat16)
    own_query = jnp.dot(
        picker,
        global_query_local.reshape(shard_len, heads_here * head_dim),
        preferred_element_type=jnp.float32,
    ).astype(jnp.bfloat16)
    gathered = (
        lax.all_gather(own_kv, "seq", axis=0, tiled=True),
        lax.all_gather(own_query, "seq", axis=0, tiled=True),
    )
    glob_kv = gathered[0].reshape(n_glob, heads_here, 2 * head_dim)
    glob_q = gathered[1].reshape(n_glob, heads_here, head_dim)
    glob_k = glob_kv[:, :, :head_dim]
    glob_v = glob_kv[:, :, head_dim:]
    seg_all = segment_ids[0]
    glob_seg = jnp.take(seg_all, all_pos)
    seg_pad = jnp.pad(seg_all, (HALF, HALF), constant_values=-1)
    query_seg = lax.dynamic_slice_in_dim(seg_all, base, shard_len, 0)
    key_seg = lax.dynamic_slice_in_dim(seg_pad, base, shard_len + 2 * HALF, 0)
    key_pos = base - HALF + jnp.arange(shard_len + 2 * HALF, dtype=jnp.int32)
    key_flag = jnp.any(key_pos[:, None] == all_pos[None, :], axis=1)
    query_pos = base + local_order
    glob_mask = query_seg[:, None] == glob_seg[None, :]
    block = min(shard_len, 512)
    k_blk = kv_ext[0 : block + 2 * HALF, :, :head_dim]
    v_blk = kv_ext[0 : block + 2 * HALF, :, head_dim:]
    s_win = jnp.einsum("qhd,khd->hqk", queries, k_blk, preferred_element_type=jnp.float32) * scale
    s_glob = jnp.einsum("qhd,ghd->hqg", queries, glob_k, preferred_element_type=jnp.float32) * scale
    m_win = (
        (jnp.abs(query_pos[:, None] - key_pos[None, :]) <= HALF)
        & (query_seg[0:block, None] == key_seg[None, 0 : block + 2 * HALF])
        & jnp.logical_not(key_flag[None, 0 : block + 2 * HALF])
    )
    top = jnp.maximum(
        jnp.max(jnp.where(m_win, s_win, neg), axis=2),
        jnp.max(jnp.where(glob_mask, s_glob, neg), axis=2),
    )
    e_win = jnp.where(m_win, jnp.exp(s_win - top[:, :, None]), 0.0)
    e_glob = jnp.where(glob_mask, jnp.exp(s_glob - top[:, :, None]), 0.0)
    total = jnp.sum(e_win, axis=2) + jnp.sum(e_glob, axis=2)
    numer = jnp.einsum(
        "hqk,khd->qhd", e_win.astype(jnp.bfloat16), v_blk, preferred_element_type=jnp.float32
    )
    numer = numer + jnp.einsum(
        "hqg,ghd->qhd", e_glob.astype(jnp.bfloat16), glob_v, preferred_element_type=jnp.float32
    )
    pieces = (numer / jnp.transpose(total)[:, :, None]).astype(jnp.bfloat16)
    s_part = (
        jnp.einsum(
            "ghd,khd->hgk",
            glob_q,
            global_kv_local[:, :, :head_dim],
            preferred_element_type=jnp.float32,
        )
        * scale
    )
    part_mask = glob_seg[:, None] == query_seg[None, :]
    part_top = jnp.max(jnp.where(part_mask, s_part, neg), axis=2)
    e_part = jnp.where(part_mask, jnp.exp(s_part - part_top[:, :, None]), 0.0)
    part_total = jnp.sum(e_part, axis=2)
    part_acc = jnp.einsum(
        "hgk,khd->hgd",
        e_part,
        global_kv_local[:, :, head_dim:].astype(jnp.float32),
        precision=lax.Precision.HIGHEST,
    )
    merged = combined_all((part_top, part_total, part_acc), "seq", combine_parts)
    glob_out = (merged[2] / merged[1][:, :, None]).astype(jnp.bfloat16)
    own_out = lax.dynamic_slice_in_dim(glob_out, seq_index * per_shard, per_shard, 1)
    placed = jnp.einsum("gt,hgd->thd", picker, own_out, preferred_element_type=jnp.float32).astype(
        jnp.bfloat16
    )
    is_own = jnp.any(own_match, axis=0)
    attention = jnp.where(is_own[:, None, None], placed, pieces).reshape(
        shard_len, heads_here * head_dim
    )
    out_rows = shard_len // n_col
    proj = lax.psum_scatter(
        jnp.dot(attention, out_weight, preferred_element_type=jnp.float32).astype(jnp.bfloat16),
        "col",
        scatter_dimension=0,
        tiled=True,
    ).astype(jnp.float32)
    residual = lax.dynamic_slice_in_dim(tokens, col_index * out_rows, out_rows, 0).astype(
        jnp.float32
    )
    middle = layer_norm(residual + proj, ln_gain, ln_bias).astype(jnp.bfloat16)
    middle_all = lax.all_gather(middle, "col", axis=0, tiled=True)
    cols = middle_all
    ffn_pre = jnp.dot(
        cols, lax.all_gather(ffn_in, "row", axis=0, tiled=True), preferred_element_type=jnp.float32
    )
    ffn_hidden = jax.nn.gelu(ffn_pre, approximate=False).astype(jnp.bfloat16)
    down_full = lax.all_gather(ffn_out, "row", axis=1, tiled=True)
    ffn_part = lax.psum_scatter(
        jnp.dot(ffn_hidden, down_full, preferred_element_type=jnp.float32).astype(jnp.bfloat16),
        "col",
        scatter_dimension=0,
        tiled=True,
    ).astype(jnp.float32)
    second = middle.astype(jnp.float32) + ffn_part
    normed = layer_norm(second, ln2_gain, ln2_bias)
    return (normed.astype(jnp.bfloat16)[None], page_pool)


def solution(mesh):
    in_specs = (
        P("row", "seq", None),
        P(None, "col", None),
        P("row", "col", None),
        P("col", None),
        P(),
        P(),
        P("row", "col"),
        P("col", "row"),
        P(),
        P(),
        P("row", None),
        P("row", None),
        P("row", "seq", None),
    )
    out_specs = (P("row", ("seq", "col"), None), P("row", "seq", None, None, None, "col", None))
    return jax.shard_map(
        per_device, mesh=mesh, in_specs=in_specs, out_specs=out_specs, check_vma=False
    )
```

profile of v0, /device:TPU:1, one launch (start us, length us, event | category | flops | bytes accessed | tf_op | source)
XLA Modules:
  0.0 482.0 jit_solution(8521363212529290202)
XLA Ops:
  8.6 1.8 gather_fusion
  12.6 37.7 %all-gather.13.cloned.1.call-done = bf16[1024,4,192]{0,2,1:T(8,128)(2,1)} async-done(((bf16[256,4,192]{0,2,1:T(8,128)(2,1)}), bf16[1024,4,192]{0,2,1:T(8,128)(2,1)}) %all-gather.13.cloned.1.call-update) | async-done | bytes 1572880 | tf_op jit(solution)/shard_map/all_gather | solution.py:84
  50.3 3.6 convolution_convert_fusion.4
  55.5 35.8 %all-gather.3 = bf16[32,4,256]{2,1,0:T(4,128)(2,1)S(1)} all-gather(bf16[1,4,256]{2,1,0:T(4,128)(2,1)S(1)} %fusion.28), channel_id=1, replica_groups=mesh['seq'=32,'row'=4,'col'=4] {'seq'}, dimensions={0}, use_global_device_ids=true | all-gather | bytes 67584 | tf_op jit(solution)/shard_map/all_gather | solution.py:135
  94.5 3.1 convolution_convert_fusion.3
  99.8 1.9 collective-permute-start
  101.7 3.1 collective-permute-start.1
  105.6 32.0 %all-gather.6 = bf16[32,4,512]{2,1,0:T(4,128)(2,1)S(1)} all-gather(bf16[1,4,512]{2,1,0:T(4,128)(2,1)S(1)} %fusion.27), channel_id=1, replica_groups=mesh['seq'=32,'row'=4,'col'=4] {'seq'}, dimensions={0}, use_global_device_ids=true | all-gather | bytes 135168 | tf_op jit(solution)/shard_map/all_gather | solution.py:134
  140.3 1.7 select_reduce_fusion
  142.2 2.7 fusion.3
  145.3 2.1 fusion.65
  147.8 31.1 %all-gather.5 = f32[32,4,128]{2,1,0:T(4,128)S(1)} all-gather(f32[1,4,128]{2,1,0:T(4,128)S(1)} %bitcast.109), channel_id=3, replica_groups=mesh['seq'=32,'row'=4,'col'=4] {'seq'}, dimensions={0}, use_global_device_ids=true | all-gather | bytes 67584 | tf_op jit(solution)/shard_map/all_gather | solution.py:25
  178.9 33.9 %all-gather.4 = f32[32,4,128]{2,1,0:T(4,128)S(1)} all-gather(f32[1,4,128]{2,1,0:T(4,128)S(1)} %bitcast.108), channel_id=2, replica_groups=mesh['seq'=32,'row'=4,'col'=4] {'seq'}, dimensions={0}, use_global_device_ids=true | all-gather | bytes 67584 | tf_op jit(solution)/shard_map/all_gather | solution.py:25
  213.9 42.2 %while.19 = (s32[]{:T(128)}, f32[4,128]{1,0:T(4,128)S(1)}, f32[4,128]{1,0:T(4,128)S(1)}, f32[4,128,64]{2,1,0:T(8,128)S(1)}, f32[32,4,128]{2,1,0:T(4,128)S(1)}, /...) while((s32[]{:T(128)}, f32[4,128]{1,0:T(4,128)S(1)}, ...), condition=%wide.region_4.5_spmd, body=%wide.region_3.4_spmd.sunk | while | flops 101381 | bytes 938135 | solution.py:31
  256.6 2.6 convolution_convert_fusion.2
  260.4 34.7 %reduce-scatter.3.cloned.1.call-done = bf16[128,1024]{1,0:T(8,128)(2,1)} async-done(((bf16[512,1024]{1,0:T(8,128)(2,1)}), bf16[128,1024]{1,0:T(8,128)(2,1)}) %reduce-scatter.3.cloned.1.call-update) | async-done | bytes 262160 | tf_op jit(solution)/shard_map/reduce_scatter | solution.py:204
  297.3 1.8 add_convert_fusion.1
  300.4 32.8 %all-gather.17.cloned.1.call-done = bf16[1024,1024]{1,0:T(8,128)(2,1)} async-done(((bf16[256,1024]{1,0:T(8,128)(2,1)}), bf16[1024,1024]{1,0:T(8,128)(2,1)}) %all-gather.17.cloned.1.call-update) | async-done | bytes 2097168 | tf_op jit(solution)/shard_map/all_gather | solution.py:217
  333.2 41.2 %all-gather.19.cloned.1.call-done = bf16[1024,1024]{1,0:T(8,128)(2,1)} async-done(((bf16[1024,256]{1,0:T(8,128)(2,1)}), bf16[1024,1024]{1,0:T(8,128)(2,1)}) %all-gather.19.cloned.1.call-update) | async-done | bytes 2097168 | tf_op jit(solution)/shard_map/all_gather | solution.py:220
  374.4 41.6 %all-gather.15.cloned.1.call-done = bf16[512,1024]{1,0:T(8,128)(2,1)} async-done(((bf16[128,1024]{1,0:T(8,128)(2,1)}), bf16[512,1024]{1,0:T(8,128)(2,1)}) %all-gather.15.cloned.1.call-update) | async-done | bytes 1048592 | tf_op jit(solution)/shard_map/all_gather | solution.py:214
  415.9 9.8 %convolution_convert_fusion.1 = bf16[512,1024]{1,0:T(8,128)(2,1)} fusion(bf16[1024,1024]{1,0:T(8,128)(2,1)} %all-gather.19.cloned.1.call-done, bf16[512,1024]{1,0:T(8,128)(2,1)} %all-gather.15.cloned.1.call-done, bf16[1024,1024]{1,0:T(8,128)(2,1)} %all-gather.17.cloned.1.call-done), kind=kOutput, calls=%fused_computation.39 | convolution fusion | flops 2182086656 | bytes 6291456 | tf_op jit(solution)/shard_map/dot_general | solution.py:222
  427.7 37.6 %all_to_all.5 = bf16[32,2,16,4,128]{4,3,2,1,0:T(4,128)(2,1)S(1)} all-to-all(bf16[32,2,16,4,128]{4,3,2,1,0:T(4,128)(2,1)} %reshape.176), channel_id=1, replica_groups=mesh['seq'=32,'row'=4,'col'=4] {'seq'}, dimensions={0} | all-to-all | bytes 2097152 | tf_op jit(solution)/shard_map/all_to_all | solution.py:113
  465.3 4.8 reduce-scatter.5.cloned.1.call-done
  472.4 1.8 fusion.87
  (219 shorter events, 67.4 us)
Async XLA Ops:
  7.2 87.3 %copy-start = (bf16[1024,4,192]{0,2,1:T(8,128)(2,1)S(1)}, bf16[1024,4,192]{0,2,1:T(8,128)(2,1)}, u32[]{:S(2)}) copy-start(bf16[1024,4,192]{0,2,1:T(8,128)(2,1)} %param.16) | copy-start | bytes 4718596
  7.2 43.1 %all-gather.13.cloned.1.call-start = ((), (), s32[]{:S(2)}) async-start(), calls=%async_computation.3 | async-start | bytes 1966080 | tf_op jit(solution)/shard_map/all_gather | solution.py:84
  7.9 204.9 %all-gather.21.cloned.1.call-start = ((), (), s32[]{:S(2)}) async-start(), calls=%async_computation.9 | async-start | bytes 4325376 | tf_op jit(solution)/shard_map/all_gather | solution.py:25
  91.8 1.0 copy-start.3
  94.4 200.6 %reduce-scatter.3.cloned.1.call-start = ((), (), s32[]{:S(2)}) async-start(), calls=%async_computation.4 | async-start | bytes 1310720 | tf_op jit(solution)/shard_map/reduce_scatter | solution.py:204
  97.6 7.3 %copy-start.2 = (s32[1,16384]{1,0:T(1,128)S(1)}, s32[1,16384]{1,0:T(1,128)}, u32[]{:S(2)}) copy-start(s32[1,16384]{1,0:T(1,128)} %param.25) | copy-start | bytes 196612
  97.6 7.3 %copy-start.10 = (s32[1,128]{1,0:T(1,128)S(1)}, s32[1,128]{1,0:T(1,128)}, u32[]{:S(2)}) copy-start(s32[1,128]{1,0:T(1,128)} %param.26) | copy-start | bytes 1540
  99.8 39.3 %collective-permute-start = (bf16[256,4,128]{0,2,1:T(8,128)(2,1)}, bf16[256,4,128]{0,2,1:T(8,128)(2,1)}, u32[]{:S(2)}, u32[]{:S(2)}) collective-permute-start(bf16[256,4,128]{0,2,1:T(8,128)(2,1)} %get-tuple-element.234), channel_id=1, source_target_pairs={{0,16},{16,32},{32,48},{48,64},{64,80},{80,96},{96,112},{112,128},... | collective-permute-start | bytes 786440 | tf_op jit(solution)/shard_map/ppermute | solution.py:16
  101.7 37.4 %collective-permute-start.1 = (bf16[256,4,128]{0,2,1:T(8,128)(2,1)S(1)}, bf16[256,4,128]{0,2,1:T(8,128)(2,1)}, u32[]{:S(2)}, u32[]{:S(2)}) collective-permute-start(bf16[256,4,128]{0,2,1:T(8,128)(2,1)S(1)} %get-tuple-element.235), channel_id=1, source_target_pairs={{16,0},{32,16},{48,32},{64,48},{80,64},{96,80},{112,96},{128,112},... | collective-permute-start | bytes 786440 | tf_op jit(solution)/shard_map/ppermute | solution.py:19
  145.3 2.1 copy-start.4
  256.5 38.5 %copy-start.5 = (bf16[1,512,1024]{2,1,0:T(8,128)(2,1)S(1)}, bf16[1,512,1024]{2,1,0:T(8,128)(2,1)}, u32[]{:S(2)}) copy-start(bf16[1,512,1024]{2,1,0:T(8,128)(2,1)} %param.15) | copy-start | bytes 3145732
  256.5 40.8 %copy-start.6 = (f32[1024]{0:T(1024)S(1)}, f32[1024]{0:T(1024)}, u32[]{:S(2)}) copy-start(f32[1024]{0:T(1024)} %param.20) | copy-start | bytes 12292
  256.5 40.8 %copy-start.7 = (f32[1024]{0:T(1024)S(1)}, f32[1024]{0:T(1024)}, u32[]{:S(2)}) copy-start(f32[1024]{0:T(1024)} %param.19) | copy-start | bytes 12292
  259.1 74.0 %all-gather.17.cloned.1.call-start = ((), (), s32[]{:S(2)}) async-start(), calls=%async_computation.6 | async-start | bytes 2621440 | tf_op jit(solution)/shard_map/all_gather | solution.py:217
  259.7 114.6 %all-gather.19.cloned.1.call-start = ((), (), s32[]{:S(2)}) async-start(), calls=%async_computation.7 | async-start | bytes 2621440 | tf_op jit(solution)/shard_map/all_gather | solution.py:220
  260.3 155.6 %all-gather.15.cloned.1.call-start = ((), (), s32[]{:S(2)}) async-start(), calls=%async_computation.5 | async-start | bytes 1310720 | tf_op jit(solution)/shard_map/all_gather | solution.py:214
  260.4 39.8 %copy-start.11 = (s32[1,32,1]{1,2,0:T(1,128)S(1)}, s32[1,32,1]{1,2,0:T(1,128)}, u32[]{:S(2)}) copy-start(s32[1,32,1]{1,2,0:T(1,128)} %param.27) | copy-start | bytes 388
  299.2 170.9 %reduce-scatter.5.cloned.1.call-start = ((), (), s32[]{:S(2)}) async-start(), calls=%async_computation.8 | async-start | bytes 1310720 | tf_op jit(solution)/shard_map/reduce_scatter | solution.py:221
  426.1 44.0 %copy-start.1 = (bf16[128,1024]{1,0:T(8,128)(2,1)S(1)}, bf16[128,1024]{1,0:T(8,128)(2,1)}, u32[]{:S(2)}) copy-start(bf16[128,1024]{1,0:T(8,128)(2,1)} %add_convert_fusion.1) | copy-start | bytes 786436
  427.7 44.7 %copy-start.8 = (f32[1024]{0:T(1024)S(1)}, f32[1024]{0:T(1024)}, u32[]{:S(2)}) copy-start(f32[1024]{0:T(1024)} %param.24) | copy-start | bytes 12292
  427.7 44.7 %copy-start.9 = (f32[1024]{0:T(1024)S(1)}, f32[1024]{0:T(1024)}, u32[]{:S(2)}) copy-start(f32[1024]{0:T(1024)} %param.23) | copy-start | bytes 12292
Sparse Core Ops, SparseCore 0:
  10.1 40.1 all-gather.12
  94.5 67.5 all-gather.20
  259.3 35.7 reduce-scatter.2
  297.2 35.9 all-gather.16
  335.3 39.0 all-gather.18
  377.1 38.7 all-gather.14
  425.8 44.2 reduce-scatter.4
where the time goes:
time: 484 us; the launch traced here: 482 us
  waiting for transfers between devices  195 us (40%)
  blocking collectives  170 us (35%)
  local copies, waits for them, and re-layouts  44.3 us (9%)
  matrix products  26.7 us (6%)
  other arithmetic  25.1 us (5%)
  between operations  14.4 us (3%)
  starting transfers between devices  5.5 us (1%)
    all_gather x2, blocking collectives, combined_all(): everything = jax.tree.map(lambda part: lax.all_gather(part, axis), array)  65 us
    all_gather x1, waiting for transfers between devices, per_device(): middle_all = lax.all_gather(middle, 'col', axis=0, tiled=True)  41.6 us
    all_gather x1, waiting for transfers between devices, per_device(): down_full = lax.all_gather(ffn_out, 'row', axis=1, tiled=True)  41.2 us
    all_gather x1, waiting for transfers between devices, per_device(): piece = lax.all_gather(qkv_global_weight, 'row', axis=0, tiled=True)  37.7 us
    all_to_all x1, blocking collectives, per_device(): lax.all_to_all(outgoing, 'seq', split_axis=0, concat_axis=0, tiled=True)  37.6 us
    all_gather x1, blocking collectives, per_device(): lax.all_gather(own_query, 'seq', axis=0, tiled=True)  35.8 us
    reduce_scatter x1, waiting for transfers between devices, per_device(): lax.psum_scatter(jnp.dot(attention, out_weight, preferred_element_type=jn...  34.7 us
    all_gather x1, waiting for transfers between devices, per_device(): lax.all_gather(ffn_in, 'row', axis=0, tiled=True)  32.8 us
  transfers between devices with their start and end apart: 9, of which 6 were waited for; matrix products, arithmetic and copies ran while one was open for 6% of the time, Pallas kernels for 0%

commit v1 on v0

v1 whole, which is shorter than its diff:
```python
import math

import jax
import jax.numpy as jnp
from jax import lax
from jax.sharding import PartitionSpec as P

HALF = 256


def padded(block, sides, width):
    for axis, dim in sides:
        count = lax.axis_size(axis)
        forward = [(i, i + 1) for i in range(count - 1)]
        backward = [(target, source) for source, target in forward]
        low = lax.ppermute(
            lax.slice_in_dim(block, block.shape[dim] - width, None, axis=dim), axis, forward
        )
        high = lax.ppermute(lax.slice_in_dim(block, 0, width, axis=dim), axis, backward)
        block = jnp.concatenate([low, block, high], axis=dim)
    return block


def layer_norm(values, gain, bias):
    center = values - jnp.mean(values, axis=1, keepdims=True)
    spread = jnp.mean(center * center, axis=1, keepdims=True)
    return center * lax.rsqrt(spread + 1e-05) * gain + bias


def per_device(
    hidden_in,
    qkv_weight,
    qkv_global_weight,
    out_weight,
    ln_gain,
    ln_bias,
    ffn_in,
    ffn_out,
    ln2_gain,
    ln2_bias,
    segment_ids,
    global_pos,
    page_owner,
):
    neg = -1e30
    tokens = hidden_in[0]
    shard_len, width = tokens.shape
    heads_here = qkv_weight.shape[1]
    triple = qkv_weight.shape[2]
    head_dim = triple // 3
    n_seq = lax.axis_size("seq")
    n_row = lax.axis_size("row")
    n_col = lax.axis_size("col")
    seq_index = lax.axis_index("seq")
    col_index = lax.axis_index("col")
    base = seq_index * shard_len
    scale = 1.0 / math.sqrt(head_dim)

    all_pos = global_pos[0]
    n_glob = all_pos.shape[0]
    per_shard = n_glob // n_seq
    own_pos = lax.dynamic_slice_in_dim(all_pos, seq_index * per_shard, per_shard, 0)
    local_order = jnp.arange(shard_len, dtype=jnp.int32)
    own_match = (own_pos - base)[:, None] == local_order[None, :]
    picker = own_match.astype(jnp.bfloat16)
    own_rows = jnp.dot(picker, tokens, preferred_element_type=jnp.float32).astype(jnp.bfloat16)
    glob_rows = lax.all_gather(own_rows, "seq", axis=0, tiled=True)

    wg_rows = qkv_global_weight.shape[0]
    fi_rows, units = ffn_in.shape
    wg_flat = qkv_global_weight.reshape(-1)
    fi_flat = ffn_in.reshape(-1)
    fo_flat = ffn_out.reshape(-1)
    n_wg, n_fi = wg_flat.shape[0], fi_flat.shape[0]
    everything = lax.all_gather(jnp.concatenate([wg_flat, fi_flat, fo_flat]), "row", axis=0)
    w_global = everything[:, :n_wg].reshape(n_row * wg_rows, heads_here * triple)
    f_in = everything[:, n_wg : n_wg + n_fi].reshape(n_row * fi_rows, units)
    f_out = jnp.transpose(
        everything[:, n_wg + n_fi :].reshape(n_row, units, ffn_out.shape[1]), (1, 0, 2)
    ).reshape(units, n_row * ffn_out.shape[1])
    w_out = lax.all_gather(out_weight, "col", axis=0, tiled=True)

    flat_weight = qkv_weight.reshape(width, heads_here * triple)
    qkv = jnp.dot(tokens, flat_weight, preferred_element_type=jnp.float32).astype(jnp.bfloat16)
    qkv_heads = qkv.reshape(shard_len, heads_here, triple)
    queries = qkv_heads[:, :, :head_dim]
    kv_local = qkv_heads[:, :, head_dim:]

    owners = page_owner[0, :, 0]
    n_pages = owners.shape[0]
    page_len = shard_len // n_pages
    capacity = max(2, n_pages // n_seq)
    page_order = jnp.arange(n_pages, dtype=jnp.int32)
    slot = jnp.sum(
        ((owners[:, None] == owners[None, :]) & (page_order[None, :] < page_order[:, None])).astype(
            jnp.int32
        ),
        axis=1,
    )
    target = owners * capacity + slot
    placing = (target[None, :] == jnp.arange(n_seq * capacity, dtype=jnp.int32)[:, None]).astype(
        jnp.bfloat16
    )
    outgoing = jnp.dot(
        placing,
        kv_local.reshape(n_pages, page_len * heads_here * 2 * head_dim),
        preferred_element_type=jnp.float32,
    ).astype(jnp.bfloat16)
    outgoing = outgoing.reshape(n_seq, capacity, page_len, heads_here, 2 * head_dim)
    arrived = lax.all_to_all(outgoing, "seq", split_axis=0, concat_axis=0, tiled=True)
    page_pool = arrived[None, None]

    kv_ext = padded(kv_local, (("seq", 0),), HALF)

    glob_qkv = jnp.dot(glob_rows, flat_weight, preferred_element_type=jnp.float32).astype(
        jnp.bfloat16
    )
    glob_kv = glob_qkv.reshape(n_glob, heads_here, triple)[:, :, head_dim:]
    glob_k = glob_kv[:, :, :head_dim]
    glob_v = glob_kv[:, :, head_dim:]
    glob_q = (
        jnp.dot(glob_rows, w_global, preferred_element_type=jnp.float32)
        .astype(jnp.bfloat16)
        .reshape(n_glob, heads_here, triple)[:, :, :head_dim]
    )
    global_kv_local = (
        jnp.dot(tokens, w_global, preferred_element_type=jnp.float32)
        .astype(jnp.bfloat16)
        .reshape(shard_len, heads_here, triple)[:, :, head_dim:]
    )

    seg_all = segment_ids[0]
    glob_seg = jnp.take(seg_all, all_pos)
    seg_pad = jnp.pad(seg_all, (HALF, HALF), constant_values=-1)
    query_seg = lax.dynamic_slice_in_dim(seg_all, base, shard_len, 0)
    key_seg = lax.dynamic_slice_in_dim(seg_pad, base, shard_len + 2 * HALF, 0)
    key_pos = base - HALF + jnp.arange(shard_len + 2 * HALF, dtype=jnp.int32)
    key_flag = jnp.any(key_pos[:, None] == all_pos[None, :], axis=1)
    query_pos = base + local_order

    s_part = (
        jnp.einsum(
            "ghd,khd->hgk",
            glob_q,
            global_kv_local[:, :, :head_dim],
            preferred_element_type=jnp.float32,
        )
        * scale
    )
    part_mask = glob_seg[:, None] == query_seg[None, :]
    part_top = jnp.max(jnp.where(part_mask, s_part, neg), axis=2)
    glob_top = lax.pmax(part_top, "seq")
    e_part = jnp.where(part_mask, jnp.exp(s_part - glob_top[:, :, None]), 0.0)
    part_total = jnp.sum(e_part, axis=2)
    part_acc = jnp.einsum(
        "hgk,khd->hgd",
        e_part,
        global_kv_local[:, :, head_dim:].astype(jnp.float32),
        precision=lax.Precision.HIGHEST,
    )
    summed = lax.psum(jnp.concatenate([part_acc, part_total[:, :, None]], axis=2), "seq")
    glob_out = (summed[:, :, :head_dim] / summed[:, :, head_dim:]).astype(jnp.bfloat16)

    glob_mask = query_seg[:, None] == glob_seg[None, :]
    k_blk = kv_ext[:, :, :head_dim]
    v_blk = kv_ext[:, :, head_dim:]
    s_win = jnp.einsum("qhd,khd->hqk", queries, k_blk, preferred_element_type=jnp.float32) * scale
    s_glob = jnp.einsum("qhd,ghd->hqg", queries, glob_k, preferred_element_type=jnp.float32) * scale
    m_win = (
        (jnp.abs(query_pos[:, None] - key_pos[None, :]) <= HALF)
        & (query_seg[:, None] == key_seg[None, :])
        & jnp.logical_not(key_flag[None, :])
    )
    top = jnp.maximum(
        jnp.max(jnp.where(m_win, s_win, neg), axis=2),
        jnp.max(jnp.where(glob_mask, s_glob, neg), axis=2),
    )
    e_win = jnp.where(m_win, jnp.exp(s_win - top[:, :, None]), 0.0)
    e_glob = jnp.where(glob_mask, jnp.exp(s_glob - top[:, :, None]), 0.0)
    total = jnp.sum(e_win, axis=2) + jnp.sum(e_glob, axis=2)
    numer = jnp.einsum(
        "hqk,khd->qhd", e_win.astype(jnp.bfloat16), v_blk, preferred_element_type=jnp.float32
    )
    numer = numer + jnp.einsum(
        "hqg,ghd->qhd", e_glob.astype(jnp.bfloat16), glob_v, preferred_element_type=jnp.float32
    )
    pieces = (numer / jnp.transpose(total)[:, :, None]).astype(jnp.bfloat16)

    own_out = lax.dynamic_slice_in_dim(glob_out, seq_index * per_shard, per_shard, 1)
    placed = jnp.einsum("gt,hgd->thd", picker, own_out, preferred_element_type=jnp.float32).astype(
        jnp.bfloat16
    )
    is_own = jnp.any(own_match, axis=0)
    attention = jnp.where(is_own[:, None, None], placed, pieces).reshape(
        shard_len, heads_here * head_dim
    )

    attn_all = lax.all_gather(attention, "col", axis=0)
    attn_full = jnp.transpose(attn_all, (1, 0, 2)).reshape(shard_len, n_col * heads_here * head_dim)
    proj = jnp.dot(attn_full, w_out, preferred_element_type=jnp.float32)
    middle = layer_norm(tokens.astype(jnp.float32) + proj, ln_gain, ln_bias).astype(jnp.bfloat16)
    ffn_pre = jnp.dot(middle, f_in, preferred_element_type=jnp.float32)
    ffn_hidden = jax.nn.gelu(ffn_pre, approximate=False).astype(jnp.bfloat16)
    ffn_part = lax.psum_scatter(
        jnp.dot(ffn_hidden, f_out, preferred_element_type=jnp.float32),
        "col",
        scatter_dimension=0,
        tiled=True,
    )
    out_rows = shard_len // n_col
    mine = lax.dynamic_slice_in_dim(middle, col_index * out_rows, out_rows, 0).astype(jnp.float32)
    normed = layer_norm(mine + ffn_part, ln2_gain, ln2_bias)
    return (normed.astype(jnp.bfloat16)[None], page_pool)


def solution(mesh):
    in_specs = (
        P("row", "seq", None),
        P(None, "col", None),
        P("row", "col", None),
        P("col", None),
        P(),
        P(),
        P("row", "col"),
        P("col", "row"),
        P(),
        P(),
        P("row", None),
        P("row", None),
        P("row", "seq", None),
    )
    out_specs = (P("row", ("seq", "col"), None), P("row", "seq", None, None, None, "col", None))
    return jax.shard_map(
        per_device, mesh=mesh, in_specs=in_specs, out_specs=out_specs, check_vma=False
    )
```

time: 484 us -> 556 us (1.15)
  waiting for transfers between devices: 195 us -> 343 us
  blocking collectives: 170 us -> 86.1 us
  starting transfers between devices: 5.5 us -> 20.2 us
  other arithmetic: 25.1 us -> 13.6 us
  matrix products: 26.7 us -> 33.5 us
    psum x0 -> x1, waiting for transfers between devices: none -> 205 us  [per_device(): lax.psum(jnp.concatenate([part_acc, part_total[:, :, None]], axis=2), 'seq')]
    all_gather x4 -> x1, blocking collectives: 133 us -> 32.6 us  [per_device(): glob_rows = lax.all_gather(own_rows, 'seq', axis=0, tiled=True)]
    all_gather x5 -> x3, waiting for transfers between devices: 153 us -> 86.6 us  [the longest x1 53.6 us: per_device(): w_out = lax.all_gather(out_weight, 'col', axis=0, tiled=True)]
    pmax x0 -> x1, blocking collectives: none -> 53.4 us  [per_device(): glob_top = lax.pmax(part_top, 'seq')]
    all_to_all x1 -> x0, blocking collectives: 37.6 us -> none  [per_device(): lax.all_to_all(outgoing, 'seq', split_axis=0, concat_axis=0, tiled=True)]
    dynamic_slice x62 -> x0, local copies, waits for them, and re-layouts: 32.5 us -> none  [lap(): return combine(so_far, jax.tree.map(lambda part: part[k], everything))]
    all_to_all x0 -> x1, waiting for transfers between devices: none -> 28.1 us  [per_device(): lax.all_to_all(outgoing, 'seq', split_axis=0, concat_axis=0, tiled=True)]
    reduce_scatter x2 -> x1, waiting for transfers between devices: 39.5 us -> 23.1 us  [per_device(): lax.psum_scatter(jnp.dot(ffn_hidden, f_out, preferred_element_type=jnp.fl...]
  transfers between devices with their start and end apart: 9 -> 8, of which waited for: 6 -> 6; matrix products, arithmetic and copies ran while one was open for 6% -> 8% of each run, Pallas kernels for 0% -> 0%
where the time goes in v1:
time: 556 us; the launch traced here: 555 us
  waiting for transfers between devices  343 us (62%)
  blocking collectives  86.1 us (15%)
  local copies, waits for them, and re-layouts  43.5 us (8%)
  matrix products  33.5 us (6%)
  starting transfers between devices  20.2 us (4%)
  between operations  14.3 us (3%)
  other arithmetic  13.6 us (2%)
    psum x1, waiting for transfers between devices, per_device(): lax.psum(jnp.concatenate([part_acc, part_total[:, :, None]], axis=2), 'seq')  205 us
    all_gather x1, waiting for transfers between devices, per_device(): w_out = lax.all_gather(out_weight, 'col', axis=0, tiled=True)  53.6 us
    pmax x1, blocking collectives, per_device(): glob_top = lax.pmax(part_top, 'seq')  53.4 us
    all_gather x1, blocking collectives, per_device(): glob_rows = lax.all_gather(own_rows, 'seq', axis=0, tiled=True)  32.6 us
    all_to_all x1, waiting for transfers between devices, per_device(): lax.all_to_all(outgoing, 'seq', split_axis=0, concat_axis=0, tiled=True)  28.1 us
    reduce_scatter x1, waiting for transfers between devices, per_device(): lax.psum_scatter(jnp.dot(ffn_hidden, f_out, preferred_element_type=jnp.fl...  23.1 us
    all_gather x1, waiting for transfers between devices, per_device(): attn_all = lax.all_gather(attention, 'col', axis=0)  23.1 us
  transfers between devices with their start and end apart: 8, of which 6 were waited for; matrix products, arithmetic and copies ran while one was open for 8% of the time, Pallas kernels for 0%

profile of v1, /device:TPU:1, one launch (start us, length us, event | category | flops | bytes accessed | tf_op | source)
XLA Modules:
  0.0 554.5 jit_solution(4400960408158859480)
XLA Ops:
  12.9 1.9 convolution_convert_fusion.1
  17.1 5.4 collective-permute-start
  22.5 5.4 collective-permute-start.1
  28.3 32.6 %all-gather.1 = bf16[32,4,1024]{2,1,0:T(4,128)(2,1)S(1)} all-gather(bf16[1,4,1024]{2,1,0:T(4,128)(2,1)S(1)} %fusion.24), channel_id=1, replica_groups=mesh['seq'=32,'row'=4,'col'=4] {'seq'}, dimensions={0}, use_global_device_ids=true | all-gather | bytes 270336 | tf_op jit(solution)/shard_map/all_gather | solution.py:67
  69.9 2.7 fusion
  72.8 2.0 fusion.70
  74.8 9.9 %all-gather.10.cloned.1.call-done = bf16[2883584]{0:T(1024)(128)(2,1)} async-done(((bf16[720896]{0:T(1024)(128)(2,1)}), bf16[2883584]{0:T(1024)(128)(2,1)}) %all-gather.10.cloned.1.call-update) | async-done | bytes 5767184 | tf_op jit(solution)/shard_map/all_gather | solution.py:75
  84.7 7.2 %reshape.195 = bf16[4,720896]{1,0:T(4,128)(2,1)} reshape(bf16[2883584]{0:T(1024)(128)(2,1)} %all-gather.10.cloned.1.call-done) | data formatting | bytes 11534336 | tf_op jit(solution)/shard_map/all_gather | solution.py:75
  95.1 3.2 convolution_convert_fusion.2
  100.0 53.4 %pmax.7 = f32[4,128]{1,0:T(4,128)S(1)} all-reduce(f32[4,128]{1,0:T(4,128)S(1)} %get-tuple-element.10), channel_id=1, replica_groups=mesh['seq'=32,'row'=4,'col'=4] {'seq'}, use_global_device_ids=true, to_apply=%region_2.3 | all-reduce | flops 512 | bytes 4096 | tf_op jit(solution)/shard_map/pmax | solution.py:152
  153.5 1.9 fusion.67
  156.5 5.3 fusion.63
  161.8 205.0 %all-reduce.3.cloned.1.call-done = f32[4,128,65]{1,2,0:T(8,128)} async-done(((f32[4,128,65]{1,2,0:T(8,128)}), f32[4,128,65]{1,2,0:T(8,128)}) %all-reduce.3.cloned.1.call-update) | async-done | bytes 133136 | tf_op jit(solution)/shard_map/psum | solution.py:161
  370.3 4.0 fusion.139
  375.9 4.0 copy.66
  379.9 4.8 reshape.182
  384.7 23.1 %all-gather.6.cloned.1.call-done = bf16[4,512,256]{2,1,0:T(8,128)(2,1)} async-done(((bf16[1,512,256]{2,1,0:T(8,128)(2,1)}), bf16[4,512,256]{2,1,0:T(8,128)(2,1)}) %all-gather.6.cloned.1.call-update) | async-done | bytes 1048592 | tf_op jit(solution)/shard_map/all_gather | solution.py:198
  409.5 53.6 %all-gather.8.cloned.1.call-done = bf16[1024,1024]{1,0:T(8,128)(2,1)} async-done(((bf16[256,1024]{1,0:T(8,128)(2,1)}), bf16[1024,1024]{1,0:T(8,128)(2,1)}) %all-gather.8.cloned.1.call-update) | async-done | bytes 2097168 | tf_op jit(solution)/shard_map/all_gather | solution.py:81
  463.1 2.9 fusion.141
  468.1 9.8 %fusion.25 = f32[512,1024]{1,0:T(8,128)} fusion(bf16[1024,1024]{0,1:T(8,128)(2,1)} %bitcast.92, bf16[512,1024]{1,0:T(8,128)(2,1)S(1)} %add_convert_fusion, bf16[1024,1024]{1,0:T(8,128)(2,1)} %reshape.182), kind=kOutput, calls=%fused_computation.47 | convolution fusion | flops 2181562368 | bytes 7340032 | tf_op jit(solution)/shard_map/dot_general | solution.py:205
  481.9 9.3 %all-to-all-start = ((bf16[32,2,16,4,128]{4,3,2,1,0:T(4,128)(2,1)}), bf16[32,2,16,4,128]{4,3,2,1,0:T(4,128)(2,1)S(1)}, u32[]{:S(2)}, u32[]{:S(2)}) async-start(bf16[32,2,16,4,128]{4,3,2,1,0:T(4,128)(2,1)} %reshape.186), calls=%async_computation.1 | async-start | bytes 2097152 | tf_op jit(solution)/shard_map/all_to_all | solution.py:110
  491.1 28.1 %all-to-all-done = bf16[32,2,16,4,128]{4,3,2,1,0:T(4,128)(2,1)S(1)} async-done(((bf16[32,2,16,4,128]{4,3,2,1,0:T(4,128)(2,1)}), bf16[32,2,16,4,128]{4,3,2,1,0:T(4,128)(2,1)S(1)}, u32[]{:S(2)}, u32[]{:S(2)}) %all-to-all-start) | async-done | bytes 1048608 | tf_op jit(solution)/shard_map/all_to_all | solution.py:110
  519.3 23.1 %reduce-scatter.2.cloned.1.call-done = f32[128,1024]{1,0:T(8,128)} async-done(((f32[512,1024]{1,0:T(8,128)}), f32[128,1024]{1,0:T(8,128)}) %reduce-scatter.2.cloned.1.call-update) | async-done | bytes 524304 | tf_op jit(solution)/shard_map/reduce_scatter | solution.py:204
  545.0 2.0 fusion.81
  (121 shorter events, 39.8 us)
Async XLA Ops:
  7.2 5.3 copy-start
  7.2 3.1 copy-start.14
  7.2 3.1 copy-start.15
  7.2 77.5 %all-gather.10.cloned.1.call-start = ((), (), s32[]{:S(2)}) async-start(), calls=%async_computation.6 | async-start | bytes 7208960 | tf_op jit(solution)/shard_map/all_gather | solution.py:75
  12.4 354.4 %all-reduce.3.cloned.1.call-start = ((), (), s32[]{:S(2)}) async-start(), calls=%async_computation.2 | async-start | bytes 294912 | tf_op jit(solution)/shard_map/psum | solution.py:161
  14.8 13.1 %copy-start.21 = (s32[1,128]{1,0:T(1,128)S(1)}, s32[1,128]{1,0:T(1,128)}, u32[]{:S(2)}) copy-start(s32[1,128]{1,0:T(1,128)} %param.24) | copy-start | bytes 1540
  14.9 46.1 %copy-start.3 = (s32[1,16384]{1,0:T(1,128)S(1)}, s32[1,16384]{1,0:T(1,128)}, u32[]{:S(2)}) copy-start(s32[1,16384]{1,0:T(1,128)} %param.23) | copy-start | bytes 196612
  17.1 49.5 %collective-permute-start = (bf16[256,4,128]{0,2,1:T(8,128)(2,1)}, bf16[256,4,128]{0,2,1:T(8,128)(2,1)}, u32[]{:S(2)}, u32[]{:S(2)}) collective-permute-start(bf16[256,4,128]{0,2,1:T(8,128)(2,1)} %get-tuple-element.4), channel_id=1, source_target_pairs={{0,16},{16,32},{32,48},{48,64},{64,80},{80,96},{96,112},{112,128},... | collective-permute-start | bytes 786440 | tf_op jit(solution)/shard_map/ppermute | solution.py:16
  22.5 44.2 %collective-permute-start.1 = (bf16[256,4,128]{0,2,1:T(8,128)(2,1)}, bf16[256,4,128]{0,2,1:T(8,128)(2,1)}, u32[]{:S(2)}, u32[]{:S(2)}) collective-permute-start(bf16[256,4,128]{0,2,1:T(8,128)(2,1)} %get-tuple-element.5), channel_id=1, source_target_pairs={{16,0},{32,16},{48,32},{64,48},{80,64},{96,80},{112,96},{128,112},... | collective-permute-start | bytes 786440 | tf_op jit(solution)/shard_map/ppermute | solution.py:19
  63.7 6.1 %copy-start.9 = (pred[512,1024]{1,0:T(8,128)(4,1)}, pred[512,1024]{1,0:T(8,128)(4,1)S(1)}, u32[]{:S(2)}) copy-start(pred[512,1024]{1,0:T(8,128)(4,1)S(1)} %fusion.15) | copy-start | bytes 1572868
  64.5 5.0 copy-start.4
  69.6 3.2 copy-start.2
  98.5 58.0 %copy-start.10 = (pred[512,1024]{1,0:T(8,128)(4,1)S(1)}, pred[512,1024]{1,0:T(8,128)(4,1)}, u32[]{:S(2)}) copy-start(pred[512,1024]{1,0:T(8,128)(4,1)} %copy-done.9) | copy-start | bytes 1572868
  98.5 58.0 %copy-start.13 = (bf16[1024,4,128]{0,2,1:T(8,128)(2,1)S(1)}, bf16[1024,4,128]{0,2,1:T(8,128)(2,1)}, u32[]{:S(2)}) copy-start(bf16[1024,4,128]{0,2,1:T(8,128)(2,1)} %copy-done.12) | copy-start | bytes 3145732
  98.5 58.0 %copy-start.16 = (f32[4,64,512]{2,1,0:T(8,128)S(1)}, f32[4,64,512]{2,1,0:T(8,128)}, u32[]{:S(2)}) copy-start(f32[4,64,512]{2,1,0:T(8,128)} %fusion.70) | copy-start | bytes 1572868
  156.4 251.3 %all-gather.6.cloned.1.call-start = ((), (), s32[]{:S(2)}) async-start(), calls=%async_computation.3 | async-start | bytes 1310720 | tf_op jit(solution)/shard_map/all_gather | solution.py:198
  369.7 93.4 %all-gather.8.cloned.1.call-start = ((), (), s32[]{:S(2)}) async-start(), calls=%async_computation.4 | async-start | bytes 2621440 | tf_op jit(solution)/shard_map/all_gather | solution.py:81
  370.3 172.1 %reduce-scatter.2.cloned.1.call-start = ((), (), s32[]{:S(2)}) async-start(), calls=%async_computation.5 | async-start | bytes 2621440 | tf_op jit(solution)/shard_map/reduce_scatter | solution.py:204
  384.7 78.4 %copy-start.7 = (bf16[1,512,1024]{2,1,0:T(8,128)(2,1)S(1)}, bf16[1,512,1024]{2,1,0:T(8,128)(2,1)}, u32[]{:S(2)}) copy-start(bf16[1,512,1024]{2,1,0:T(8,128)(2,1)} %param.13) | copy-start | bytes 3145732
  477.9 1.8 copy-start.22
  481.8 63.2 %copy-start.19 = (f32[1024]{0:T(1024)S(1)}, f32[1024]{0:T(1024)}, u32[]{:S(2)}) copy-start(f32[1024]{0:T(1024)} %param.22) | copy-start | bytes 12292
  481.9 63.2 %copy-start.20 = (f32[1024]{0:T(1024)S(1)}, f32[1024]{0:T(1024)}, u32[]{:S(2)}) copy-start(f32[1024]{0:T(1024)} %param.21) | copy-start | bytes 12292
  481.9 37.4 %all-to-all-start = ((bf16[32,2,16,4,128]{4,3,2,1,0:T(4,128)(2,1)}), bf16[32,2,16,4,128]{4,3,2,1,0:T(4,128)(2,1)S(1)}, u32[]{:S(2)}, u32[]{:S(2)}) async-start(bf16[32,2,16,4,128]{4,3,2,1,0:T(4,128)(2,1)} %reshape.186), calls=%async_computation.1 | async-start | bytes 2097152 | tf_op jit(solution)/shard_map/all_to_all | solution.py:110
  542.3 5.7 %copy-start.1 = (bf16[1024,4,192]{0,2,1:T(8,128)(2,1)S(1)}, bf16[1024,4,192]{0,2,1:T(8,128)(2,1)}, u32[]{:S(2)}) copy-start(bf16[1024,4,192]{0,2,1:T(8,128)(2,1)} %param.14) | copy-start | bytes 4718596
  (8 other events, 9.3 us)
Sparse Core Ops, SparseCore 0:
  12.6 72.0 all-gather.9
  156.6 210.2 all-reduce.2
  369.8 37.9 all-gather.5
  409.9 53.1 all-gather.7
  478.1 64.2 reduce-scatter.1

commit v2 on v1

--- a/solution.py
+++ b/solution.py
@@ -1,9 +1,14 @@
+import functools
 import math
 
 import jax
 import jax.numpy as jnp
 from jax import lax
+from jax.experimental import pallas as pl
+from jax.experimental.pallas import tpu as pltpu
 from jax.sharding import PartitionSpec as P
+
+MESH = pl.DeviceIdType.MESH
 
 HALF = 256
 
@@ -19,6 +24,116 @@
         high = lax.ppermute(lax.slice_in_dim(block, 0, width, axis=dim), axis, backward)
         block = jnp.concatenate([low, block, high], axis=dim)
     return block
+
+
+def butterfly_partners(n):
+    me = lax.axis_index("seq")
+    partners = []
+    step = 1
+    while step < n:
+        bit = (me // step) % 2
+        partners.append(me + step - 2 * step * bit)
+        step *= 2
+    return me, partners
+
+
+def enter(partners):
+    row, col = lax.axis_index("row"), lax.axis_index("col")
+    barrier = pltpu.get_barrier_semaphore()
+    for partner in partners:
+        pl.semaphore_signal(barrier, inc=1, device_id=(partner, row, col), device_id_type=MESH)
+    pl.semaphore_wait(barrier, len(partners))
+    return row, col
+
+
+def gather_kernel(n, x_ref, out_ref, self_sem, send_sem, recv_sem):
+    me, partners = butterfly_partners(n)
+    row, col = enter(partners)
+    own = pltpu.make_async_copy(x_ref, out_ref.at[me], self_sem)
+    own.start()
+    own.wait()
+    size = 1
+    for k, partner in enumerate(partners):
+        start = (me // size) * size
+        copy = pltpu.make_async_remote_copy(
+            src_ref=out_ref.at[pl.ds(start, size)],
+            dst_ref=out_ref.at[pl.ds(start, size)],
+            send_sem=send_sem.at[k],
+            recv_sem=recv_sem.at[k],
+            device_id=(partner, row, col),
+            device_id_type=MESH,
+        )
+        copy.start()
+        copy.wait()
+        size *= 2
+
+
+def seq_gather(block):
+    n = lax.axis_size("seq")
+    rounds = n.bit_length() - 1
+    return pl.pallas_call(
+        functools.partial(gather_kernel, n),
+        out_shape=jax.ShapeDtypeStruct((n,) + block.shape, block.dtype),
+        in_specs=[pl.BlockSpec(memory_space=pltpu.VMEM)],
+        out_specs=pl.BlockSpec(memory_space=pltpu.VMEM),
+        scratch_shapes=[
+            pltpu.SemaphoreType.DMA(()),
+            pltpu.SemaphoreType.DMA((rounds,)),
+            pltpu.SemaphoreType.DMA((rounds,)),
+        ],
+        compiler_params=pltpu.CompilerParams(collective_id=0, has_side_effects=True),
+    )(block)
+
+
+def merge_parts(mine, theirs, top_lane):
+    lane = lax.broadcasted_iota(jnp.int32, mine.shape, 1)
+    is_top = lane == top_lane
+    top_a = jnp.max(jnp.where(is_top, mine, -jnp.inf), axis=1, keepdims=True)
+    top_b = jnp.max(jnp.where(is_top, theirs, -jnp.inf), axis=1, keepdims=True)
+    top = jnp.maximum(top_a, top_b)
+    merged = mine * jnp.exp(top_a - top) + theirs * jnp.exp(top_b - top)
+    return jnp.where(is_top, top, merged)
+
+
+def combine_kernel(n, top_lane, x_ref, out_ref, cur, got, send_sem, recv_sem):
+    me, partners = butterfly_partners(n)
+    row, col = enter(partners)
+    source = x_ref
+    value = x_ref[...]
+    for k, partner in enumerate(partners):
+        copy = pltpu.make_async_remote_copy(
+            src_ref=source,
+            dst_ref=got.at[k],
+            send_sem=send_sem.at[k],
+            recv_sem=recv_sem.at[k],
+            device_id=(partner, row, col),
+            device_id_type=MESH,
+        )
+        copy.start()
+        copy.wait()
+        value = merge_parts(value, got[k], top_lane)
+        if k + 1 < len(partners):
+            cur[k] = value
+            source = cur.at[k]
+    out_ref[...] = value
+
+
+def seq_softmax_combine(parts, top_lane):
+    n = lax.axis_size("seq")
+    rounds = n.bit_length() - 1
+    return pl.pallas_call(
+        functools.partial(combine_kernel, n, top_lane),
+        out_shape=jax.ShapeDtypeStruct(parts.shape, parts.dtype),
+        in_specs=[pl.BlockSpec(memory_space=pltpu.VMEM)],
+        out_specs=pl.BlockSpec(memory_space=pltpu.VMEM),
+        scratch_shapes=[
+            pltpu.VMEM((max(rounds - 1, 1),) + parts.shape, parts.dtype),
+            pltpu.VMEM((rounds,) + parts.shape, parts.dtype),
+            pltpu.SemaphoreType.DMA((rounds,)),
+            pltpu.SemaphoreType.DMA((rounds,)),
+        ],
+        compiler_params=pltpu.CompilerParams(collective_id=1, has_side_effects=True),
+    )(parts)
 
 
 def layer_norm(values, gain, bias):
@@ -64,7 +179,7 @@
     own_match = (own_pos - base)[:, None] == local_order[None, :]
     picker = own_match.astype(jnp.bfloat16)
     own_rows = jnp.dot(picker, tokens, preferred_element_type=jnp.float32).astype(jnp.bfloat16)
-    glob_rows = lax.all_gather(own_rows, "seq", axis=0, tiled=True)
+    glob_rows = seq_gather(own_rows.reshape(-1, 128)).reshape(n_glob, width)
 
     wg_rows = qkv_global_weight.shape[0]
     fi_rows, units = ffn_in.shape
@@ -149,8 +264,7 @@
     )
     part_mask = glob_seg[:, None] == query_seg[None, :]
     part_top = jnp.max(jnp.where(part_mask, s_part, neg), axis=2)
-    glob_top = lax.pmax(part_top, "seq")
-    e_part = jnp.where(part_mask, jnp.exp(s_part - glob_top[:, :, None]), 0.0)
+    e_part = jnp.where(part_mask, jnp.exp(s_part - part_top[:, :, None]), 0.0)
     part_total = jnp.sum(e_part, axis=2)
     part_acc = jnp.einsum(
         "hgk,khd->hgd",
@@ -158,8 +272,18 @@
         global_kv_local[:, :, head_dim:].astype(jnp.float32),
         precision=lax.Precision.HIGHEST,
     )
-    summed = lax.psum(jnp.concatenate([part_acc, part_total[:, :, None]], axis=2), "seq")
-    glob_out = (summed[:, :, :head_dim] / summed[:, :, head_dim:]).astype(jnp.bfloat16)
+    packed = jnp.concatenate(
+        [
+            part_acc,
+            part_total[:, :, None],
+            jnp.broadcast_to(part_top[:, :, None], part_top.shape + (128 - head_dim - 1,)),
+        ],
+        axis=2,
+    ).reshape(heads_here * n_glob, 128)
+    merged = seq_softmax_combine(packed, head_dim + 1).reshape(heads_here, n_glob, 128)
+    glob_out = (merged[:, :, :head_dim] / merged[:, :, head_dim : head_dim + 1]).astype(
+        jnp.bfloat16
+    )
 
     glob_mask = query_seg[:, None] == glob_seg[None, :]
     k_blk = kv_ext[:, :, :head_dim]

time: 556 us -> 341 us (0.61)
  waiting for transfers between devices: 343 us -> 146 us
  blocking collectives: 86.1 us -> 0 us
  Pallas kernels: 0 us -> 70.2 us
    psum x1 -> x0, waiting for transfers between devices: 205 us -> none  [per_device(): lax.psum(jnp.concatenate([part_acc, part_total[:, :, None]], axis=2), 'seq')]
    pallas_call x0 -> x2, Pallas kernels: none -> 70.2 us  [the longest x1 52.4 us: seq_softmax_combine(): pl.pallas_call(functools.partial(combine_kernel, n, top_lane), out_shape=...]
    pmax x1 -> x0, blocking collectives: 53.4 us -> none  [per_device(): glob_top = lax.pmax(part_top, 'seq')]
    all_gather x1 -> x0, blocking collectives: 32.6 us -> none  [per_device(): glob_rows = lax.all_gather(own_rows, 'seq', axis=0, tiled=True)]
    all_gather x1, waiting for transfers between devices: 9.93 us -> 21.4 us  [per_device(): lax.all_gather(jnp.concatenate([wg_flat, fi_flat, fo_flat]), 'row', axis=0)]
  transfers between devices with their start and end apart: 8 -> 7, of which waited for: 6 -> 5; matrix products, arithmetic and copies ran while one was open for 8% -> 12% of each run, Pallas kernels for 0% -> 5%
where the time goes in v2:
time: 341 us; the launch traced here: 340 us
  waiting for transfers between devices  146 us (43%)
  Pallas kernels  70.2 us (21%)
  local copies, waits for them, and re-layouts  44.8 us (13%)
  matrix products  30.7 us (9%)
  starting transfers between devices  20.2 us (6%)
  between operations  14.2 us (4%)
  other arithmetic  13.9 us (4%)
    all_gather x1, waiting for transfers between devices, per_device(): w_out = lax.all_gather(out_weight, 'col', axis=0, tiled=True)  53.6 us
    pallas_call x1, Pallas kernels, seq_softmax_combine(): pl.pallas_call(functools.partial(combine_kernel, n, top_lane), out_shape=...  52.4 us
    all_to_all x1, waiting for transfers between devices, per_device(): lax.all_to_all(outgoing, 'seq', split_axis=0, concat_axis=0, tiled=True)  28.1 us
    reduce_scatter x1, waiting for transfers between devices, per_device(): lax.psum_scatter(jnp.dot(ffn_hidden, f_out, preferred_element_type=jnp.fl...  23.5 us
    all_gather x1, waiting for transfers between devices, per_device(): lax.all_gather(jnp.concatenate([wg_flat, fi_flat, fo_flat]), 'row', axis=0)  21.4 us
    all_gather x1, waiting for transfers between devices, per_device(): attn_all = lax.all_gather(attention, 'col', axis=0)  18.3 us
    pallas_call x1, Pallas kernels, seq_gather(): pl.pallas_call(functools.partial(gather_kernel, n), out_shape=jax.ShapeDt...  17.7 us
    dot_general x1, matrix products, per_device(): jnp.dot(ffn_hidden, f_out, preferred_element_type=jnp.float32)  9.79 us
  transfers between devices with their start and end apart: 7, of which 5 were waited for; matrix products, arithmetic and copies ran while one was open for 12% of the time, Pallas kernels for 5%

profile of v2, /device:TPU:1, one launch (start us, length us, event | category | flops | bytes accessed | tf_op | source)
XLA Modules:
  0.0 339.6 jit_solution(4944841068021577894)
XLA Ops:
  12.9 1.9 convolution_convert_fusion.1
  17.1 5.4 %collective-permute-start = (bf16[256,4,128]{0,2,1:T(8,128)(2,1)}, bf16[256,4,128]{0,2,1:T(8,128)(2,1)}, u32[]{:S(2)}, u32[]{:S(2)}) collective-permute-start(bf16[256,4,128]{0,2,1:T(8,128)(2,1)} %get-tuple-element.4), channel_id=1, source_target_pairs={{0,16},{16,32},{32,48},{48,64},{64,80},{80,96},{96,112},{112,128},... | collective-permute-start | bytes 786440 | tf_op jit(solution)/shard_map/ppermute | solution.py:21
  22.5 5.4 %collective-permute-start.1 = (bf16[256,4,128]{0,2,1:T(8,128)(2,1)}, bf16[256,4,128]{0,2,1:T(8,128)(2,1)}, u32[]{:S(2)}, u32[]{:S(2)}) collective-permute-start(bf16[256,4,128]{0,2,1:T(8,128)(2,1)} %get-tuple-element.5), channel_id=1, source_target_pairs={{16,0},{32,16},{48,32},{64,48},{80,64},{96,80},{112,96},{128,112},... | collective-permute-start | bytes 786440 | tf_op jit(solution)/shard_map/ppermute | solution.py:24
  28.9 17.7 %shard_map.140 = bf16[32,32,128]{2,1,0:T(8,128)(2,1)} custom-call(bf16[32,128]{1,0:T(8,128)(2,1)} %reshape.187.x_ref), custom_call_target="tpu_custom_call" | custom-call | tf_op jit(solution)/shard_map/pallas_call | solution.py:74
  54.6 1.7 select_reduce_fusion
  56.6 2.7 fusion
  60.5 2.9 fusion.62
  63.3 21.4 %all-gather.9.cloned.1.call-done = bf16[2883584]{0:T(1024)(128)(2,1)} async-done(((bf16[720896]{0:T(1024)(128)(2,1)}), bf16[2883584]{0:T(1024)(128)(2,1)}) %all-gather.9.cloned.1.call-update) | async-done | bytes 5767184 | tf_op jit(solution)/shard_map/all_gather | solution.py:190
  84.7 7.3 %reshape.213 = bf16[4,720896]{1,0:T(4,128)(2,1)} reshape(bf16[2883584]{0:T(1024)(128)(2,1)} %all-gather.9.cloned.1.call-done) | data formatting | bytes 11534336 | tf_op jit(solution)/shard_map/all_gather | solution.py:190
  95.2 3.1 convolution_convert_fusion.2
  99.9 1.8 fusion.66
  103.2 52.4 %shard_map.141 = f32[512,128]{1,0:T(8,128)} custom-call(f32[512,128]{1,0:T(8,128)} %pad_maximum_fusion.2.x_ref), custom_call_target="tpu_custom_call" | custom-call | tf_op jit(solution)/shard_map/pallas_call | solution.py:124
  159.7 4.0 %fusion.138 = (bf16[4,262144]{1,0:T(4,128)(2,1)}, bf16[4,262144]{1,0:T(4,128)(2,1)S(1)}) fusion(bf16[4,720896]{1,0:T(4,128)(2,1)} %reshape.213), kind=kLoop, calls=%fused_computation.188 | loop fusion | bytes 8388608 | tf_op jit(solution)/shard_map/slice | solution.py:192
  165.3 4.0 %copy.71 = bf16[1024,4,256]{0,2,1:T(8,128)(2,1)} copy(bf16[1024,4,256]{2,0,1:T(8,128)(2,1)} %bitcast.83) | data formatting | bytes 4194304 | tf_op jit(solution)/shard_map/transpose | solution.py:193
  169.3 4.9 %reshape.200 = bf16[1024,1024]{1,0:T(8,128)(2,1)} reshape(bf16[4,262144]{1,0:T(4,128)(2,1)} %get-tuple-element.2) | data formatting | bytes 4194304 | tf_op jit(solution)/shard_map/reshape | solution.py:192
  174.1 18.3 %all-gather.5.cloned.1.call-done = bf16[4,512,256]{2,1,0:T(8,128)(2,1)} async-done(((bf16[1,512,256]{2,1,0:T(8,128)(2,1)}), bf16[4,512,256]{2,1,0:T(8,128)(2,1)}) %all-gather.5.cloned.1.call-update) | async-done | bytes 1048592 | tf_op jit(solution)/shard_map/all_gather | solution.py:322
  192.4 1.7 copy.70
  194.1 53.6 %all-gather.7.cloned.1.call-done = bf16[1024,1024]{1,0:T(8,128)(2,1)} async-done(((bf16[256,1024]{1,0:T(8,128)(2,1)}), bf16[1024,1024]{1,0:T(8,128)(2,1)}) %all-gather.7.cloned.1.call-update) | async-done | bytes 2097168 | tf_op jit(solution)/shard_map/all_gather | solution.py:196
  247.7 2.9 fusion.140
  252.7 9.8 %fusion.24 = f32[512,1024]{1,0:T(8,128)} fusion(bf16[1024,1024]{0,1:T(8,128)(2,1)} %bitcast.93, bf16[512,1024]{1,0:T(8,128)(2,1)S(1)} %add_convert_fusion, bf16[1024,1024]{1,0:T(8,128)(2,1)} %reshape.200), kind=kOutput, calls=%fused_computation.46 | convolution fusion | flops 2181562368 | bytes 7340032 | tf_op jit(solution)/shard_map/dot_general | solution.py:329
  266.5 9.3 %all-to-all-start = ((bf16[32,2,16,4,128]{4,3,2,1,0:T(4,128)(2,1)}), bf16[32,2,16,4,128]{4,3,2,1,0:T(4,128)(2,1)S(1)}, u32[]{:S(2)}, u32[]{:S(2)}) async-start(bf16[32,2,16,4,128]{4,3,2,1,0:T(4,128)(2,1)} %reshape.204), calls=%async_computation.1 | async-start | bytes 2097152 | tf_op jit(solution)/shard_map/all_to_all | solution.py:225
  275.8 28.1 %all-to-all-done = bf16[32,2,16,4,128]{4,3,2,1,0:T(4,128)(2,1)S(1)} async-done(((bf16[32,2,16,4,128]{4,3,2,1,0:T(4,128)(2,1)}), bf16[32,2,16,4,128]{4,3,2,1,0:T(4,128)(2,1)S(1)}, u32[]{:S(2)}, u32[]{:S(2)}) %all-to-all-start) | async-done | bytes 1048608 | tf_op jit(solution)/shard_map/all_to_all | solution.py:225
  303.9 23.5 %reduce-scatter.2.cloned.1.call-done = f32[128,1024]{1,0:T(8,128)} async-done(((f32[512,1024]{1,0:T(8,128)}), f32[128,1024]{1,0:T(8,128)}) %reduce-scatter.2.cloned.1.call-update) | async-done | bytes 524304 | tf_op jit(solution)/shard_map/reduce_scatter | solution.py:328
  330.1 2.0 fusion.80
  (110 shorter events, 39.7 us)
Async XLA Ops:
  7.2 5.3 %copy-start = (bf16[1024,4,192]{0,2,1:T(8,128)(2,1)S(1)}, bf16[1024,4,192]{0,2,1:T(8,128)(2,1)}, u32[]{:S(2)}) copy-start(bf16[1024,4,192]{0,2,1:T(8,128)(2,1)} %param.14) | copy-start | bytes 4718596
  7.2 3.1 copy-start.9
  7.2 3.1 copy-start.10
  7.2 77.5 %all-gather.9.cloned.1.call-start = ((), (), s32[]{:S(2)}) async-start(), calls=%async_computation.5 | async-start | bytes 7208960 | tf_op jit(solution)/shard_map/all_gather | solution.py:190
  10.2 1.0 copy-start.8
  11.2 1.7 copy-start.5
  12.5 180.0 %all-gather.5.cloned.1.call-start = ((), (), s32[]{:S(2)}) async-start(), calls=%async_computation.2 | async-start | bytes 1310720 | tf_op jit(solution)/shard_map/all_gather | solution.py:322
  14.8 13.1 %copy-start.15 = (s32[1,128]{1,0:T(1,128)S(1)}, s32[1,128]{1,0:T(1,128)}, u32[]{:S(2)}) copy-start(s32[1,128]{1,0:T(1,128)} %param.24) | copy-start | bytes 1540
  14.9 32.9 %copy-start.2 = (s32[1,16384]{1,0:T(1,128)S(1)}, s32[1,16384]{1,0:T(1,128)}, u32[]{:S(2)}) copy-start(s32[1,16384]{1,0:T(1,128)} %param.23) | copy-start | bytes 196612
  17.1 36.3 %collective-permute-start = (bf16[256,4,128]{0,2,1:T(8,128)(2,1)}, bf16[256,4,128]{0,2,1:T(8,128)(2,1)}, u32[]{:S(2)}, u32[]{:S(2)}) collective-permute-start(bf16[256,4,128]{0,2,1:T(8,128)(2,1)} %get-tuple-element.4), channel_id=1, source_target_pairs={{0,16},{16,32},{32,48},{48,64},{64,80},{80,96},{96,112},{112,128},... | collective-permute-start | bytes 786440 | tf_op jit(solution)/shard_map/ppermute | solution.py:21
  22.5 30.9 %collective-permute-start.1 = (bf16[256,4,128]{0,2,1:T(8,128)(2,1)}, bf16[256,4,128]{0,2,1:T(8,128)(2,1)}, u32[]{:S(2)}, u32[]{:S(2)}) collective-permute-start(bf16[256,4,128]{0,2,1:T(8,128)(2,1)} %get-tuple-element.5), channel_id=1, source_target_pairs={{16,0},{32,16},{48,32},{64,48},{80,64},{96,80},{112,96},{128,112},... | collective-permute-start | bytes 786440 | tf_op jit(solution)/shard_map/ppermute | solution.py:24
  51.3 5.1 %copy-start.3 = (bf16[512,4,128]{0,2,1:T(8,128)(2,1)}, bf16[512,4,128]{0,2,1:T(8,128)(2,1)S(1)}, u32[]{:S(2)}) copy-start(bf16[512,4,128]{0,2,1:T(8,128)(2,1)S(1)} %slice.81) | copy-start | bytes 1572868
  92.0 1.4 slice-start
  101.7 55.3 %copy-start.17 = (bf16[512,4,64]{0,2,1:T(8,128)(2,1)S(1)}, bf16[512,4,64]{0,2,1:T(8,128)(2,1)}, u32[]{:S(2)}) copy-start(bf16[512,4,64]{0,2,1:T(8,128)(2,1)} %fusion.62) | copy-start | bytes 786436
  158.9 88.8 %all-gather.7.cloned.1.call-start = ((), (), s32[]{:S(2)}) async-start(), calls=%async_computation.3 | async-start | bytes 2621440 | tf_op jit(solution)/shard_map/all_gather | solution.py:196
  159.6 167.7 %reduce-scatter.2.cloned.1.call-start = ((), (), s32[]{:S(2)}) async-start(), calls=%async_computation.4 | async-start | bytes 2621440 | tf_op jit(solution)/shard_map/reduce_scatter | solution.py:328
  174.1 73.6 %copy-start.6 = (bf16[1,512,1024]{2,1,0:T(8,128)(2,1)S(1)}, bf16[1,512,1024]{2,1,0:T(8,128)(2,1)}, u32[]{:S(2)}) copy-start(bf16[1,512,1024]{2,1,0:T(8,128)(2,1)} %param.13) | copy-start | bytes 3145732
  251.8 1.0 copy-start.7
  262.5 1.0 copy-start.4
  262.5 1.8 copy-start.16
  266.5 63.6 %copy-start.13 = (f32[1024]{0:T(1024)S(1)}, f32[1024]{0:T(1024)}, u32[]{:S(2)}) copy-start(f32[1024]{0:T(1024)} %param.22) | copy-start | bytes 12292
  266.5 63.6 %copy-start.14 = (f32[1024]{0:T(1024)S(1)}, f32[1024]{0:T(1024)}, u32[]{:S(2)}) copy-start(f32[1024]{0:T(1024)} %param.21) | copy-start | bytes 12292
  266.5 37.4 %all-to-all-start = ((bf16[32,2,16,4,128]{4,3,2,1,0:T(4,128)(2,1)}), bf16[32,2,16,4,128]{4,3,2,1,0:T(4,128)(2,1)S(1)}, u32[]{:S(2)}, u32[]{:S(2)}) async-start(bf16[32,2,16,4,128]{4,3,2,1,0:T(4,128)(2,1)} %reshape.204), calls=%async_computation.1 | async-start | bytes 2097152 | tf_op jit(solution)/shard_map/all_to_all | solution.py:225
  327.4 5.7 %copy-start.1 = (bf16[1024,4,192]{0,2,1:T(8,128)(2,1)S(1)}, bf16[1024,4,192]{0,2,1:T(8,128)(2,1)}, u32[]{:S(2)}) copy-start(bf16[1024,4,192]{0,2,1:T(8,128)(2,1)} %param.14) | copy-start | bytes 4718596
  (2 other events, 1.4 us)
Sparse Core Ops, SparseCore 0:
  12.6 72.0 all-gather.8
  159.0 33.3 all-gather.4
  194.5 53.1 all-gather.6
  262.7 64.6 reduce-scatter.1

commit v3 on v2

--- a/solution.py
+++ b/solution.py
@@ -95,43 +95,57 @@
     return jnp.where(is_top, top, merged)
 
 
-def combine_kernel(n, top_lane, x_ref, out_ref, cur, got, send_sem, recv_sem):
-    me, partners = butterfly_partners(n)
-    row, col = enter(partners)
+def halving_kernel(n, top_lane, x_ref, out_ref, *scratch):
+    rounds = len(scratch) // 3
+    kept, got, sems = scratch[:rounds], scratch[rounds : 2 * rounds], scratch[2 * rounds :]
+    me = lax.axis_index("seq")
+    steps = []
+    step = n // 2
+    while step >= 1:
+        bit = (me // step) % 2
+        steps.append((me + step - 2 * step * bit, bit))
+        step //= 2
+    row, col = enter([partner for partner, _ in steps])
     source = x_ref
-    value = x_ref[...]
-    for k, partner in enumerate(partners):
+    for k, (partner, bit) in enumerate(steps):
+        half = source.shape[0] // 2
+        send_at = pl.multiple_of((1 - bit) * half, 8)
+        keep_at = pl.multiple_of(bit * half, 8)
         copy = pltpu.make_async_remote_copy(
-            src_ref=source,
-            dst_ref=got.at[k],
-            send_sem=send_sem.at[k],
-            recv_sem=recv_sem.at[k],
+            src_ref=source.at[pl.ds(send_at, half)],
+            dst_ref=got[k],
+            send_sem=sems[k].at[0],
+            recv_sem=sems[k].at[1],
             device_id=(partner, row, col),
             device_id_type=MESH,
         )
         copy.start()
         copy.wait()
-        value = merge_parts(value, got[k], top_lane)
-        if k + 1 < len(partners):
-            cur[k] = value
-            source = cur.at[k]
-    out_ref[...] = value
+        value = merge_parts(source[pl.ds(keep_at, half)], got[k][...], top_lane)
+        if k + 1 < rounds:
+            kept[k][...] = value
+            source = kept[k]
+        else:
+            out_ref[...] = value
 
 
 def seq_softmax_combine(parts, top_lane):
     n = lax.axis_size("seq")
     rounds = n.bit_length() - 1
+    rows, lanes = parts.shape
+    scratch = []
+    for k in range(rounds):
+        scratch.append(pltpu.VMEM((rows >> (k + 1), lanes), parts.dtype))
+    for k in range(rounds):
+        scratch.append(pltpu.VMEM((rows >> (k + 1), lanes), parts.dtype))
+    for k in range(rounds):
+        scratch.append(pltpu.SemaphoreType.DMA((2,)))
     return pl.pallas_call(
-        functools.partial(combine_kernel, n, top_lane),
-        out_shape=jax.ShapeDtypeStruct(parts.shape, parts.dtype),
+        functools.partial(halving_kernel, n, top_lane),
+        out_shape=jax.ShapeDtypeStruct((rows // n, lanes), parts.dtype),
         in_specs=[pl.BlockSpec(memory_space=pltpu.VMEM)],
         out_specs=pl.BlockSpec(memory_space=pltpu.VMEM),
-        scratch_shapes=[
-            pltpu.VMEM((max(rounds - 1, 1),) + parts.shape, parts.dtype),
-            pltpu.VMEM((rounds,) + parts.shape, parts.dtype),
-            pltpu.SemaphoreType.DMA((rounds,)),
-            pltpu.SemaphoreType.DMA((rounds,)),
-        ],
+        scratch_shapes=scratch,
         compiler_params=pltpu.CompilerParams(collective_id=1, has_side_effects=True),
     )(parts)
 
@@ -181,17 +195,18 @@
     own_rows = jnp.dot(picker, tokens, preferred_element_type=jnp.float32).astype(jnp.bfloat16)
     glob_rows = seq_gather(own_rows.reshape(-1, 128)).reshape(n_glob, width)
 
-    wg_rows = qkv_global_weight.shape[0]
+    w_global = lax.all_gather(
+        qkv_global_weight.reshape(qkv_global_weight.shape[0], -1), "row", axis=0, tiled=True
+    )
     fi_rows, units = ffn_in.shape
-    wg_flat = qkv_global_weight.reshape(-1)
     fi_flat = ffn_in.reshape(-1)
-    fo_flat = ffn_out.reshape(-1)
-    n_wg, n_fi = wg_flat.shape[0], fi_flat.shape[0]
-    everything = lax.all_gather(jnp.concatenate([wg_flat, fi_flat, fo_flat]), "row", axis=0)
-    w_global = everything[:, :n_wg].reshape(n_row * wg_rows, heads_here * triple)
-    f_in = everything[:, n_wg : n_wg + n_fi].reshape(n_row * fi_rows, units)
+    n_fi = fi_flat.shape[0]
+    everything = lax.all_gather(
+        jnp.concatenate([fi_flat, ffn_out.reshape(-1)]), "row", axis=0
+    )
+    f_in = everything[:, :n_fi].reshape(n_row * fi_rows, units)
     f_out = jnp.transpose(
-        everything[:, n_wg + n_fi :].reshape(n_row, units, ffn_out.shape[1]), (1, 0, 2)
+        everything[:, n_fi:].reshape(n_row, units, ffn_out.shape[1]), (1, 0, 2)
     ).reshape(units, n_row * ffn_out.shape[1])
     w_out = lax.all_gather(out_weight, "col", axis=0, tiled=True)
 
@@ -224,6 +239,7 @@
     outgoing = outgoing.reshape(n_seq, capacity, page_len, heads_here, 2 * head_dim)
     arrived = lax.all_to_all(outgoing, "seq", split_axis=0, concat_axis=0, tiled=True)
     page_pool = arrived[None, None]
+    page_pool, glob_rows = lax.optimization_barrier((page_pool, glob_rows))
 
     kv_ext = padded(kv_local, (("seq", 0),), HALF)
 
@@ -279,10 +295,12 @@
             jnp.broadcast_to(part_top[:, :, None], part_top.shape + (128 - head_dim - 1,)),
         ],
         axis=2,
-    ).reshape(heads_here * n_glob, 128)
-    merged = seq_softmax_combine(packed, head_dim + 1).reshape(heads_here, n_glob, 128)
-    glob_out = (merged[:, :, :head_dim] / merged[:, :, head_dim : head_dim + 1]).astype(
-        jnp.bfloat16
+    )
+    packed = jnp.transpose(packed, (1, 0, 2)).reshape(n_glob * heads_here, 128)
+    merged = seq_softmax_combine(packed, head_dim + 1).reshape(per_shard, heads_here, 128)
+    own_out = jnp.transpose(
+        (merged[:, :, :head_dim] / merged[:, :, head_dim : head_dim + 1]).astype(jnp.bfloat16),
+        (1, 0, 2),
     )
 
     glob_mask = query_seg[:, None] == glob_seg[None, :]
@@ -310,7 +328,6 @@
     )
     pieces = (numer / jnp.transpose(total)[:, :, None]).astype(jnp.bfloat16)
 
-    own_out = lax.dynamic_slice_in_dim(glob_out, seq_index * per_shard, per_shard, 1)
     placed = jnp.einsum("gt,hgd->thd", picker, own_out, preferred_element_type=jnp.float32).astype(
         jnp.bfloat16
     )

time: 341 us -> 382 us (1.12)
  waiting for transfers between devices: 146 us -> 193 us
  Pallas kernels: 70.2 us -> 57.1 us
  matrix products: 30.7 us -> 39 us
    reduce_scatter x1, waiting for transfers between devices: 23.5 us -> 54.4 us  [per_device(): lax.psum_scatter(jnp.dot(ffn_hidden, f_out, preferred_element_type=jnp.fl...]
    all_gather x1 -> x2, waiting for transfers between devices: 21.4 us -> 51.1 us  [the longest x1 51.1 us: per_device(): lax.all_gather(jnp.concatenate([fi_flat, ffn_out.reshape(-1)]), 'row', ax...]
    all_to_all x1, waiting for transfers between devices: 28.1 us -> 0.01 us  [per_device(): lax.all_to_all(outgoing, 'seq', split_axis=0, concat_axis=0, tiled=True)]
    pallas_call x1, Pallas kernels: 52.4 us -> 29.5 us  [seq_softmax_combine(): pl.pallas_call(functools.partial(halving_kernel, n, top_lane), out_shape=...]
    all_gather x1, waiting for transfers between devices: 18.3 us -> 33.1 us  [per_device(): attn_all = lax.all_gather(attention, 'col', axis=0)]
    pallas_call x1, Pallas kernels: 17.7 us -> 27.6 us  [seq_gather(): pl.pallas_call(functools.partial(gather_kernel, n), out_shape=jax.ShapeDt...]
    reshape x3 -> x1, local copies, waits for them, and re-layouts: 7.81 us -> 4.79 us  [per_device(): f_in = everything[:, :n_fi].reshape(n_row * fi_rows, units)]
    unnamed x41 -> x34, local copies, waits for them, and re-layouts: 7.76 us -> 8.74 us
  transfers between devices with their start and end apart: 7 -> 8, of which waited for: 5 -> 4; matrix products, arithmetic and copies ran while one was open for 12% -> 9% of each run, Pallas kernels for 5% -> 7%
where the time goes in v3:
time: 382 us; the launch traced here: 381 us
  waiting for transfers between devices  193 us (51%)
  Pallas kernels  57.1 us (15%)
  local copies, waits for them, and re-layouts  45.3 us (12%)
  matrix products  39 us (10%)
  starting transfers between devices  17.3 us (5%)
  other arithmetic  14.9 us (4%)
  between operations  14.2 us (4%)
    reduce_scatter x1, waiting for transfers between devices, per_device(): lax.psum_scatter(jnp.dot(ffn_hidden, f_out, preferred_element_type=jnp.fl...  54.4 us
    all_gather x1, waiting for transfers between devices, per_device(): w_out = lax.all_gather(out_weight, 'col', axis=0, tiled=True)  53 us
    all_gather x1, waiting for transfers between devices, per_device(): lax.all_gather(jnp.concatenate([fi_flat, ffn_out.reshape(-1)]), 'row', ax...  51.1 us
    all_gather x1, waiting for transfers between devices, per_device(): attn_all = lax.all_gather(attention, 'col', axis=0)  33.1 us
    pallas_call x1, Pallas kernels, seq_softmax_combine(): pl.pallas_call(functools.partial(halving_kernel, n, top_lane), out_shape=...  29.5 us
    pallas_call x1, Pallas kernels, seq_gather(): pl.pallas_call(functools.partial(gather_kernel, n), out_shape=jax.ShapeDt...  27.6 us
    all_to_all x1, starting transfers between devices, per_device(): lax.all_to_all(outgoing, 'seq', split_axis=0, concat_axis=0, tiled=True)  11.2 us
    dot_general x1, matrix products, per_device(): jnp.dot(ffn_hidden, f_out, preferred_element_type=jnp.float32)  9.8 us
  transfers between devices with their start and end apart: 8, of which 4 were waited for; matrix products, arithmetic and copies ran while one was open for 9% of the time, Pallas kernels for 7%

profile of v3, /device:TPU:1, one launch (start us, length us, event | category | flops | bytes accessed | tf_op | source)
XLA Modules:
  0.0 380.9 jit_solution(10596821452369992287)
XLA Ops:
  8.6 3.1 convolution_convert_fusion.2
  17.3 2.6 reshape.184
  19.8 11.2 %all-to-all-start = ((bf16[32,2,16,4,128]{4,3,2,1,0:T(4,128)(2,1)}), bf16[32,2,16,4,128]{4,3,2,1,0:T(4,128)(2,1)}, u32[]{:S(2)}, u32[]{:S(2)}) async-start(bf16[32,2,16,4,128]{4,3,2,1,0:T(4,128)(2,1)} %reshape.184), calls=%async_computation | async-start | bytes 2097152 | tf_op jit(solution)/shard_map/all_to_all | solution.py:240
  32.7 3.5 collective-permute-start
  36.2 2.1 collective-permute-start.1
  42.2 27.6 %shard_map.140 = bf16[32,32,128]{2,1,0:T(8,128)(2,1)} custom-call(bf16[32,128]{1,0:T(8,128)(2,1)} %reshape.185.x_ref), custom_call_target="tpu_custom_call" | custom-call | tf_op jit(solution)/shard_map/pallas_call | solution.py:74
  74.5 4.8 %select_reduce_fusion = (f32[4,512]{1,0:T(4,128)S(1)}, f32[4,512,1024]{2,1,0:T(8,128)}) fusion(pred[512,1024]{1,0:T(8,128)(4,1)S(1)} %fusion.15, bf16[1024,4,128]{0,2,1:T(8,128)(2,1)S(1)} %pad_maximum_fusion, bf16[512,4,192]{0,2,1:T(8,128)(2,1)S(1)} %bitcast.94), kind=kOutput, calls=%fused_computation.3 | convolution fusion | flops 274724864 | bytes 9707520 | tf_op jit(solution)/shard_map/qhd,khd->hqk/dot_general | solution.py:309
  82.3 5.0 %fusion = f32[4,512]{1,0:T(4,128)S(1)} fusion(f32[4,512,1024]{2,1,0:T(8,128)} %get-tuple-element.11, f32[4,512]{1,0:T(4,128)S(1)} %max.7, pred[512,1024]{1,0:T(8,128)(4,1)S(1)} %copy-done.5), kind=kLoop, calls=%fused_computation.4 | loop fusion | flops 8386560 | bytes 8929280 | tf_op jit(solution)/shard_map/reduce_sum | solution.py:322
  88.6 2.9 fusion.62
  91.5 2.1 convolution_convert_fusion.5
  94.4 3.3 convolution_convert_fusion.1
  102.7 29.5 %shard_map.141 = f32[16,128]{1,0:T(8,128)} custom-call(f32[512,128]{1,0:T(8,128)} %bitcast.100), custom_call_target="tpu_custom_call" | custom-call | tf_op jit(solution)/shard_map/pallas_call | solution.py:143
  138.9 33.1 %all-gather.8.cloned.1.call-done = bf16[4,512,256]{2,1,0:T(8,128)(2,1)} async-done(((bf16[1,512,256]{2,1,0:T(8,128)(2,1)}), bf16[4,512,256]{2,1,0:T(8,128)(2,1)}) %all-gather.8.cloned.1.call-update) | async-done | bytes 1048592 | tf_op jit(solution)/shard_map/all_gather | solution.py:339
  172.0 2.3 copy.86
  174.3 53.0 %all-gather.10.cloned.1.call-done = bf16[1024,1024]{1,0:T(8,128)(2,1)} async-done(((bf16[256,1024]{1,0:T(8,128)(2,1)}), bf16[1024,1024]{1,0:T(8,128)(2,1)}) %all-gather.10.cloned.1.call-update) | async-done | bytes 2097168 | tf_op jit(solution)/shard_map/all_gather | solution.py:211
  227.3 3.3 fusion.139
  231.7 51.1 %all-gather.12.cloned.1.call-done = bf16[2097152]{0:T(1024)(128)(2,1)} async-done(((bf16[524288]{0:T(1024)(128)(2,1)}), bf16[2097152]{0:T(1024)(128)(2,1)}) %all-gather.12.cloned.1.call-update) | async-done | bytes 4194320 | tf_op jit(solution)/shard_map/all_gather | solution.py:204
  282.7 5.7 %reshape.207 = bf16[4,524288]{1,0:T(4,128)(2,1)} reshape(bf16[2097152]{0:T(1024)(128)(2,1)} %all-gather.12.cloned.1.call-done) | data formatting | bytes 8388608 | tf_op jit(solution)/shard_map/all_gather | solution.py:204
  288.4 4.0 %fusion.137 = (bf16[4,262144]{1,0:T(4,128)(2,1)}, bf16[4,262144]{1,0:T(4,128)(2,1)S(1)}) fusion(bf16[4,524288]{1,0:T(4,128)(2,1)} %reshape.207), kind=kLoop, calls=%fused_computation.185 | loop fusion | bytes 8388608 | tf_op jit(solution)/shard_map/slice | solution.py:207
  294.1 4.0 %copy.87 = bf16[1024,4,256]{0,2,1:T(8,128)(2,1)} copy(bf16[1024,4,256]{2,0,1:T(8,128)(2,1)} %bitcast.88) | data formatting | bytes 4194304 | tf_op jit(solution)/shard_map/transpose | solution.py:208
  298.1 4.8 %reshape.196 = bf16[1024,1024]{1,0:T(8,128)(2,1)} reshape(bf16[4,262144]{1,0:T(4,128)(2,1)} %get-tuple-element.6) | data formatting | bytes 4194304 | tf_op jit(solution)/shard_map/reshape | solution.py:207
  302.8 9.8 %fusion.24 = f32[512,1024]{1,0:T(8,128)} fusion(bf16[1024,1024]{0,1:T(8,128)(2,1)} %bitcast.97, bf16[512,1024]{1,0:T(8,128)(2,1)S(1)} %add_convert_fusion, bf16[1024,1024]{1,0:T(8,128)(2,1)} %reshape.196), kind=kOutput, calls=%fused_computation.45 | convolution fusion | flops 2181562368 | bytes 7340032 | tf_op jit(solution)/shard_map/dot_general | solution.py:346
  312.7 54.4 %reduce-scatter.2.cloned.1.call-done = f32[128,1024]{1,0:T(8,128)} async-done(((f32[512,1024]{1,0:T(8,128)}), f32[128,1024]{1,0:T(8,128)}) %reduce-scatter.2.cloned.1.call-update) | async-done | bytes 524304 | tf_op jit(solution)/shard_map/reduce_scatter | solution.py:345
  371.5 2.8 copy.104
  (103 shorter events, 40.6 us)
Async XLA Ops:
  7.2 1.4 copy-start
  11.7 4.0 %copy-start.14 = (s32[1,32,1]{1,2,0:T(1,128)S(1)}, s32[1,32,1]{1,2,0:T(1,128)}, u32[]{:S(2)}) copy-start(s32[1,32,1]{1,2,0:T(1,128)} %param.25) | copy-start | bytes 388
  19.8 18.5 %copy-start.13 = (s32[1,128]{1,0:T(1,128)S(1)}, s32[1,128]{1,0:T(1,128)}, u32[]{:S(2)}) copy-start(s32[1,128]{1,0:T(1,128)} %param.24) | copy-start | bytes 1540
  19.8 20.1 %copy-start.2 = (s32[1,16384]{1,0:T(1,128)S(1)}, s32[1,16384]{1,0:T(1,128)}, u32[]{:S(2)}) copy-start(s32[1,16384]{1,0:T(1,128)} %param.23) | copy-start | bytes 196612
  19.8 59.5 %all-to-all-start = ((bf16[32,2,16,4,128]{4,3,2,1,0:T(4,128)(2,1)}), bf16[32,2,16,4,128]{4,3,2,1,0:T(4,128)(2,1)}, u32[]{:S(2)}, u32[]{:S(2)}) async-start(bf16[32,2,16,4,128]{4,3,2,1,0:T(4,128)(2,1)} %reshape.184), calls=%async_computation | async-start | bytes 2097152 | tf_op jit(solution)/shard_map/all_to_all | solution.py:240
  31.1 60.4 %all-gather.6.cloned.1.call-start = ((), (), s32[]{:S(2)}) async-start(), calls=%async_computation.2 | async-start | bytes 1966080 | tf_op jit(solution)/shard_map/all_gather | solution.py:198
  31.8 140.2 %all-gather.8.cloned.1.call-start = ((), (), s32[]{:S(2)}) async-start(), calls=%async_computation.3 | async-start | bytes 1310720 | tf_op jit(solution)/shard_map/all_gather | solution.py:339
  32.7 39.4 %collective-permute-start = (bf16[256,4,128]{0,2,1:T(8,128)(2,1)}, bf16[256,4,128]{0,2,1:T(8,128)(2,1)}, u32[]{:S(2)}, u32[]{:S(2)}) collective-permute-start(bf16[256,4,128]{0,2,1:T(8,128)(2,1)} %get-tuple-element.8), channel_id=1, source_target_pairs={{0,16},{16,32},{32,48},{48,64},{64,80},{80,96},{96,112},{112,128},... | collective-permute-start | bytes 786440 | tf_op jit(solution)/shard_map/ppermute | solution.py:21
  36.2 35.9 %collective-permute-start.1 = (bf16[256,4,128]{0,2,1:T(8,128)(2,1)}, bf16[256,4,128]{0,2,1:T(8,128)(2,1)}, u32[]{:S(2)}, u32[]{:S(2)}) collective-permute-start(bf16[256,4,128]{0,2,1:T(8,128)(2,1)} %get-tuple-element.9), channel_id=1, source_target_pairs={{16,0},{32,16},{48,32},{64,48},{80,64},{96,80},{112,96},{128,112},... | collective-permute-start | bytes 786440 | tf_op jit(solution)/shard_map/ppermute | solution.py:24
  72.1 1.4 copy-start.4
  73.5 1.0 copy-start.6
  79.3 2.9 copy-start.5
  82.2 6.3 %copy-start.1 = (f32[4,512,1024]{2,1,0:T(8,128)S(1)}, f32[4,512,1024]{2,1,0:T(8,128)}, u32[]{:S(2)}) copy-start(f32[4,512,1024]{2,1,0:T(8,128)} %get-tuple-element.11) | copy-start | bytes 25165828
  82.3 6.3 %copy-start.7 = (bf16[1024,4,128]{0,2,1:T(8,128)(2,1)S(1)}, bf16[1024,4,128]{0,2,1:T(8,128)(2,1)}, u32[]{:S(2)}) copy-start(bf16[1024,4,128]{0,2,1:T(8,128)(2,1)} %copy-done.6) | copy-start | bytes 3145732
  91.5 3.0 copy-start.3
  101.4 34.6 %copy-start.8 = (bf16[256,1024]{1,0:T(8,128)(2,1)S(1)}, bf16[256,1024]{1,0:T(8,128)(2,1)}, u32[]{:S(2)}) copy-start(bf16[256,1024]{1,0:T(8,128)(2,1)} %param.19) | copy-start | bytes 1572868
  135.2 92.1 %all-gather.10.cloned.1.call-start = ((), (), s32[]{:S(2)}) async-start(), calls=%async_computation.4 | async-start | bytes 2621440 | tf_op jit(solution)/shard_map/all_gather | solution.py:211
  135.9 146.8 %all-gather.12.cloned.1.call-start = ((), (), s32[]{:S(2)}) async-start(), calls=%async_computation.6 | async-start | bytes 5242880 | tf_op jit(solution)/shard_map/all_gather | solution.py:204
  138.6 228.5 %reduce-scatter.2.cloned.1.call-start = ((), (), s32[]{:S(2)}) async-start(), calls=%async_computation.5 | async-start | bytes 2621440 | tf_op jit(solution)/shard_map/reduce_scatter | solution.py:345
  230.6 0.7 copy-start.9
  230.6 0.7 copy-start.10
  312.6 56.9 %copy-start.11 = (f32[1024]{0:T(1024)S(1)}, f32[1024]{0:T(1024)}, u32[]{:S(2)}) copy-start(f32[1024]{0:T(1024)} %param.22) | copy-start | bytes 12292
  312.6 56.9 %copy-start.12 = (f32[1024]{0:T(1024)S(1)}, f32[1024]{0:T(1024)}, u32[]{:S(2)}) copy-start(f32[1024]{0:T(1024)} %param.21) | copy-start | bytes 12292
Sparse Core Ops, SparseCore 0:
  34.0 37.3 all-gather.5
  135.3 36.6 all-gather.7
  174.1 53.1 all-gather.9
  229.8 52.8 all-gather.11
  312.8 54.2 reduce-scatter.1

commit v4 on v3

--- a/solution.py
+++ b/solution.py
@@ -148,6 +148,99 @@
         scratch_shapes=scratch,
         compiler_params=pltpu.CompilerParams(collective_id=1, has_side_effects=True),
     )(parts)
+
+
+def col_peers():
+    me, m = lax.axis_index("col"), lax.axis_size("col")
+    seq, row = lax.axis_index("seq"), lax.axis_index("row")
+    peers = [lax.rem(me + j, m) for j in range(1, m)]
+    barrier = pltpu.get_barrier_semaphore()
+    for peer in peers:
+        pl.semaphore_signal(barrier, inc=1, device_id=(seq, row, peer), device_id_type=MESH)
+    pl.semaphore_wait(barrier, len(peers))
+    return me, [(seq, row, peer) for peer in peers]
+
+
+def col_gather_kernel(x_ref, out_ref, self_sem, send_sem, recv_sem):
+    me, peers = col_peers()
+    own = pltpu.make_async_copy(x_ref, out_ref.at[me], self_sem)
+    own.start()
+    copies = []
+    for j, peer in enumerate(peers):
+        copy = pltpu.make_async_remote_copy(
+            src_ref=x_ref,
+            dst_ref=out_ref.at[me],
+            send_sem=send_sem.at[j],
+            recv_sem=recv_sem.at[j],
+            device_id=peer,
+            device_id_type=MESH,
+        )
+        copy.start()
+        copies.append(copy)
+    own.wait()
+    for copy in copies:
+        copy.wait()
+
+
+def col_gather(block):
+    m = lax.axis_size("col")
+    return pl.pallas_call(
+        col_gather_kernel,
+        out_shape=jax.ShapeDtypeStruct((m,) + block.shape, block.dtype),
+        in_specs=[pl.BlockSpec(memory_space=pltpu.VMEM)],
+        out_specs=pl.BlockSpec(memory_space=pltpu.VMEM),
+        scratch_shapes=[
+            pltpu.SemaphoreType.DMA(()),
+            pltpu.SemaphoreType.DMA((m - 1,)),
+            pltpu.SemaphoreType.DMA((m - 1,)),
+        ],
+        compiler_params=pltpu.CompilerParams(collective_id=2, has_side_effects=True),
+    )(block)
+
+
+def col_sum_kernel(x_ref, own_ref, out_ref, got, send_sem, recv_sem):
+    me, peers = col_peers()
+    copies = []
+    for j, peer in enumerate(peers):
+        copy = pltpu.make_async_remote_copy(
+            src_ref=x_ref.at[peer[2]],
+            dst_ref=got.at[j],
+            send_sem=send_sem.at[j],
+            recv_sem=recv_sem.at[j],
+            device_id=peer,
+            device_id_type=MESH,
+        )
+        copy.start()
+        copies.append(copy)
+    for copy in copies:
+        copy.wait()
+    chunk = 32
+
+    def body(i, carry):
+        rows = pl.ds(pl.multiple_of(i * chunk, chunk), chunk)
+        total = own_ref[rows, :]
+        for j in range(len(copies)):
+            total = total + got[j, rows, :].astype(jnp.float32)
+        out_ref[rows, :] = total
+        return carry
+
+    lax.fori_loop(0, out_ref.shape[0] // chunk, body, 0)
+
+
+def col_reduce_scatter(parts, own):
+    m = lax.axis_size("col")
+    return pl.pallas_call(
+        col_sum_kernel,
+        out_shape=jax.ShapeDtypeStruct(own.shape, jnp.float32),
+        in_specs=[pl.BlockSpec(memory_space=pltpu.VMEM)] * 2,
+        out_specs=pl.BlockSpec(memory_space=pltpu.VMEM),
+        scratch_shapes=[
+            pltpu.VMEM((m - 1,) + parts.shape[1:], parts.dtype),
+            pltpu.SemaphoreType.DMA((m - 1,)),
+            pltpu.SemaphoreType.DMA((m - 1,)),
+        ],
+        compiler_params=pltpu.CompilerParams(collective_id=3, has_side_effects=True),
+    )(parts, own)
 
 
 def layer_norm(values, gain, bias):
@@ -297,6 +390,7 @@
         axis=2,
     )
     packed = jnp.transpose(packed, (1, 0, 2)).reshape(n_glob * heads_here, 128)
+    packed, everything = lax.optimization_barrier((packed, everything))
     merged = seq_softmax_combine(packed, head_dim + 1).reshape(per_shard, heads_here, 128)
     own_out = jnp.transpose(
         (merged[:, :, :head_dim] / merged[:, :, head_dim : head_dim + 1]).astype(jnp.bfloat16),
@@ -336,21 +430,21 @@
         shard_len, heads_here * head_dim
     )
 
-    attn_all = lax.all_gather(attention, "col", axis=0)
+    attention, w_out = lax.optimization_barrier((attention, w_out))
+    attn_all = col_gather(attention)
     attn_full = jnp.transpose(attn_all, (1, 0, 2)).reshape(shard_len, n_col * heads_here * head_dim)
     proj = jnp.dot(attn_full, w_out, preferred_element_type=jnp.float32)
     middle = layer_norm(tokens.astype(jnp.float32) + proj, ln_gain, ln_bias).astype(jnp.bfloat16)
     ffn_pre = jnp.dot(middle, f_in, preferred_element_type=jnp.float32)
     ffn_hidden = jax.nn.gelu(ffn_pre, approximate=False).astype(jnp.bfloat16)
-    ffn_part = lax.psum_scatter(
-        jnp.dot(ffn_hidden, f_out, preferred_element_type=jnp.float32),
-        "col",
-        scatter_dimension=0,
-        tiled=True,
-    )
     out_rows = shard_len // n_col
+    ffn_full = jnp.dot(ffn_hidden, f_out, preferred_element_type=jnp.float32)
+    ffn_own = lax.dynamic_slice_in_dim(ffn_full, col_index * out_rows, out_rows, 0)
     mine = lax.dynamic_slice_in_dim(middle, col_index * out_rows, out_rows, 0).astype(jnp.float32)
-    normed = layer_norm(mine + ffn_part, ln2_gain, ln2_bias)
+    second = col_reduce_scatter(
+        ffn_full.astype(jnp.bfloat16).reshape(n_col, out_rows, width), mine + ffn_own
+    )
+    normed = layer_norm(second, ln2_gain, ln2_bias)
     return (normed.astype(jnp.bfloat16)[None], page_pool)
 
 

time: 382 us -> 277 us (0.73)
  the two profiles are of different devices: /device:TPU:1 before, /device:TPU:32 now
where the time goes in v4:
time: 277 us; the launch traced here: 275 us
  Pallas kernels  119 us (43%)
  local copies, waits for them, and re-layouts  47.8 us (17%)
  matrix products  36.1 us (13%)
  waiting for transfers between devices  22.1 us (8%)
  other arithmetic  18.4 us (7%)
  starting transfers between devices  17.7 us (6%)
  between operations  14.2 us (5%)
    pallas_call x1, Pallas kernels, col_reduce_scatter(): pl.pallas_call(col_sum_kernel, out_shape=jax.ShapeDtypeStruct(own.shape,...  31.7 us
    pallas_call x1, Pallas kernels, col_gather(): pl.pallas_call(col_gather_kernel, out_shape=jax.ShapeDtypeStruct((m,) + b...  31.5 us
    pallas_call x1, Pallas kernels, seq_gather(): pl.pallas_call(functools.partial(gather_kernel, n), out_shape=jax.ShapeDt...  30.6 us
    pallas_call x1, Pallas kernels, seq_softmax_combine(): pl.pallas_call(functools.partial(halving_kernel, n, top_lane), out_shape=...  25.2 us
    all_gather x1, waiting for transfers between devices, per_device(): w_out = lax.all_gather(out_weight, 'col', axis=0, tiled=True)  20.7 us
    unnamed x40, local copies, waits for them, and re-layouts  11.3 us
    dot_general x1, matrix products, per_device(): ffn_full = jnp.dot(ffn_hidden, f_out, preferred_element_type=jnp.float32)  10.1 us
    all_to_all x1, starting transfers between devices, per_device(): lax.all_to_all(outgoing, 'seq', split_axis=0, concat_axis=0, tiled=True)  9.97 us
  transfers between devices with their start and end apart: 6, of which 2 were waited for; matrix products, arithmetic and copies ran while one was open for 22% of the time, Pallas kernels for 20%

profile of v4, /device:TPU:32, one launch (start us, length us, event | category | flops | bytes accessed | tf_op | source)
XLA Modules:
  0.0 275.3 jit_solution(17700534373300147899)
XLA Ops:
  11.7 1.9 convolution_convert_fusion.2
  19.3 2.6 reshape.190
  21.9 10.0 %all-to-all-start = ((bf16[32,2,16,4,128]{4,3,2,1,0:T(4,128)(2,1)}), bf16[32,2,16,4,128]{4,3,2,1,0:T(4,128)(2,1)}, u32[]{:S(2)}, u32[]{:S(2)}) async-start(bf16[32,2,16,4,128]{4,3,2,1,0:T(4,128)(2,1)} %reshape.190), calls=%async_computation | async-start | bytes 2097152 | tf_op jit(solution)/shard_map/all_to_all | solution.py:333
  32.8 2.0 collective-permute-start
  34.8 5.6 %collective-permute-start.1 = (bf16[256,4,128]{0,2,1:T(8,128)(2,1)}, bf16[256,4,128]{0,2,1:T(8,128)(2,1)}, u32[]{:S(2)}, u32[]{:S(2)}) collective-permute-start(bf16[256,4,128]{0,2,1:T(8,128)(2,1)} %get-tuple-element.15), channel_id=1, source_target_pairs={{16,0},{32,16},{48,32},{64,48},{80,64},{96,80},{112,96},{128,112},... | collective-permute-start | bytes 786440 | tf_op jit(solution)/shard_map/ppermute | solution.py:24
  44.5 30.6 %shard_map.140 = bf16[32,32,128]{2,1,0:T(8,128)(2,1)} custom-call(bf16[32,128]{1,0:T(8,128)(2,1)} %reshape.191.x_ref), custom_call_target="tpu_custom_call" | custom-call | tf_op jit(solution)/shard_map/pallas_call | solution.py:74
  79.8 4.8 %select_reduce_fusion = (f32[4,512]{1,0:T(4,128)S(1)}, f32[4,512,1024]{2,1,0:T(8,128)}) fusion(pred[512,1024]{1,0:T(8,128)(4,1)S(1)} %fusion.15, bf16[1024,4,128]{0,2,1:T(8,128)(2,1)S(1)} %pad_maximum_fusion.1, bf16[512,4,192]{0,2,1:T(8,128)(2,1)S(1)} %bitcast.94), kind=kOutput, calls=%fused_computation.3 | convolution fusion | flops 274724864 | bytes 9707520 | tf_op jit(solution)/shard_map/qhd,khd->hqk/dot_general | solution.py:403
  86.5 5.0 %fusion = f32[4,512]{1,0:T(4,128)S(1)} fusion(f32[4,512,1024]{2,1,0:T(8,128)} %get-tuple-element.17, f32[4,512]{1,0:T(4,128)S(1)} %max.7, pred[512,1024]{1,0:T(8,128)(4,1)S(1)} %copy-done.8), kind=kLoop, calls=%fused_computation.4 | loop fusion | flops 8386560 | bytes 8929280 | tf_op jit(solution)/shard_map/reduce_sum | solution.py:416
  92.5 2.9 %fusion.62 = bf16[512,4,64]{0,2,1:T(8,128)(2,1)} fusion(f32[4,64,512]{2,1,0:T(8,128)S(1)} %fusion.69, f32[4,512,1024]{2,1,0:T(8,128)S(1)} %copy-done.2, f32[4,512]{1,0:T(4,128)S(1)} %max.7, pred[512,1024]{1,0:T(8,128)(4,1)S(1)} %copy-done.8, bf16[1024,4,128]{0,2,1:T(8,128)(2,1)S(1)} %copy-done.10, f32[512,4]{0,1:T(4,128)S(1)} %add_bitcast_fusion), kind=kOutput, calls=%fused_computation.86 | convolution fusion | flops 277217280 | bytes 10240000 | tf_op jit(solution)/shard_map/hqk,khd->qhd/dot_general | solution.py:417
  95.4 2.1 convolution_convert_fusion.5
  98.4 3.3 %convolution_convert_fusion.1 = bf16[512,768]{1,0:T(8,128)(2,1)} fusion(bf16[1024,768]{0,1:T(8,128)(2,1)} %all-gather.5.cloned.1.call-done, bf16[1,512,1024]{2,1,0:T(8,128)(2,1)S(1)} %copy-done.6), kind=kOutput, calls=%fused_computation.34 | convolution fusion | flops 805699584 | bytes 3407872 | tf_op jit(solution)/shard_map/dot_general | solution.py:351
  107.3 5.7 %reshape.215 = bf16[4,524288]{1,0:T(4,128)(2,1)} reshape(bf16[2097152]{0:T(1024)(128)(2,1)} %all-gather.9.cloned.1.call-done) | data formatting | bytes 8388608 | tf_op jit(solution)/shard_map/all_gather | solution.py:297
  112.9 4.4 %fusion.136 = (bf16[4,262144]{1,0:T(4,128)(2,1)}, bf16[4,262144]{1,0:T(4,128)(2,1)}) fusion(bf16[4,524288]{1,0:T(4,128)(2,1)} %reshape.215), kind=kLoop, calls=%fused_computation.184 | loop fusion | bytes 8388608 | tf_op jit(solution)/shard_map/slice | solution.py:300
  117.3 25.2 %shard_map.141 = f32[16,128]{1,0:T(8,128)} custom-call(f32[512,128]{1,0:T(8,128)} %bitcast.102), custom_call_target="tpu_custom_call" | custom-call | tf_op jit(solution)/shard_map/pallas_call | solution.py:143
  144.4 20.7 %all-gather.7.cloned.1.call-done = bf16[1024,1024]{1,0:T(8,128)(2,1)} async-done(((bf16[256,1024]{1,0:T(8,128)(2,1)}), bf16[1024,1024]{1,0:T(8,128)(2,1)}) %all-gather.7.cloned.1.call-update) | async-done | bytes 2097168 | tf_op jit(solution)/shard_map/all_gather | solution.py:304
  166.0 31.5 %shard_map.142 = bf16[4,512,256]{2,1,0:T(8,128)(2,1)} custom-call(bf16[512,256]{1,0:T(8,128)(2,1)} %copy.78.x_ref), custom_call_target="tpu_custom_call" | custom-call | tf_op jit(solution)/shard_map/pallas_call | solution.py:187
  197.5 2.3 copy.79
  199.8 3.3 %fusion.138 = (f32[512]{0:T(512)S(1)}, f32[512,1024]{1,0:T(8,128)S(1)}) fusion(bf16[512,1024]{0,1:T(8,128)(2,1)} %bitcast.97, bf16[1024,1024]{1,0:T(8,128)(2,1)} %all-gather.7.cloned.1.call-done, bf16[1,512,1024]{2,1,0:T(8,128)(2,1)S(1)} %copy-done.6), kind=kOutput, calls=%fused_computation.186 | convolution fusion | flops 1075314176 | bytes 6293504 | tf_op jit(solution)/shard_map/dot_general | solution.py:436
  207.0 4.0 %copy.80 = bf16[1024,4,256]{0,2,1:T(8,128)(2,1)} copy(bf16[1024,4,256]{2,0,1:T(8,128)(2,1)} %bitcast.88) | data formatting | bytes 4194304 | tf_op jit(solution)/shard_map/transpose | solution.py:301
  211.0 4.8 %reshape.203 = bf16[1024,1024]{1,0:T(8,128)(2,1)} reshape(bf16[4,262144]{1,0:T(4,128)(2,1)} %get-tuple-element.12) | data formatting | bytes 4194304 | tf_op jit(solution)/shard_map/reshape | solution.py:300
  215.8 2.0 add_convert_fusion
  217.8 10.1 %fusion.139 = (bf16[512,1024]{1,0:T(8,128)(2,1)}, f32[512,1024]{1,0:T(8,128)}) fusion(bf16[1024,1024]{0,1:T(8,128)(2,1)} %bitcast.98, bf16[512,1024]{1,0:T(8,128)(2,1)S(1)} %add_convert_fusion, bf16[1024,1024]{1,0:T(8,128)(2,1)} %reshape.203), kind=kOutput, calls=%fused_computation.187 | convolution fusion | flops 2182086656 | bytes 8388608 | tf_op jit(solution)/shard_map/dot_general | solution.py:441
  229.9 31.7 %shard_map.143 = f32[128,1024]{1,0:T(8,128)} custom-call(bf16[4,128,1024]{2,1,0:T(8,128)(2,1)} %bitcast.101, f32[128,1024]{1,0:T(8,128)} %dynamic-slice_add_fusion.own_ref), custom_call_target="tpu_custom_call" | custom-call | tf_op jit(solution)/shard_map/pallas_call | solution.py:232
  265.9 2.8 %copy.97 = bf16[1,1,32,2,16,4,128]{6,5,4,3,2,1,0:T(4,128)(2,1)} copy(bf16[1,1,32,2,16,4,128]{6,5,4,3,2,1,0:T(4,128)(2,1)} %bitcast.9) | data formatting | bytes 2097152
  (106 shorter events, 41.7 us)
Async XLA Ops:
  7.2 4.6 %copy-start = (bf16[1024,4,192]{0,2,1:T(8,128)(2,1)S(1)}, bf16[1024,4,192]{0,2,1:T(8,128)(2,1)}, u32[]{:S(2)}) copy-start(bf16[1024,4,192]{0,2,1:T(8,128)(2,1)} %param.14) | copy-start | bytes 4718596
  7.2 88.2 %all-gather.5.cloned.1.call-start = ((), (), s32[]{:S(2)}) async-start(), calls=%async_computation.1 | async-start | bytes 1966080 | tf_op jit(solution)/shard_map/all_gather | solution.py:291
  7.9 99.4 %all-gather.9.cloned.1.call-start = ((), (), s32[]{:S(2)}) async-start(), calls=%async_computation.3 | async-start | bytes 5242880 | tf_op jit(solution)/shard_map/all_gather | solution.py:297
  9.1 2.6 copy-start.5
  13.7 4.0 %copy-start.16 = (s32[1,32,1]{1,2,0:T(1,128)S(1)}, s32[1,32,1]{1,2,0:T(1,128)}, u32[]{:S(2)}) copy-start(s32[1,32,1]{1,2,0:T(1,128)} %param.25) | copy-start | bytes 388
  21.9 18.6 %copy-start.15 = (s32[1,128]{1,0:T(1,128)S(1)}, s32[1,128]{1,0:T(1,128)}, u32[]{:S(2)}) copy-start(s32[1,128]{1,0:T(1,128)} %param.24) | copy-start | bytes 1540
  21.9 20.2 %copy-start.4 = (s32[1,16384]{1,0:T(1,128)S(1)}, s32[1,16384]{1,0:T(1,128)}, u32[]{:S(2)}) copy-start(s32[1,16384]{1,0:T(1,128)} %param.23) | copy-start | bytes 196612
  21.9 62.7 %all-to-all-start = ((bf16[32,2,16,4,128]{4,3,2,1,0:T(4,128)(2,1)}), bf16[32,2,16,4,128]{4,3,2,1,0:T(4,128)(2,1)}, u32[]{:S(2)}, u32[]{:S(2)}) async-start(bf16[32,2,16,4,128]{4,3,2,1,0:T(4,128)(2,1)} %reshape.190), calls=%async_computation | async-start | bytes 2097152 | tf_op jit(solution)/shard_map/all_to_all | solution.py:333
  31.9 133.3 %all-gather.7.cloned.1.call-start = ((), (), s32[]{:S(2)}) async-start(), calls=%async_computation.2 | async-start | bytes 2621440 | tf_op jit(solution)/shard_map/all_gather | solution.py:304
  32.8 44.6 %collective-permute-start = (bf16[256,4,128]{0,2,1:T(8,128)(2,1)}, bf16[256,4,128]{0,2,1:T(8,128)(2,1)}, u32[]{:S(2)}, u32[]{:S(2)}) collective-permute-start(bf16[256,4,128]{0,2,1:T(8,128)(2,1)} %get-tuple-element.14), channel_id=1, source_target_pairs={{0,16},{16,32},{32,48},{48,64},{64,80},{80,96},{96,112},{112,128},... | collective-permute-start | bytes 786440 | tf_op jit(solution)/shard_map/ppermute | solution.py:21
  34.8 42.6 %collective-permute-start.1 = (bf16[256,4,128]{0,2,1:T(8,128)(2,1)}, bf16[256,4,128]{0,2,1:T(8,128)(2,1)}, u32[]{:S(2)}, u32[]{:S(2)}) collective-permute-start(bf16[256,4,128]{0,2,1:T(8,128)(2,1)} %get-tuple-element.15), channel_id=1, source_target_pairs={{16,0},{32,16},{48,32},{64,48},{80,64},{96,80},{112,96},{128,112},... | collective-permute-start | bytes 786440 | tf_op jit(solution)/shard_map/ppermute | solution.py:24
  77.4 1.4 copy-start.7
  78.8 1.0 copy-start.9
  85.4 1.1 copy-start.8
  86.1 5.4 %copy-start.10 = (bf16[1024,4,128]{0,2,1:T(8,128)(2,1)S(1)}, bf16[1024,4,128]{0,2,1:T(8,128)(2,1)}, u32[]{:S(2)}) copy-start(bf16[1024,4,128]{0,2,1:T(8,128)(2,1)} %copy-done.9) | copy-start | bytes 3145732
  86.5 6.1 %copy-start.2 = (f32[4,512,1024]{2,1,0:T(8,128)S(1)}, f32[4,512,1024]{2,1,0:T(8,128)}, u32[]{:S(2)}) copy-start(f32[4,512,1024]{2,1,0:T(8,128)} %get-tuple-element.17) | copy-start | bytes 25165828
  95.4 3.0 %copy-start.6 = (bf16[1,512,1024]{2,1,0:T(8,128)(2,1)S(1)}, bf16[1,512,1024]{2,1,0:T(8,128)(2,1)}, u32[]{:S(2)}) copy-start(bf16[1,512,1024]{2,1,0:T(8,128)(2,1)} %param.13) | copy-start | bytes 3145732
  112.9 30.5 %copy-start.17 = (bf16[512,4,64]{0,2,1:T(8,128)(2,1)S(1)}, bf16[512,4,64]{0,2,1:T(8,128)(2,1)}, u32[]{:S(2)}) copy-start(bf16[512,4,64]{0,2,1:T(8,128)(2,1)} %fusion.62) | copy-start | bytes 786436
  203.1 1.4 copy-start.1
  203.1 2.3 copy-start.3
  211.0 4.8 %copy-start.11 = (f32[1024]{0:T(1024)S(1)}, f32[1024]{0:T(1024)}, u32[]{:S(2)}) copy-start(f32[1024]{0:T(1024)} %param.18) | copy-start | bytes 12292
  211.0 4.8 %copy-start.12 = (f32[1024]{0:T(1024)S(1)}, f32[1024]{0:T(1024)}, u32[]{:S(2)}) copy-start(f32[1024]{0:T(1024)} %param.17) | copy-start | bytes 12292
  228.0 36.0 %copy-start.13 = (f32[1024]{0:T(1024)S(1)}, f32[1024]{0:T(1024)}, u32[]{:S(2)}) copy-start(f32[1024]{0:T(1024)} %param.22) | copy-start | bytes 12292
  228.0 36.0 %copy-start.14 = (f32[1024]{0:T(1024)S(1)}, f32[1024]{0:T(1024)}, u32[]{:S(2)}) copy-start(f32[1024]{0:T(1024)} %param.21) | copy-start | bytes 12292
Sparse Core Ops, SparseCore 0:
  10.1 39.7 all-gather.4
  52.6 54.6 all-gather.8
  109.4 55.7 all-gather.6

commit v5 on v4

--- a/solution.py
+++ b/solution.py
@@ -147,6 +147,92 @@
         out_specs=pl.BlockSpec(memory_space=pltpu.VMEM),
         scratch_shapes=scratch,
         compiler_params=pltpu.CompilerParams(collective_id=1, has_side_effects=True),
+    )(parts)
+
+
+def seq_peers():
+    me, n = lax.axis_index("seq"), lax.axis_size("seq")
+    row, col = lax.axis_index("row"), lax.axis_index("col")
+    peers = [lax.rem(me + j, n) for j in range(1, n)]
+    barrier = pltpu.get_barrier_semaphore()
+    for peer in peers:
+        pl.semaphore_signal(barrier, inc=1, device_id=(peer, row, col), device_id_type=MESH)
+    pl.semaphore_wait(barrier, len(peers))
+    return me, [(peer, row, col) for peer in peers]
+
+
+def seq_direct_gather_kernel(x_ref, out_ref, self_sem, send_sem, recv_sem):
+    me, peers = seq_peers()
+    own = pltpu.make_async_copy(x_ref, out_ref.at[me], self_sem)
+    own.start()
+    copies = []
+    for j, peer in enumerate(peers):
+        copy = pltpu.make_async_remote_copy(
+            src_ref=x_ref,
+            dst_ref=out_ref.at[me],
+            send_sem=send_sem.at[j],
+            recv_sem=recv_sem.at[j],
+            device_id=peer,
+            device_id_type=MESH,
+        )
+        copy.start()
+        copies.append(copy)
+    own.wait()
+    for copy in copies:
+        copy.wait()
+
+
+def seq_direct_gather(block):
+    n = lax.axis_size("seq")
+    return pl.pallas_call(
+        seq_direct_gather_kernel,
+        out_shape=jax.ShapeDtypeStruct((n,) + block.shape, block.dtype),
+        in_specs=[pl.BlockSpec(memory_space=pltpu.VMEM)],
+        out_specs=pl.BlockSpec(memory_space=pltpu.VMEM),
+        scratch_shapes=[
+            pltpu.SemaphoreType.DMA(()),
+            pltpu.SemaphoreType.DMA((n - 1,)),
+            pltpu.SemaphoreType.DMA((n - 1,)),
+        ],
+        compiler_params=pltpu.CompilerParams(collective_id=4, has_side_effects=True),
+    )(block)
+
+
+def seq_merge_kernel(top_lane, x_ref, out_ref, got, send_sem, recv_sem):
+    me, peers = seq_peers()
+    copies = []
+    for j, peer in enumerate(peers):
+        copy = pltpu.make_async_remote_copy(
+            src_ref=x_ref.at[peer[0]],
+            dst_ref=got.at[j],
+            send_sem=send_sem.at[j],
+            recv_sem=recv_sem.at[j],
+            device_id=peer,
+            device_id_type=MESH,
+        )
+        copy.start()
+        copies.append(copy)
+    for copy in copies:
+        copy.wait()
+    value = x_ref[me]
+    for j in range(len(copies)):
+        value = merge_parts(value, got[j], top_lane)
+    out_ref[...] = value
+
+
+def seq_direct_merge(parts, top_lane):
+    n = parts.shape[0]
+    return pl.pallas_call(
+        functools.partial(seq_merge_kernel, top_lane),
+        out_shape=jax.ShapeDtypeStruct(parts.shape[1:], parts.dtype),
+        in_specs=[pl.BlockSpec(memory_space=pltpu.VMEM)],
+        out_specs=pl.BlockSpec(memory_space=pltpu.VMEM),
+        scratch_shapes=[
+            pltpu.VMEM((n - 1,) + parts.shape[1:], parts.dtype),
+            pltpu.SemaphoreType.DMA((n - 1,)),
+            pltpu.SemaphoreType.DMA((n - 1,)),
+        ],
+        compiler_params=pltpu.CompilerParams(collective_id=5, has_side_effects=True),
     )(parts)
 
 
@@ -286,7 +372,7 @@
     own_match = (own_pos - base)[:, None] == local_order[None, :]
     picker = own_match.astype(jnp.bfloat16)
     own_rows = jnp.dot(picker, tokens, preferred_element_type=jnp.float32).astype(jnp.bfloat16)
-    glob_rows = seq_gather(own_rows.reshape(-1, 128)).reshape(n_glob, width)
+    glob_rows = seq_direct_gather(own_rows.reshape(-1, 128)).reshape(n_glob, width)
 
     w_global = lax.all_gather(
         qkv_global_weight.reshape(qkv_global_weight.shape[0], -1), "row", axis=0, tiled=True
@@ -390,8 +476,10 @@
         axis=2,
     )
     packed = jnp.transpose(packed, (1, 0, 2)).reshape(n_glob * heads_here, 128)
-    packed, everything = lax.optimization_barrier((packed, everything))
-    merged = seq_softmax_combine(packed, head_dim + 1).reshape(per_shard, heads_here, 128)
+    packed, w_out = lax.optimization_barrier((packed, w_out))
+    merged = seq_direct_merge(packed.reshape(n_seq, -1, 128), head_dim + 1).reshape(
+        per_shard, heads_here, 128
+    )
     own_out = jnp.transpose(
         (merged[:, :, :head_dim] / merged[:, :, head_dim : head_dim + 1]).astype(jnp.bfloat16),
         (1, 0, 2),
@@ -430,10 +518,14 @@
         shard_len, heads_here * head_dim
     )
 
-    attention, w_out = lax.optimization_barrier((attention, w_out))
+    attention, everything = lax.optimization_barrier((attention, everything))
     attn_all = col_gather(attention)
-    attn_full = jnp.transpose(attn_all, (1, 0, 2)).reshape(shard_len, n_col * heads_here * head_dim)
-    proj = jnp.dot(attn_full, w_out, preferred_element_type=jnp.float32)
+    proj = jnp.einsum(
+        "ctk,ckn->tn",
+        attn_all,
+        w_out.reshape(n_col, heads_here * head_dim, width),
+        preferred_element_type=jnp.float32,
+    )
     middle = layer_norm(tokens.astype(jnp.float32) + proj, ln_gain, ln_bias).astype(jnp.bfloat16)
     ffn_pre = jnp.dot(middle, f_in, preferred_element_type=jnp.float32)
     ffn_hidden = jax.nn.gelu(ffn_pre, approximate=False).astype(jnp.bfloat16)

time: 277 us -> 283 us (1.022)
  the two profiles are of different devices: /device:TPU:32 before, /device:TPU:1 now
where the time goes in v5:
time: 283 us; the launch traced here: 281 us
  Pallas kernels  109 us (39%)
  local copies, waits for them, and re-layouts  44.3 us (16%)
  matrix products  39.4 us (14%)
  waiting for transfers between devices  39.2 us (14%)
  other arithmetic  18.4 us (7%)
  starting transfers between devices  17 us (6%)
  between operations  14.2 us (5%)
    pallas_call x1, Pallas kernels, col_reduce_scatter(): pl.pallas_call(col_sum_kernel, out_shape=jax.ShapeDtypeStruct(own.shape,...  35.9 us
    all_gather x1, waiting for transfers between devices, per_device(): lax.all_gather(jnp.concatenate([fi_flat, ffn_out.reshape(-1)]), 'row', ax...  33.8 us
    pallas_call x1, Pallas kernels, col_gather(): pl.pallas_call(col_gather_kernel, out_shape=jax.ShapeDtypeStruct((m,) + b...  27.4 us
    pallas_call x1, Pallas kernels, seq_direct_gather(): pl.pallas_call(seq_direct_gather_kernel, out_shape=jax.ShapeDtypeStruct((...  26.1 us
    pallas_call x1, Pallas kernels, seq_direct_merge(): pl.pallas_call(functools.partial(seq_merge_kernel, top_lane), out_shape=j...  19.6 us
    all_to_all x1, starting transfers between devices, per_device(): lax.all_to_all(outgoing, 'seq', split_axis=0, concat_axis=0, tiled=True)  11.2 us
    dot_general x1, matrix products, per_device(): ffn_full = jnp.dot(ffn_hidden, f_out, preferred_element_type=jnp.float32)  10.1 us
    unnamed x38, local copies, waits for them, and re-layouts  9.67 us
  transfers between devices with their start and end apart: 6, of which 2 were waited for; matrix products, arithmetic and copies ran while one was open for 19% of the time, Pallas kernels for 16%

profile of v5, /device:TPU:1, one launch (start us, length us, event | category | flops | bytes accessed | tf_op | source)
XLA Modules:
  0.0 281.4 jit_solution(2471094581879583623)
XLA Ops:
  8.6 3.1 %convolution_convert_fusion.2 = bf16[512,768]{1,0:T(8,128)(2,1)} fusion(bf16[1024,768]{0,1:T(8,128)(2,1)S(1)} %bitcast.88, bf16[1,512,1024]{2,1,0:T(8,128)(2,1)} %param.13), kind=kOutput, calls=%fused_computation.35 | convolution fusion | flops 805699584 | bytes 3407872 | tf_op jit(solution)/shard_map/dot_general | solution.py:393
  17.3 2.6 reshape.193
  19.9 11.2 %all-to-all-start = ((bf16[32,2,16,4,128]{4,3,2,1,0:T(4,128)(2,1)}), bf16[32,2,16,4,128]{4,3,2,1,0:T(4,128)(2,1)}, u32[]{:S(2)}, u32[]{:S(2)}) async-start(bf16[32,2,16,4,128]{4,3,2,1,0:T(4,128)(2,1)} %reshape.193), calls=%async_computation | async-start | bytes 2097152 | tf_op jit(solution)/shard_map/all_to_all | solution.py:419
  32.0 3.5 %collective-permute-start = (bf16[256,4,128]{0,2,1:T(8,128)(2,1)}, bf16[256,4,128]{0,2,1:T(8,128)(2,1)}, u32[]{:S(2)}, u32[]{:S(2)}) collective-permute-start(bf16[256,4,128]{0,2,1:T(8,128)(2,1)} %get-tuple-element.14), channel_id=1, source_target_pairs={{0,16},{16,32},{32,48},{48,64},{64,80},{80,96},{96,112},{112,128},... | collective-permute-start | bytes 786440 | tf_op jit(solution)/shard_map/ppermute | solution.py:21
  44.3 26.1 %shard_map.140 = bf16[32,32,128]{2,1,0:T(8,128)(2,1)} custom-call(bf16[32,128]{1,0:T(8,128)(2,1)} %reshape.194.x_ref), custom_call_target="tpu_custom_call" | custom-call | tf_op jit(solution)/shard_map/pallas_call | solution.py:187
  75.0 4.8 %select_reduce_fusion = (f32[4,512]{1,0:T(4,128)S(1)}, f32[4,512,1024]{2,1,0:T(8,128)}) fusion(pred[512,1024]{1,0:T(8,128)(4,1)S(1)} %fusion.15, bf16[1024,4,128]{0,2,1:T(8,128)(2,1)S(1)} %pad_maximum_fusion, bf16[512,4,192]{0,2,1:T(8,128)(2,1)S(1)} %bitcast.96), kind=kOutput, calls=%fused_computation.3 | convolution fusion | flops 274724864 | bytes 9707520 | tf_op jit(solution)/shard_map/qhd,khd->hqk/dot_general | solution.py:491
  82.8 5.0 %fusion = f32[4,512]{1,0:T(4,128)S(1)} fusion(f32[4,512,1024]{2,1,0:T(8,128)} %get-tuple-element.17, f32[4,512]{1,0:T(4,128)S(1)} %max.7, pred[512,1024]{1,0:T(8,128)(4,1)S(1)} %copy-done.6), kind=kLoop, calls=%fused_computation.4 | loop fusion | flops 8386560 | bytes 8929280 | tf_op jit(solution)/shard_map/reduce_sum | solution.py:504
  89.1 2.9 %fusion.62 = bf16[512,4,64]{0,2,1:T(8,128)(2,1)} fusion(f32[4,64,512]{2,1,0:T(8,128)S(1)} %fusion.69, f32[4,512,1024]{2,1,0:T(8,128)S(1)} %copy-done.1, f32[4,512]{1,0:T(4,128)S(1)} %max.7, pred[512,1024]{1,0:T(8,128)(4,1)S(1)} %copy-done.6, bf16[1024,4,128]{0,2,1:T(8,128)(2,1)S(1)} %copy-done.9, f32[512,4]{0,1:T(4,128)S(1)} %add_bitcast_fusion), kind=kOutput, calls=%fused_computation.86 | convolution fusion | flops 277217280 | bytes 10240000 | tf_op jit(solution)/shard_map/hqk,khd->qhd/dot_general | solution.py:505
  92.0 2.1 convolution_convert_fusion.5
  95.0 3.3 %convolution_convert_fusion.1 = bf16[512,768]{1,0:T(8,128)(2,1)} fusion(bf16[1024,768]{0,1:T(8,128)(2,1)} %all-gather.5.cloned.1.call-done, bf16[1,512,1024]{2,1,0:T(8,128)(2,1)S(1)} %copy-done.7), kind=kOutput, calls=%fused_computation.34 | convolution fusion | flops 805699584 | bytes 3407872 | tf_op jit(solution)/shard_map/dot_general | solution.py:437
  103.2 4.7 %all-gather.7.cloned.1.call-done = bf16[1024,1024]{1,0:T(8,128)(2,1)} async-done(((bf16[256,1024]{1,0:T(8,128)(2,1)}), bf16[1024,1024]{1,0:T(8,128)(2,1)}) %all-gather.7.cloned.1.call-update) | async-done | bytes 2097168 | tf_op jit(solution)/shard_map/all_gather | solution.py:390
  107.9 19.6 %shard_map.141 = f32[16,128]{1,0:T(8,128)} custom-call(f32[32,16,128]{2,1,0:T(8,128)} %bitcast.102), custom_call_target="tpu_custom_call" | custom-call | tf_op jit(solution)/shard_map/pallas_call | solution.py:225
  129.7 33.8 %all-gather.9.cloned.1.call-done = bf16[2097152]{0:T(1024)(128)(2,1)} async-done(((bf16[524288]{0:T(1024)(128)(2,1)}), bf16[2097152]{0:T(1024)(128)(2,1)}) %all-gather.9.cloned.1.call-update) | async-done | bytes 4194320 | tf_op jit(solution)/shard_map/all_gather | solution.py:383
  163.5 5.7 %reshape.219 = bf16[4,524288]{1,0:T(4,128)(2,1)} reshape(bf16[2097152]{0:T(1024)(128)(2,1)} %all-gather.9.cloned.1.call-done) | data formatting | bytes 8388608 | tf_op jit(solution)/shard_map/all_gather | solution.py:383
  169.2 4.3 %fusion.136 = (bf16[4,262144]{1,0:T(4,128)(2,1)}, bf16[4,262144]{1,0:T(4,128)(2,1)}) fusion(bf16[4,524288]{1,0:T(4,128)(2,1)} %reshape.219), kind=kLoop, calls=%fused_computation.184 | loop fusion | bytes 8388608 | tf_op jit(solution)/shard_map/slice | solution.py:386
  174.3 27.4 %shard_map.142 = bf16[4,512,256]{2,1,0:T(8,128)(2,1)} custom-call(bf16[512,256]{1,0:T(8,128)(2,1)} %copy.74.x_ref), custom_call_target="tpu_custom_call" | custom-call | tf_op jit(solution)/shard_map/pallas_call | solution.py:273
  201.7 3.3 %fusion.138 = (f32[512]{0:T(512)S(1)}, f32[512,1024]{1,0:T(8,128)S(1)}) fusion(bf16[4,512,256]{2,1,0:T(8,128)(2,1)} %shard_map.142, bf16[4,256,1024]{2,1,0:T(8,128)(2,1)} %bitcast.120, bf16[1,512,1024]{2,1,0:T(8,128)(2,1)S(1)} %copy-done.7), kind=kOutput, calls=%fused_computation.186 | convolution fusion | flops 1075314176 | bytes 6293504 | tf_op jit(solution)/shard_map/ctk,ckn->tn/dot_general | solution.py:523
  209.0 4.0 %copy.75 = bf16[1024,4,256]{0,2,1:T(8,128)(2,1)} copy(bf16[1024,4,256]{2,0,1:T(8,128)(2,1)} %bitcast.90) | data formatting | bytes 4194304 | tf_op jit(solution)/shard_map/transpose | solution.py:387
  212.9 4.8 %reshape.207 = bf16[1024,1024]{1,0:T(8,128)(2,1)} reshape(bf16[4,262144]{1,0:T(4,128)(2,1)} %get-tuple-element.12) | data formatting | bytes 4194304 | tf_op jit(solution)/shard_map/reshape | solution.py:386
  217.8 2.0 add_convert_fusion
  219.8 10.1 %fusion.139 = (bf16[512,1024]{1,0:T(8,128)(2,1)}, f32[512,1024]{1,0:T(8,128)}) fusion(bf16[1024,1024]{0,1:T(8,128)(2,1)} %bitcast.98, bf16[512,1024]{1,0:T(8,128)(2,1)S(1)} %add_convert_fusion, bf16[1024,1024]{1,0:T(8,128)(2,1)} %reshape.207), kind=kOutput, calls=%fused_computation.187 | convolution fusion | flops 2182086656 | bytes 8388608 | tf_op jit(solution)/shard_map/dot_general | solution.py:533
  229.9 1.9 dynamic-slice_add_fusion.own_ref
  231.8 35.9 %shard_map.143 = f32[128,1024]{1,0:T(8,128)} custom-call(bf16[4,128,1024]{2,1,0:T(8,128)(2,1)} %bitcast.101, f32[128,1024]{1,0:T(8,128)} %dynamic-slice_add_fusion.own_ref), custom_call_target="tpu_custom_call" | custom-call | tf_op jit(solution)/shard_map/pallas_call | solution.py:318
  272.1 2.8 %copy.92 = bf16[1,1,32,2,16,4,128]{6,5,4,3,2,1,0:T(4,128)(2,1)} copy(bf16[1,1,32,2,16,4,128]{6,5,4,3,2,1,0:T(4,128)(2,1)} %bitcast.9) | data formatting | bytes 2097152
  (103 shorter events, 42.3 us)
Async XLA Ops:
  7.2 1.4 copy-start
  7.2 84.8 %all-gather.5.cloned.1.call-start = ((), (), s32[]{:S(2)}) async-start(), calls=%async_computation.1 | async-start | bytes 1966080 | tf_op jit(solution)/shard_map/all_gather | solution.py:377
  11.7 4.0 %copy-start.16 = (s32[1,32,1]{1,2,0:T(1,128)S(1)}, s32[1,32,1]{1,2,0:T(1,128)}, u32[]{:S(2)}) copy-start(s32[1,32,1]{1,2,0:T(1,128)} %param.25) | copy-start | bytes 388
  19.9 17.9 %copy-start.10 = (bf16[256,1024]{1,0:T(8,128)(2,1)S(1)}, bf16[256,1024]{1,0:T(8,128)(2,1)}, u32[]{:S(2)}) copy-start(bf16[256,1024]{1,0:T(8,128)(2,1)} %param.19) | copy-start | bytes 1572868
  19.9 59.9 %all-to-all-start = ((bf16[32,2,16,4,128]{4,3,2,1,0:T(4,128)(2,1)}), bf16[32,2,16,4,128]{4,3,2,1,0:T(4,128)(2,1)}, u32[]{:S(2)}, u32[]{:S(2)}) async-start(bf16[32,2,16,4,128]{4,3,2,1,0:T(4,128)(2,1)} %reshape.193), calls=%async_computation | async-start | bytes 2097152 | tf_op jit(solution)/shard_map/all_to_all | solution.py:419
  31.1 76.8 %all-gather.7.cloned.1.call-start = ((), (), s32[]{:S(2)}) async-start(), calls=%async_computation.2 | async-start | bytes 2621440 | tf_op jit(solution)/shard_map/all_gather | solution.py:390
  32.0 40.6 %collective-permute-start = (bf16[256,4,128]{0,2,1:T(8,128)(2,1)}, bf16[256,4,128]{0,2,1:T(8,128)(2,1)}, u32[]{:S(2)}, u32[]{:S(2)}) collective-permute-start(bf16[256,4,128]{0,2,1:T(8,128)(2,1)} %get-tuple-element.14), channel_id=1, source_target_pairs={{0,16},{16,32},{32,48},{48,64},{64,80},{80,96},{96,112},{112,128},... | collective-permute-start | bytes 786440 | tf_op jit(solution)/shard_map/ppermute | solution.py:21
  35.5 37.1 %collective-permute-start.1 = (bf16[256,4,128]{0,2,1:T(8,128)(2,1)}, bf16[256,4,128]{0,2,1:T(8,128)(2,1)}, u32[]{:S(2)}, u32[]{:S(2)}) collective-permute-start(bf16[256,4,128]{0,2,1:T(8,128)(2,1)} %get-tuple-element.15), channel_id=1, source_target_pairs={{16,0},{32,16},{48,32},{64,48},{80,64},{96,80},{112,96},{128,112},... | collective-permute-start | bytes 786440 | tf_op jit(solution)/shard_map/ppermute | solution.py:24
  37.5 126.0 %all-gather.9.cloned.1.call-start = ((), (), s32[]{:S(2)}) async-start(), calls=%async_computation.3 | async-start | bytes 5242880 | tf_op jit(solution)/shard_map/all_gather | solution.py:383
  37.8 2.6 copy-start.15
  39.3 2.7 copy-start.4
  72.6 1.4 copy-start.5
  74.0 1.0 copy-start.8
  79.8 2.9 %copy-start.6 = (pred[512,1024]{1,0:T(8,128)(4,1)S(1)}, pred[512,1024]{1,0:T(8,128)(4,1)}, u32[]{:S(2)}) copy-start(pred[512,1024]{1,0:T(8,128)(4,1)} %copy-done.5) | copy-start | bytes 1572868
  82.7 6.4 %copy-start.1 = (f32[4,512,1024]{2,1,0:T(8,128)S(1)}, f32[4,512,1024]{2,1,0:T(8,128)}, u32[]{:S(2)}) copy-start(f32[4,512,1024]{2,1,0:T(8,128)} %get-tuple-element.17) | copy-start | bytes 25165828
  82.8 6.4 %copy-start.9 = (bf16[1024,4,128]{0,2,1:T(8,128)(2,1)S(1)}, bf16[1024,4,128]{0,2,1:T(8,128)(2,1)}, u32[]{:S(2)}) copy-start(bf16[1024,4,128]{0,2,1:T(8,128)(2,1)} %copy-done.8) | copy-start | bytes 3145732
  92.0 3.0 %copy-start.7 = (bf16[1,512,1024]{2,1,0:T(8,128)(2,1)S(1)}, bf16[1,512,1024]{2,1,0:T(8,128)(2,1)}, u32[]{:S(2)}) copy-start(bf16[1,512,1024]{2,1,0:T(8,128)(2,1)} %param.13) | copy-start | bytes 3145732
  205.0 1.4 copy-start.2
  205.0 2.3 copy-start.3
  212.9 4.8 %copy-start.11 = (f32[1024]{0:T(1024)S(1)}, f32[1024]{0:T(1024)}, u32[]{:S(2)}) copy-start(f32[1024]{0:T(1024)} %param.18) | copy-start | bytes 12292
  212.9 4.8 %copy-start.12 = (f32[1024]{0:T(1024)S(1)}, f32[1024]{0:T(1024)}, u32[]{:S(2)}) copy-start(f32[1024]{0:T(1024)} %param.17) | copy-start | bytes 12292
  229.9 40.2 %copy-start.13 = (f32[1024]{0:T(1024)S(1)}, f32[1024]{0:T(1024)}, u32[]{:S(2)}) copy-start(f32[1024]{0:T(1024)} %param.22) | copy-start | bytes 12292
  229.9 40.2 %copy-start.14 = (f32[1024]{0:T(1024)S(1)}, f32[1024]{0:T(1024)}, u32[]{:S(2)}) copy-start(f32[1024]{0:T(1024)} %param.21) | copy-start | bytes 12292
Sparse Core Ops, SparseCore 0:
  10.1 40.0 all-gather.4
  52.3 55.5 all-gather.6
  110.6 52.8 all-gather.8

commit v6 on v5

--- a/solution.py
+++ b/solution.py
@@ -313,7 +313,7 @@
     lax.fori_loop(0, out_ref.shape[0] // chunk, body, 0)
 
 
-def col_reduce_scatter(parts, own):
+def col_reduce_scatter(parts, own, collective_id):
     m = lax.axis_size("col")
     return pl.pallas_call(
         col_sum_kernel,
@@ -325,7 +325,7 @@
             pltpu.SemaphoreType.DMA((m - 1,)),
             pltpu.SemaphoreType.DMA((m - 1,)),
         ],
-        compiler_params=pltpu.CompilerParams(collective_id=3, has_side_effects=True),
+        compiler_params=pltpu.CompilerParams(collective_id=collective_id, has_side_effects=True),
     )(parts, own)
 
 
@@ -377,17 +377,8 @@
     w_global = lax.all_gather(
         qkv_global_weight.reshape(qkv_global_weight.shape[0], -1), "row", axis=0, tiled=True
     )
-    fi_rows, units = ffn_in.shape
-    fi_flat = ffn_in.reshape(-1)
-    n_fi = fi_flat.shape[0]
-    everything = lax.all_gather(
-        jnp.concatenate([fi_flat, ffn_out.reshape(-1)]), "row", axis=0
-    )
-    f_in = everything[:, :n_fi].reshape(n_row * fi_rows, units)
-    f_out = jnp.transpose(
-        everything[:, n_fi:].reshape(n_row, units, ffn_out.shape[1]), (1, 0, 2)
-    ).reshape(units, n_row * ffn_out.shape[1])
-    w_out = lax.all_gather(out_weight, "col", axis=0, tiled=True)
+    f_in = lax.all_gather(ffn_in, "row", axis=0, tiled=True)
+    f_out = lax.all_gather(ffn_out, "row", axis=1, tiled=True)
 
     flat_weight = qkv_weight.reshape(width, heads_here * triple)
     qkv = jnp.dot(tokens, flat_weight, preferred_element_type=jnp.float32).astype(jnp.bfloat16)
@@ -476,7 +467,7 @@
         axis=2,
     )
     packed = jnp.transpose(packed, (1, 0, 2)).reshape(n_glob * heads_here, 128)
-    packed, w_out = lax.optimization_barrier((packed, w_out))
+    packed, f_in = lax.optimization_barrier((packed, f_in))
     merged = seq_direct_merge(packed.reshape(n_seq, -1, 128), head_dim + 1).reshape(
         per_shard, heads_here, 128
     )
@@ -518,23 +509,27 @@
         shard_len, heads_here * head_dim
     )
 
-    attention, everything = lax.optimization_barrier((attention, everything))
-    attn_all = col_gather(attention)
-    proj = jnp.einsum(
-        "ctk,ckn->tn",
-        attn_all,
-        w_out.reshape(n_col, heads_here * head_dim, width),
-        preferred_element_type=jnp.float32,
-    )
-    middle = layer_norm(tokens.astype(jnp.float32) + proj, ln_gain, ln_bias).astype(jnp.bfloat16)
+    attention, f_out = lax.optimization_barrier((attention, f_out))
+
+    out_rows = shard_len // n_col
+    proj = jnp.dot(attention, out_weight, preferred_element_type=jnp.float32)
+    proj_own = lax.dynamic_slice_in_dim(proj, col_index * out_rows, out_rows, 0)
+    token_own = lax.dynamic_slice_in_dim(tokens, col_index * out_rows, out_rows, 0)
+    summed = col_reduce_scatter(
+        proj.astype(jnp.bfloat16).reshape(n_col, out_rows, width),
+        token_own.astype(jnp.float32) + proj_own,
+        3,
+    )
+    mine = layer_norm(summed, ln_gain, ln_bias).astype(jnp.bfloat16)
+    middle = col_gather(mine).reshape(shard_len, width)
     ffn_pre = jnp.dot(middle, f_in, preferred_element_type=jnp.float32)
     ffn_hidden = jax.nn.gelu(ffn_pre, approximate=False).astype(jnp.bfloat16)
-    out_rows = shard_len // n_col
     ffn_full = jnp.dot(ffn_hidden, f_out, preferred_element_type=jnp.float32)
     ffn_own = lax.dynamic_slice_in_dim(ffn_full, col_index * out_rows, out_rows, 0)
-    mine = lax.dynamic_slice_in_dim(middle, col_index * out_rows, out_rows, 0).astype(jnp.float32)
     second = col_reduce_scatter(
-        ffn_full.astype(jnp.bfloat16).reshape(n_col, out_rows, width), mine + ffn_own
+        ffn_full.astype(jnp.bfloat16).reshape(n_col, out_rows, width),
+        mine.astype(jnp.float32) + ffn_own,
+        6,
     )
     normed = layer_norm(second, ln2_gain, ln2_bias)
     return (normed.astype(jnp.bfloat16)[None], page_pool)

time: 283 us -> 259 us (0.915)
  Pallas kernels: 109 us -> 138 us
  local copies, waits for them, and re-layouts: 44.3 us -> 17 us
  waiting for transfers between devices: 39.2 us -> 13.7 us
  matrix products: 39.4 us -> 36.1 us
  other arithmetic: 18.4 us -> 21.3 us
    all_gather x2, waiting for transfers between devices: 38.5 us -> 12.3 us  [the longest x1 12.3 us: per_device(): f_out = lax.all_gather(ffn_out, 'row', axis=1, tiled=True)]
    pallas_call x1 -> x2, Pallas kernels: 35.9 us -> 55 us  [col_reduce_scatter(): pl.pallas_call(col_sum_kernel, out_shape=jax.ShapeDtypeStruct(own.shape,...]
    pallas_call x1, Pallas kernels: 27.4 us -> 36.9 us  [col_gather(): pl.pallas_call(col_gather_kernel, out_shape=jax.ShapeDtypeStruct((m,) + b...]
    unnamed x38 -> x33, local copies, waits for them, and re-layouts: 9.67 us -> 3.88 us
    all_gather x1 -> x0, local copies, waits for them, and re-layouts: 5.66 us -> none  [per_device(): lax.all_gather(jnp.concatenate([fi_flat, ffn_out.reshape(-1)]), 'row', ax...]
    reshape x1 -> x0, local copies, waits for them, and re-layouts: 4.83 us -> none  [per_device(): f_in = everything[:, :n_fi].reshape(n_row * fi_rows, units)]
    slice x1 -> x0, local copies, waits for them, and re-layouts: 4.33 us -> none  [per_device(): f_in = everything[:, :n_fi].reshape(n_row * fi_rows, units)]
    transpose x1 -> x0, local copies, waits for them, and re-layouts: 3.97 us -> none  [per_device(): jnp.transpose(everything[:, n_fi:].reshape(n_row, units, ffn_out.shape[1]...]
  transfers between devices with their start and end apart: 6 -> 6, of which waited for: 2 -> 1; matrix products, arithmetic and copies ran while one was open for 19% -> 18% of each run, Pallas kernels for 16% -> 18%
where the time goes in v6:
time: 259 us; the launch traced here: 257 us
  Pallas kernels  138 us (53%)
  matrix products  36.1 us (14%)
  other arithmetic  21.3 us (8%)
  local copies, waits for them, and re-layouts  17 us (7%)
  starting transfers between devices  16.9 us (7%)
  between operations  14.2 us (5%)
  waiting for transfers between devices  13.7 us (5%)
    pallas_call x2, Pallas kernels, col_reduce_scatter(): pl.pallas_call(col_sum_kernel, out_shape=jax.ShapeDtypeStruct(own.shape,...  55 us
    pallas_call x1, Pallas kernels, col_gather(): pl.pallas_call(col_gather_kernel, out_shape=jax.ShapeDtypeStruct((m,) + b...  36.9 us
    pallas_call x1, Pallas kernels, seq_direct_gather(): pl.pallas_call(seq_direct_gather_kernel, out_shape=jax.ShapeDtypeStruct((...  28.9 us
    pallas_call x1, Pallas kernels, seq_direct_merge(): pl.pallas_call(functools.partial(seq_merge_kernel, top_lane), out_shape=j...  17.4 us
    all_gather x1, waiting for transfers between devices, per_device(): f_out = lax.all_gather(ffn_out, 'row', axis=1, tiled=True)  12.3 us
    all_to_all x1, starting transfers between devices, per_device(): lax.all_to_all(outgoing, 'seq', split_axis=0, concat_axis=0, tiled=True)  11.2 us
    dot_general x1, matrix products, per_device(): ffn_full = jnp.dot(ffn_hidden, f_out, preferred_element_type=jnp.float32)  10.5 us
    reduce_sum x2, other arithmetic, per_device(): total = jnp.sum(e_win, axis=2) + jnp.sum(e_glob, axis=2)  5.21 us
  transfers between devices with their start and end apart: 6, of which 1 were waited for; matrix products, arithmetic and copies ran while one was open for 18% of the time, Pallas kernels for 18%

profile of v6, /device:TPU:1, one launch (start us, length us, event | category | flops | bytes accessed | tf_op | source)
XLA Modules:
  0.0 257.5 jit_solution(165654385198974638)
XLA Ops:
  8.7 2.2 convolution_convert_fusion.2
  15.3 2.6 reshape.184
  17.9 11.2 %all-to-all-start = ((bf16[32,2,16,4,128]{4,3,2,1,0:T(4,128)(2,1)}), bf16[32,2,16,4,128]{4,3,2,1,0:T(4,128)(2,1)}, u32[]{:S(2)}, u32[]{:S(2)}) async-start(bf16[32,2,16,4,128]{4,3,2,1,0:T(4,128)(2,1)} %reshape.184), calls=%async_computation | async-start | bytes 2097152 | tf_op jit(solution)/shard_map/all_to_all | solution.py:410
  30.0 2.3 collective-permute-start.1
  32.4 3.2 %collective-permute-start = (bf16[256,4,128]{0,2,1:T(8,128)(2,1)}, bf16[256,4,128]{0,2,1:T(8,128)(2,1)}, u32[]{:S(2)}, u32[]{:S(2)}) collective-permute-start(bf16[256,4,128]{0,2,1:T(8,128)(2,1)} %get-tuple-element.14), channel_id=1, source_target_pairs={{0,16},{16,32},{32,48},{48,64},{64,80},{80,96},{96,112},{112,128},... | collective-permute-start | bytes 786440 | tf_op jit(solution)/shard_map/ppermute | solution.py:21
  35.8 1.5 convolution_convert_fusion.6
  39.5 28.9 %shard_map.140 = bf16[32,32,128]{2,1,0:T(8,128)(2,1)} custom-call(bf16[32,128]{1,0:T(8,128)(2,1)} %reshape.185.x_ref), custom_call_target="tpu_custom_call" | custom-call | tf_op jit(solution)/shard_map/pallas_call | solution.py:187
  73.0 4.8 %select_reduce_fusion = (f32[4,512]{1,0:T(4,128)S(1)}, f32[4,512,1024]{2,1,0:T(8,128)}) fusion(pred[512,1024]{1,0:T(8,128)(4,1)S(1)} %fusion.15, bf16[1024,4,128]{0,2,1:T(8,128)(2,1)S(1)} %pad_maximum_fusion, bf16[512,4,192]{0,2,1:T(8,128)(2,1)S(1)} %bitcast.83), kind=kOutput, calls=%fused_computation.3 | convolution fusion | flops 274724864 | bytes 9707520 | tf_op jit(solution)/shard_map/qhd,khd->hqk/dot_general | solution.py:482
  80.6 5.0 %fusion = f32[4,512]{1,0:T(4,128)S(1)} fusion(f32[4,512,1024]{2,1,0:T(8,128)} %get-tuple-element.17, f32[4,512]{1,0:T(4,128)S(1)} %max.7, pred[512,1024]{1,0:T(8,128)(4,1)S(1)} %copy-done.5), kind=kLoop, calls=%fused_computation.4 | loop fusion | flops 8386560 | bytes 8929280 | tf_op jit(solution)/shard_map/reduce_sum | solution.py:495
  87.1 2.9 %fusion.62 = bf16[512,4,64]{0,2,1:T(8,128)(2,1)} fusion(f32[4,64,512]{2,1,0:T(8,128)S(1)} %fusion.69, f32[4,512,1024]{2,1,0:T(8,128)S(1)} %copy-done.2, f32[4,512]{1,0:T(4,128)S(1)} %max.7, pred[512,1024]{1,0:T(8,128)(4,1)S(1)} %copy-done.5, bf16[1024,4,128]{0,2,1:T(8,128)(2,1)S(1)} %copy-done.7, f32[512,4]{0,1:T(4,128)S(1)} %add_bitcast_fusion), kind=kOutput, calls=%fused_computation.81 | convolution fusion | flops 277217280 | bytes 10240000 | tf_op jit(solution)/shard_map/hqk,khd->qhd/dot_general | solution.py:496
  90.0 3.6 %convolution_convert_fusion.1 = bf16[512,768]{1,0:T(8,128)(2,1)} fusion(bf16[1024,768]{0,1:T(8,128)(2,1)} %all-gather.4.cloned.1.call-done, bf16[1,512,1024]{2,1,0:T(8,128)(2,1)} %param.13), kind=kOutput, calls=%fused_computation.30 | convolution fusion | flops 805699584 | bytes 3407872 | tf_op jit(solution)/shard_map/dot_general | solution.py:428
  95.0 2.1 convolution_convert_fusion.5
  100.0 17.4 %shard_map.141 = f32[16,128]{1,0:T(8,128)} custom-call(f32[32,16,128]{2,1,0:T(8,128)} %bitcast.88), custom_call_target="tpu_custom_call" | custom-call | tf_op jit(solution)/shard_map/pallas_call | solution.py:225
  119.3 12.3 %all-gather.8.cloned.1.call-done = bf16[1024,1024]{1,0:T(8,128)(2,1)} async-done(((bf16[1024,256]{1,0:T(8,128)(2,1)}), bf16[1024,1024]{1,0:T(8,128)(2,1)}) %all-gather.8.cloned.1.call-update) | async-done | bytes 2097168 | tf_op jit(solution)/shard_map/all_gather | solution.py:381
  131.6 1.4 fusion.137
  133.1 1.9 convert_add_fusion.own_ref
  134.9 26.5 %shard_map.142 = f32[128,1024]{1,0:T(8,128)} custom-call(bf16[4,128,1024]{2,1,0:T(8,128)(2,1)} %bitcast.85, f32[128,1024]{1,0:T(8,128)} %convert_add_fusion.own_ref), custom_call_target="tpu_custom_call" | custom-call | tf_op jit(solution)/shard_map/pallas_call | solution.py:318
  163.8 1.9 add_convert_fusion.1.x_ref
  165.7 36.9 %shard_map.143 = bf16[4,128,1024]{2,1,0:T(8,128)(2,1)} custom-call(bf16[128,1024]{1,0:T(8,128)(2,1)} %add_convert_fusion.1.x_ref), custom_call_target="tpu_custom_call" | custom-call | tf_op jit(solution)/shard_map/pallas_call | solution.py:273
  202.7 10.5 %fusion.138 = (bf16[512,1024]{1,0:T(8,128)(2,1)}, f32[512,1024]{1,0:T(8,128)}) fusion(bf16[1024,1024]{1,0:T(8,128)(2,1)} %all-gather.8.cloned.1.call-done, bf16[512,1024]{1,0:T(8,128)(2,1)} %bitcast.86, bf16[1024,1024]{1,0:T(8,128)(2,1)} %all-gather.6.cloned.1.call-done), kind=kOutput, calls=%fused_computation.184 | convolution fusion | flops 2182086656 | bytes 8388608 | tf_op jit(solution)/shard_map/dot_general | solution.py:527
  213.2 2.0 dynamic-slice_add_fusion.own_ref
  215.2 28.5 %shard_map.144 = f32[128,1024]{1,0:T(8,128)} custom-call(bf16[4,128,1024]{2,1,0:T(8,128)(2,1)} %bitcast.87, f32[128,1024]{1,0:T(8,128)} %dynamic-slice_add_fusion.own_ref), custom_call_target="tpu_custom_call" | custom-call | tf_op jit(solution)/shard_map/pallas_call | solution.py:318
  246.2 1.9 fusion.80
  248.1 2.8 %copy.59 = bf16[1,1,32,2,16,4,128]{6,5,4,3,2,1,0:T(4,128)(2,1)} copy(bf16[1,1,32,2,16,4,128]{6,5,4,3,2,1,0:T(4,128)(2,1)} %bitcast.9) | data formatting | bytes 2097152
  (95 shorter events, 28.7 us)
Async XLA Ops:
  7.2 1.5 copy-start
  7.2 82.8 %all-gather.4.cloned.1.call-start = ((), (), s32[]{:S(2)}) async-start(), calls=%async_computation.1 | async-start | bytes 1966080 | tf_op jit(solution)/shard_map/all_gather | solution.py:377
  7.9 92.0 %all-gather.6.cloned.1.call-start = ((), (), s32[]{:S(2)}) async-start(), calls=%async_computation.2 | async-start | bytes 2621440 | tf_op jit(solution)/shard_map/all_gather | solution.py:380
  10.9 2.8 %copy-start.14 = (s32[1,32,1]{1,2,0:T(1,128)S(1)}, s32[1,32,1]{1,2,0:T(1,128)}, u32[]{:S(2)}) copy-start(s32[1,32,1]{1,2,0:T(1,128)} %param.25) | copy-start | bytes 388
  17.9 17.7 %copy-start.13 = (s32[1,128]{1,0:T(1,128)S(1)}, s32[1,128]{1,0:T(1,128)}, u32[]{:S(2)}) copy-start(s32[1,128]{1,0:T(1,128)} %param.24) | copy-start | bytes 1540
  17.9 19.4 %copy-start.3 = (s32[1,16384]{1,0:T(1,128)S(1)}, s32[1,16384]{1,0:T(1,128)}, u32[]{:S(2)}) copy-start(s32[1,16384]{1,0:T(1,128)} %param.23) | copy-start | bytes 196612
  17.9 60.0 %all-to-all-start = ((bf16[32,2,16,4,128]{4,3,2,1,0:T(4,128)(2,1)}), bf16[32,2,16,4,128]{4,3,2,1,0:T(4,128)(2,1)}, u32[]{:S(2)}, u32[]{:S(2)}) async-start(bf16[32,2,16,4,128]{4,3,2,1,0:T(4,128)(2,1)} %reshape.184), calls=%async_computation | async-start | bytes 2097152 | tf_op jit(solution)/shard_map/all_to_all | solution.py:410
  29.2 102.5 %all-gather.8.cloned.1.call-start = ((), (), s32[]{:S(2)}) async-start(), calls=%async_computation.3 | async-start | bytes 2621440 | tf_op jit(solution)/shard_map/all_gather | solution.py:381
  30.0 40.6 %collective-permute-start.1 = (bf16[256,4,128]{0,2,1:T(8,128)(2,1)}, bf16[256,4,128]{0,2,1:T(8,128)(2,1)}, u32[]{:S(2)}, u32[]{:S(2)}) collective-permute-start(bf16[256,4,128]{0,2,1:T(8,128)(2,1)} %get-tuple-element.15), channel_id=1, source_target_pairs={{16,0},{32,16},{48,32},{64,48},{80,64},{96,80},{112,96},{128,112},... | collective-permute-start | bytes 786440 | tf_op jit(solution)/shard_map/ppermute | solution.py:24
  32.4 38.3 %collective-permute-start = (bf16[256,4,128]{0,2,1:T(8,128)(2,1)}, bf16[256,4,128]{0,2,1:T(8,128)(2,1)}, u32[]{:S(2)}, u32[]{:S(2)}) collective-permute-start(bf16[256,4,128]{0,2,1:T(8,128)(2,1)} %get-tuple-element.14), channel_id=1, source_target_pairs={{0,16},{16,32},{32,48},{48,64},{64,80},{80,96},{96,112},{112,128},... | collective-permute-start | bytes 786440 | tf_op jit(solution)/shard_map/ppermute | solution.py:21
  70.7 1.4 copy-start.4
  72.1 1.0 copy-start.6
  77.9 2.7 %copy-start.5 = (pred[512,1024]{1,0:T(8,128)(4,1)S(1)}, pred[512,1024]{1,0:T(8,128)(4,1)}, u32[]{:S(2)}) copy-start(pred[512,1024]{1,0:T(8,128)(4,1)} %copy-done.4) | copy-start | bytes 1572868
  80.6 6.5 %copy-start.2 = (f32[4,512,1024]{2,1,0:T(8,128)S(1)}, f32[4,512,1024]{2,1,0:T(8,128)}, u32[]{:S(2)}) copy-start(f32[4,512,1024]{2,1,0:T(8,128)} %get-tuple-element.17) | copy-start | bytes 25165828
  85.6 1.5 copy-start.7
  97.7 20.6 %copy-start.15 = (bf16[512,4,64]{0,2,1:T(8,128)(2,1)S(1)}, bf16[512,4,64]{0,2,1:T(8,128)(2,1)}, u32[]{:S(2)}) copy-start(bf16[512,4,64]{0,2,1:T(8,128)(2,1)} %fusion.62) | copy-start | bytes 786436
  98.1 33.5 %copy-start.8 = (bf16[256,1024]{1,0:T(8,128)(2,1)S(1)}, bf16[256,1024]{1,0:T(8,128)(2,1)}, u32[]{:S(2)}) copy-start(bf16[256,1024]{1,0:T(8,128)(2,1)} %param.16) | copy-start | bytes 1572868
  133.1 30.8 %copy-start.9 = (f32[1024]{0:T(1024)S(1)}, f32[1024]{0:T(1024)}, u32[]{:S(2)}) copy-start(f32[1024]{0:T(1024)} %param.18) | copy-start | bytes 12292
  133.1 30.8 %copy-start.10 = (f32[1024]{0:T(1024)S(1)}, f32[1024]{0:T(1024)}, u32[]{:S(2)}) copy-start(f32[1024]{0:T(1024)} %param.17) | copy-start | bytes 12292
  202.6 10.5 %copy-start.1 = (f32[128,1024]{1,0:T(8,128)S(1)}, f32[128,1024]{1,0:T(8,128)}, u32[]{:S(2)}) copy-start(f32[128,1024]{1,0:T(8,128)} %shard_map.142) | copy-start | bytes 1572868
  213.2 33.0 %copy-start.11 = (f32[1024]{0:T(1024)S(1)}, f32[1024]{0:T(1024)}, u32[]{:S(2)}) copy-start(f32[1024]{0:T(1024)} %param.22) | copy-start | bytes 12292
  213.2 33.0 %copy-start.12 = (f32[1024]{0:T(1024)S(1)}, f32[1024]{0:T(1024)}, u32[]{:S(2)}) copy-start(f32[1024]{0:T(1024)} %param.21) | copy-start | bytes 12292
Sparse Core Ops, SparseCore 0:
  10.1 40.1 all-gather.3
  52.4 38.0 all-gather.5
  92.6 39.0 all-gather.7

commit v7 on v6

--- a/solution.py
+++ b/solution.py
@@ -408,8 +408,8 @@
     ).astype(jnp.bfloat16)
     outgoing = outgoing.reshape(n_seq, capacity, page_len, heads_here, 2 * head_dim)
     arrived = lax.all_to_all(outgoing, "seq", split_axis=0, concat_axis=0, tiled=True)
+    arrived, glob_rows = lax.optimization_barrier((arrived, glob_rows))
     page_pool = arrived[None, None]
-    page_pool, glob_rows = lax.optimization_barrier((page_pool, glob_rows))
 
     kv_ext = padded(kv_local, (("seq", 0),), HALF)
 
@@ -509,7 +509,6 @@
         shard_len, heads_here * head_dim
     )
 
-    attention, f_out = lax.optimization_barrier((attention, f_out))
 
     out_rows = shard_len // n_col
     proj = jnp.dot(attention, out_weight, preferred_element_type=jnp.float32)

time: 259 us -> 248 us (0.958)
  the two profiles are of different devices: /device:TPU:1 before, /device:TPU:20 now
where the time goes in v7:
time: 248 us; the launch traced here: 246 us
  Pallas kernels  141 us (57%)
  matrix products  35.2 us (14%)
  other arithmetic  20.4 us (8%)
  local copies, waits for them, and re-layouts  18.2 us (7%)
  starting transfers between devices  16.2 us (7%)
  between operations  14.2 us (6%)
    pallas_call x2, Pallas kernels, col_reduce_scatter(): pl.pallas_call(col_sum_kernel, out_shape=jax.ShapeDtypeStruct(own.shape,...  65.6 us
    pallas_call x1, Pallas kernels, col_gather(): pl.pallas_call(col_gather_kernel, out_shape=jax.ShapeDtypeStruct((m,) + b...  32 us
    pallas_call x1, Pallas kernels, seq_direct_gather(): pl.pallas_call(seq_direct_gather_kernel, out_shape=jax.ShapeDtypeStruct((...  24.9 us
    pallas_call x1, Pallas kernels, seq_direct_merge(): pl.pallas_call(functools.partial(seq_merge_kernel, top_lane), out_shape=j...  18.5 us
    dot_general x1, matrix products, per_device(): ffn_full = jnp.dot(ffn_hidden, f_out, preferred_element_type=jnp.float32)  10.5 us
    all_to_all x1, starting transfers between devices, per_device(): lax.all_to_all(outgoing, 'seq', split_axis=0, concat_axis=0, tiled=True)  9.59 us
    reduce_sum x2, other arithmetic, per_device(): total = jnp.sum(e_win, axis=2) + jnp.sum(e_glob, axis=2)  5.2 us
    unnamed x33, local copies, waits for them, and re-layouts  5.03 us
  transfers between devices with their start and end apart: 6, of which 0 were waited for; matrix products, arithmetic and copies ran while one was open for 21% of the time, Pallas kernels for 45%

profile of v7, /device:TPU:20, one launch (start us, length us, event | category | flops | bytes accessed | tf_op | source)
XLA Modules:
  0.0 246.4 jit_solution(5500164303266651697)
XLA Ops:
  8.7 2.2 convolution_convert_fusion.2
  12.3 1.4 reshape.183
  15.3 2.6 %reshape.184 = bf16[32,2,16,4,128]{4,3,2,1,0:T(4,128)(2,1)} reshape(bf16[64,8192]{1,0:T(8,128)(2,1)} %convolution_convert_fusion) | data formatting | bytes 2097152 | tf_op jit(solution)/shard_map/reshape | solution.py:409
  17.9 9.6 %all-to-all-start = ((bf16[32,2,16,4,128]{4,3,2,1,0:T(4,128)(2,1)}), bf16[32,2,16,4,128]{4,3,2,1,0:T(4,128)(2,1)}, u32[]{:S(2)}, u32[]{:S(2)}) async-start(bf16[32,2,16,4,128]{4,3,2,1,0:T(4,128)(2,1)} %reshape.184), calls=%async_computation | async-start | bytes 2097152 | tf_op jit(solution)/shard_map/all_to_all | solution.py:410
  28.4 2.0 collective-permute-start
  30.4 4.4 %collective-permute-start.1 = (bf16[256,4,128]{0,2,1:T(8,128)(2,1)}, bf16[256,4,128]{0,2,1:T(8,128)(2,1)}, u32[]{:S(2)}, u32[]{:S(2)}) collective-permute-start(bf16[256,4,128]{0,2,1:T(8,128)(2,1)} %get-tuple-element.11), channel_id=1, source_target_pairs={{16,0},{32,16},{48,32},{64,48},{80,64},{96,80},{112,96},{128,112},... | collective-permute-start | bytes 786440 | tf_op jit(solution)/shard_map/ppermute | solution.py:24
  35.0 1.5 convolution_convert_fusion.6
  38.7 24.9 %shard_map.140 = bf16[32,32,128]{2,1,0:T(8,128)(2,1)} custom-call(bf16[32,128]{1,0:T(8,128)(2,1)} %reshape.185.x_ref), custom_call_target="tpu_custom_call" | custom-call | tf_op jit(solution)/shard_map/pallas_call | solution.py:187
  68.3 4.8 %select_reduce_fusion = (f32[4,512]{1,0:T(4,128)S(1)}, f32[4,512,1024]{2,1,0:T(8,128)}) fusion(pred[512,1024]{1,0:T(8,128)(4,1)S(1)} %fusion.15, bf16[1024,4,128]{0,2,1:T(8,128)(2,1)S(1)} %pad_maximum_fusion, bf16[512,4,192]{0,2,1:T(8,128)(2,1)S(1)} %bitcast.83), kind=kOutput, calls=%fused_computation.3 | convolution fusion | flops 274724864 | bytes 9707520 | tf_op jit(solution)/shard_map/qhd,khd->hqk/dot_general | solution.py:482
  75.0 5.0 %fusion = f32[4,512]{1,0:T(4,128)S(1)} fusion(f32[4,512,1024]{2,1,0:T(8,128)} %get-tuple-element.13, f32[4,512]{1,0:T(4,128)S(1)} %max.7, pred[512,1024]{1,0:T(8,128)(4,1)S(1)} %copy-done.5), kind=kLoop, calls=%fused_computation.4 | loop fusion | flops 8386560 | bytes 8929280 | tf_op jit(solution)/shard_map/reduce_sum | solution.py:495
  81.1 2.9 %fusion.62 = bf16[512,4,64]{0,2,1:T(8,128)(2,1)} fusion(f32[4,64,512]{2,1,0:T(8,128)S(1)} %fusion.69, f32[4,512,1024]{2,1,0:T(8,128)S(1)} %copy-done.2, f32[4,512]{1,0:T(4,128)S(1)} %max.7, pred[512,1024]{1,0:T(8,128)(4,1)S(1)} %copy-done.5, bf16[1024,4,128]{0,2,1:T(8,128)(2,1)S(1)} %copy-done.8, f32[512,4]{0,1:T(4,128)S(1)} %add_bitcast_fusion), kind=kOutput, calls=%fused_computation.81 | convolution fusion | flops 277217280 | bytes 10240000 | tf_op jit(solution)/shard_map/hqk,khd->qhd/dot_general | solution.py:496
  83.9 2.1 convolution_convert_fusion.5
  86.9 3.3 %convolution_convert_fusion.1 = bf16[512,768]{1,0:T(8,128)(2,1)} fusion(bf16[1024,768]{0,1:T(8,128)(2,1)} %all-gather.4.cloned.1.call-done, bf16[1,512,1024]{2,1,0:T(8,128)(2,1)S(1)} %copy-done.6), kind=kOutput, calls=%fused_computation.30 | convolution fusion | flops 805699584 | bytes 3407872 | tf_op jit(solution)/shard_map/dot_general | solution.py:428
  90.2 1.4 copy.41
  95.1 18.5 %shard_map.141 = f32[16,128]{1,0:T(8,128)} custom-call(f32[32,16,128]{2,1,0:T(8,128)} %bitcast.88), custom_call_target="tpu_custom_call" | custom-call | tf_op jit(solution)/shard_map/pallas_call | solution.py:225
  115.8 1.4 fusion.137
  118.2 34.9 %shard_map.142 = f32[128,1024]{1,0:T(8,128)} custom-call(bf16[4,128,1024]{2,1,0:T(8,128)(2,1)} %bitcast.85, f32[128,1024]{1,0:T(8,128)} %convert_add_fusion.own_ref), custom_call_target="tpu_custom_call" | custom-call | tf_op jit(solution)/shard_map/pallas_call | solution.py:318
  155.5 1.9 add_convert_fusion.1.x_ref
  157.4 32.0 %shard_map.143 = bf16[4,128,1024]{2,1,0:T(8,128)(2,1)} custom-call(bf16[128,1024]{1,0:T(8,128)(2,1)} %add_convert_fusion.1.x_ref), custom_call_target="tpu_custom_call" | custom-call | tf_op jit(solution)/shard_map/pallas_call | solution.py:273
  189.5 10.5 %fusion.138 = (bf16[512,1024]{1,0:T(8,128)(2,1)}, f32[512,1024]{1,0:T(8,128)}) fusion(bf16[1024,1024]{1,0:T(8,128)(2,1)} %all-gather.8.cloned.1.call-done, bf16[512,1024]{1,0:T(8,128)(2,1)} %bitcast.86, bf16[1024,1024]{1,0:T(8,128)(2,1)} %all-gather.6.cloned.1.call-done), kind=kOutput, calls=%fused_computation.184 | convolution fusion | flops 2182086656 | bytes 8388608 | tf_op jit(solution)/shard_map/dot_general | solution.py:526
  200.0 2.0 dynamic-slice_add_fusion.own_ref
  202.0 30.7 %shard_map.144 = f32[128,1024]{1,0:T(8,128)} custom-call(bf16[4,128,1024]{2,1,0:T(8,128)(2,1)} %bitcast.87, f32[128,1024]{1,0:T(8,128)} %dynamic-slice_add_fusion.own_ref), custom_call_target="tpu_custom_call" | custom-call | tf_op jit(solution)/shard_map/pallas_call | solution.py:318
  235.2 1.9 fusion.80
  237.1 2.8 %copy.59 = bf16[1,1,32,2,16,4,128]{6,5,4,3,2,1,0:T(4,128)(2,1)} copy(bf16[1,1,32,2,16,4,128]{6,5,4,3,2,1,0:T(4,128)(2,1)} %bitcast.33) | data formatting | bytes 2097152
  (95 shorter events, 27.3 us)
Async XLA Ops:
  7.2 1.5 copy-start
  7.2 76.8 %all-gather.4.cloned.1.call-start = ((), (), s32[]{:S(2)}) async-start(), calls=%async_computation.1 | async-start | bytes 1966080 | tf_op jit(solution)/shard_map/all_gather | solution.py:377
  7.9 87.2 %all-gather.6.cloned.1.call-start = ((), (), s32[]{:S(2)}) async-start(), calls=%async_computation.2 | async-start | bytes 2621440 | tf_op jit(solution)/shard_map/all_gather | solution.py:380
  10.9 2.8 %copy-start.15 = (s32[1,32,1]{1,2,0:T(1,128)S(1)}, s32[1,32,1]{1,2,0:T(1,128)}, u32[]{:S(2)}) copy-start(s32[1,32,1]{1,2,0:T(1,128)} %param.25) | copy-start | bytes 388
  17.9 17.0 %copy-start.14 = (s32[1,128]{1,0:T(1,128)S(1)}, s32[1,128]{1,0:T(1,128)}, u32[]{:S(2)}) copy-start(s32[1,128]{1,0:T(1,128)} %param.24) | copy-start | bytes 1540
  17.9 18.6 %copy-start.3 = (s32[1,16384]{1,0:T(1,128)S(1)}, s32[1,16384]{1,0:T(1,128)}, u32[]{:S(2)}) copy-start(s32[1,16384]{1,0:T(1,128)} %param.23) | copy-start | bytes 196612
  17.9 55.2 %all-to-all-start = ((bf16[32,2,16,4,128]{4,3,2,1,0:T(4,128)(2,1)}), bf16[32,2,16,4,128]{4,3,2,1,0:T(4,128)(2,1)}, u32[]{:S(2)}, u32[]{:S(2)}) async-start(bf16[32,2,16,4,128]{4,3,2,1,0:T(4,128)(2,1)} %reshape.184), calls=%async_computation | async-start | bytes 2097152 | tf_op jit(solution)/shard_map/all_to_all | solution.py:410
  27.5 161.9 %all-gather.8.cloned.1.call-start = ((), (), s32[]{:S(2)}) async-start(), calls=%async_computation.3 | async-start | bytes 2621440 | tf_op jit(solution)/shard_map/all_gather | solution.py:381
  28.4 37.5 %collective-permute-start = (bf16[256,4,128]{0,2,1:T(8,128)(2,1)}, bf16[256,4,128]{0,2,1:T(8,128)(2,1)}, u32[]{:S(2)}, u32[]{:S(2)}) collective-permute-start(bf16[256,4,128]{0,2,1:T(8,128)(2,1)} %get-tuple-element.10), channel_id=1, source_target_pairs={{0,16},{16,32},{32,48},{48,64},{64,80},{80,96},{96,112},{112,128},... | collective-permute-start | bytes 786440 | tf_op jit(solution)/shard_map/ppermute | solution.py:21
  30.4 35.5 %collective-permute-start.1 = (bf16[256,4,128]{0,2,1:T(8,128)(2,1)}, bf16[256,4,128]{0,2,1:T(8,128)(2,1)}, u32[]{:S(2)}, u32[]{:S(2)}) collective-permute-start(bf16[256,4,128]{0,2,1:T(8,128)(2,1)} %get-tuple-element.11), channel_id=1, source_target_pairs={{16,0},{32,16},{48,32},{64,48},{80,64},{96,80},{112,96},{128,112},... | collective-permute-start | bytes 786440 | tf_op jit(solution)/shard_map/ppermute | solution.py:24
  65.9 1.4 copy-start.4
  67.3 1.0 copy-start.7
  73.9 1.1 copy-start.5
  74.6 5.4 %copy-start.8 = (bf16[1024,4,128]{0,2,1:T(8,128)(2,1)S(1)}, bf16[1024,4,128]{0,2,1:T(8,128)(2,1)}, u32[]{:S(2)}) copy-start(bf16[1024,4,128]{0,2,1:T(8,128)(2,1)} %copy-done.7) | copy-start | bytes 3145732
  75.0 6.1 %copy-start.2 = (f32[4,512,1024]{2,1,0:T(8,128)S(1)}, f32[4,512,1024]{2,1,0:T(8,128)}, u32[]{:S(2)}) copy-start(f32[4,512,1024]{2,1,0:T(8,128)} %get-tuple-element.13) | copy-start | bytes 25165828
  83.9 3.0 %copy-start.6 = (bf16[1,512,1024]{2,1,0:T(8,128)(2,1)S(1)}, bf16[1,512,1024]{2,1,0:T(8,128)(2,1)}, u32[]{:S(2)}) copy-start(bf16[1,512,1024]{2,1,0:T(8,128)(2,1)} %param.13) | copy-start | bytes 3145732
  94.3 21.6 %copy-start.9 = (bf16[256,1024]{1,0:T(8,128)(2,1)S(1)}, bf16[256,1024]{1,0:T(8,128)(2,1)}, u32[]{:S(2)}) copy-start(bf16[256,1024]{1,0:T(8,128)(2,1)} %param.16) | copy-start | bytes 1572868
  117.3 38.2 %copy-start.10 = (f32[1024]{0:T(1024)S(1)}, f32[1024]{0:T(1024)}, u32[]{:S(2)}) copy-start(f32[1024]{0:T(1024)} %param.18) | copy-start | bytes 12292
  117.3 38.3 %copy-start.11 = (f32[1024]{0:T(1024)S(1)}, f32[1024]{0:T(1024)}, u32[]{:S(2)}) copy-start(f32[1024]{0:T(1024)} %param.17) | copy-start | bytes 12292
  189.4 10.5 %copy-start.1 = (f32[128,1024]{1,0:T(8,128)S(1)}, f32[128,1024]{1,0:T(8,128)}, u32[]{:S(2)}) copy-start(f32[128,1024]{1,0:T(8,128)} %shard_map.142) | copy-start | bytes 1572868
  200.0 35.2 %copy-start.12 = (f32[1024]{0:T(1024)S(1)}, f32[1024]{0:T(1024)}, u32[]{:S(2)}) copy-start(f32[1024]{0:T(1024)} %param.22) | copy-start | bytes 12292
  200.0 35.2 %copy-start.13 = (f32[1024]{0:T(1024)S(1)}, f32[1024]{0:T(1024)}, u32[]{:S(2)}) copy-start(f32[1024]{0:T(1024)} %param.21) | copy-start | bytes 12292
Sparse Core Ops, SparseCore 0:
  10.1 39.6 all-gather.3
  51.9 36.3 all-gather.5
  90.4 40.8 all-gather.7

commit v8 on v7

--- a/solution.py
+++ b/solution.py
@@ -327,6 +327,72 @@
         ],
         compiler_params=pltpu.CompilerParams(collective_id=collective_id, has_side_effects=True),
     )(parts, own)
+
+
+def col_mid_kernel(x_ref, own_ref, gain_ref, bias_ref, out_ref, got, rs_send, rs_recv, g_send, g_recv):
+    me, peers = col_peers()
+    copies = []
+    for j, peer in enumerate(peers):
+        copy = pltpu.make_async_remote_copy(
+            src_ref=x_ref.at[peer[2]],
+            dst_ref=got.at[j],
+            send_sem=rs_send.at[j],
+            recv_sem=rs_recv.at[j],
+            device_id=peer,
+            device_id_type=MESH,
+        )
+        copy.start()
+        copies.append(copy)
+    for copy in copies:
+        copy.wait()
+    chunk = 32
+    width = out_ref.shape[2]
+
+    def body(i, carry):
+        rows = pl.ds(pl.multiple_of(i * chunk, chunk), chunk)
+        total = own_ref[rows, :]
+        for j in range(len(copies)):
+            total = total + got[j, rows, :].astype(jnp.float32)
+        center = total - jnp.sum(total, axis=1, keepdims=True) / width
+        spread = jnp.sum(center * center, axis=1, keepdims=True) / width
+        normed = center / jnp.sqrt(spread + 1e-05) * gain_ref[...] + bias_ref[...]
+        out_ref[me, rows, :] = normed.astype(out_ref.dtype)
+        return carry
+
+    lax.fori_loop(0, out_ref.shape[1] // chunk, body, 0)
+    sends = []
+    for j, peer in enumerate(peers):
+        copy = pltpu.make_async_remote_copy(
+            src_ref=out_ref.at[me],
+            dst_ref=out_ref.at[me],
+            send_sem=g_send.at[j],
+            recv_sem=g_recv.at[j],
+            device_id=peer,
+            device_id_type=MESH,
+        )
+        copy.start()
+        sends.append(copy)
+    for copy in sends:
+        copy.wait()
+
+
+def col_sum_norm_gather(parts, own, gain, bias):
+    m = lax.axis_size("col")
+    rows, width = own.shape
+    return pl.pallas_call(
+        col_mid_kernel,
+        out_shape=jax.ShapeDtypeStruct((m, rows, width), jnp.bfloat16),
+        in_specs=[pl.BlockSpec(memory_space=pltpu.VMEM)] * 4,
+        out_specs=pl.BlockSpec(memory_space=pltpu.VMEM),
+        scratch_shapes=[
+            pltpu.VMEM((m - 1,) + parts.shape[1:], parts.dtype),
+            pltpu.SemaphoreType.DMA((m - 1,)),
+            pltpu.SemaphoreType.DMA((m - 1,)),
+            pltpu.SemaphoreType.DMA((m - 1,)),
+            pltpu.SemaphoreType.DMA((m - 1,)),
+        ],
+        compiler_params=pltpu.CompilerParams(collective_id=7, has_side_effects=True),
+    )(parts, own, gain.reshape(1, width), bias.reshape(1, width))
 
 
 def layer_norm(values, gain, bias):
@@ -514,13 +580,14 @@
     proj = jnp.dot(attention, out_weight, preferred_element_type=jnp.float32)
     proj_own = lax.dynamic_slice_in_dim(proj, col_index * out_rows, out_rows, 0)
     token_own = lax.dynamic_slice_in_dim(tokens, col_index * out_rows, out_rows, 0)
-    summed = col_reduce_scatter(
+    middle_all = col_sum_norm_gather(
         proj.astype(jnp.bfloat16).reshape(n_col, out_rows, width),
         token_own.astype(jnp.float32) + proj_own,
-        3,
-    )
-    mine = layer_norm(summed, ln_gain, ln_bias).astype(jnp.bfloat16)
-    middle = col_gather(mine).reshape(shard_len, width)
+        ln_gain,
+        ln_bias,
+    )
+    mine = middle_all[col_index]
+    middle = middle_all.reshape(shard_len, width)
     ffn_pre = jnp.dot(middle, f_in, preferred_element_type=jnp.float32)
     ffn_hidden = jax.nn.gelu(ffn_pre, approximate=False).astype(jnp.bfloat16)
     ffn_full = jnp.dot(ffn_hidden, f_out, preferred_element_type=jnp.float32)

time: 248 us -> 241 us (0.972)
  the two profiles are of different devices: /device:TPU:20 before, /device:TPU:25 now
where the time goes in v8:
time: 241 us; the launch traced here: 240 us
  Pallas kernels  138 us (57%)
  matrix products  37.1 us (15%)
  local copies, waits for them, and re-layouts  17.7 us (7%)
  other arithmetic  16 us (7%)
  starting transfers between devices  15.8 us (7%)
  between operations  14.2 us (6%)
    pallas_call x1, Pallas kernels, col_sum_norm_gather(): pl.pallas_call(col_mid_kernel, out_shape=jax.ShapeDtypeStruct((m, rows, w...  55.2 us
    pallas_call x1, Pallas kernels, col_reduce_scatter(): pl.pallas_call(col_sum_kernel, out_shape=jax.ShapeDtypeStruct(own.shape,...  37.9 us
    pallas_call x1, Pallas kernels, seq_direct_gather(): pl.pallas_call(seq_direct_gather_kernel, out_shape=jax.ShapeDtypeStruct((...  25.5 us
    pallas_call x1, Pallas kernels, seq_direct_merge(): pl.pallas_call(functools.partial(seq_merge_kernel, top_lane), out_shape=j...  19.1 us
    dot_general x1, matrix products, per_device(): ffn_full = jnp.dot(ffn_hidden, f_out, preferred_element_type=jnp.float32)  10.5 us
    all_to_all x1, starting transfers between devices, per_device(): lax.all_to_all(outgoing, 'seq', split_axis=0, concat_axis=0, tiled=True)  10.4 us
    reduce_sum x2, other arithmetic, per_device(): total = jnp.sum(e_win, axis=2) + jnp.sum(e_glob, axis=2)  5.22 us
    dot_general x1, matrix products, per_device(): jnp.einsum('qhd,khd->hqk', queries, k_blk, preferred_element_type=jnp.flo...  4.83 us
  transfers between devices with their start and end apart: 6, of which 0 were waited for; matrix products, arithmetic and copies ran while one was open for 21% of the time, Pallas kernels for 42%

profile of v8, /device:TPU:25, one launch (start us, length us, event | category | flops | bytes accessed | tf_op | source)
XLA Modules:
  0.0 239.7 jit_solution(5200816928297512794)
XLA Ops:
  8.7 2.2 convolution_convert_fusion.2
  12.3 1.4 reshape.177
  14.0 1.4 convolution_convert_fusion
  15.3 2.6 %reshape.178 = bf16[32,2,16,4,128]{4,3,2,1,0:T(4,128)(2,1)} reshape(bf16[64,8192]{1,0:T(8,128)(2,1)} %convolution_convert_fusion) | data formatting | bytes 2097152 | tf_op jit(solution)/shard_map/reshape | solution.py:475
  17.9 10.4 %all-to-all-start = ((bf16[32,2,16,4,128]{4,3,2,1,0:T(4,128)(2,1)}), bf16[32,2,16,4,128]{4,3,2,1,0:T(4,128)(2,1)}, u32[]{:S(2)}, u32[]{:S(2)}) async-start(bf16[32,2,16,4,128]{4,3,2,1,0:T(4,128)(2,1)} %reshape.178), calls=%async_computation | async-start | bytes 2097152 | tf_op jit(solution)/shard_map/all_to_all | solution.py:476
  29.2 3.4 %collective-permute-start = (bf16[256,4,128]{0,2,1:T(8,128)(2,1)}, bf16[256,4,128]{0,2,1:T(8,128)(2,1)}, u32[]{:S(2)}, u32[]{:S(2)}) collective-permute-start(bf16[256,4,128]{0,2,1:T(8,128)(2,1)} %get-tuple-element.10), channel_id=1, source_target_pairs={{0,16},{16,32},{32,48},{48,64},{64,80},{80,96},{96,112},{112,128},... | collective-permute-start | bytes 786440 | tf_op jit(solution)/shard_map/ppermute | solution.py:21
  32.6 1.9 collective-permute-start.1
  34.6 1.5 convolution_convert_fusion.6
  38.4 25.5 %shard_map.140 = bf16[32,32,128]{2,1,0:T(8,128)(2,1)} custom-call(bf16[32,128]{1,0:T(8,128)(2,1)} %reshape.179.x_ref), custom_call_target="tpu_custom_call" | custom-call | tf_op jit(solution)/shard_map/pallas_call | solution.py:187
  68.5 4.8 %select_reduce_fusion = (f32[4,512]{1,0:T(4,128)S(1)}, f32[4,512,1024]{2,1,0:T(8,128)}) fusion(pred[512,1024]{1,0:T(8,128)(4,1)S(1)} %fusion.15, bf16[1024,4,128]{0,2,1:T(8,128)(2,1)S(1)} %pad_maximum_fusion, bf16[512,4,192]{0,2,1:T(8,128)(2,1)S(1)} %bitcast.88), kind=kOutput, calls=%fused_computation.3 | convolution fusion | flops 274724864 | bytes 9707520 | tf_op jit(solution)/shard_map/qhd,khd->hqk/dot_general | solution.py:548
  76.3 5.0 %fusion = f32[4,512]{1,0:T(4,128)S(1)} fusion(f32[4,512,1024]{2,1,0:T(8,128)} %get-tuple-element.13, f32[4,512]{1,0:T(4,128)S(1)} %max.7, pred[512,1024]{1,0:T(8,128)(4,1)S(1)} %copy-done.4), kind=kLoop, calls=%fused_computation.4 | loop fusion | flops 8386560 | bytes 8929280 | tf_op jit(solution)/shard_map/reduce_sum | solution.py:561
  81.3 1.4 fusion.69
  82.8 2.9 %fusion.62 = bf16[512,4,64]{0,2,1:T(8,128)(2,1)} fusion(f32[4,64,512]{2,1,0:T(8,128)S(1)} %fusion.69, f32[4,512,1024]{2,1,0:T(8,128)S(1)} %copy-done.1, f32[4,512]{1,0:T(4,128)S(1)} %max.7, pred[512,1024]{1,0:T(8,128)(4,1)S(1)} %copy-done.4, bf16[1024,4,128]{0,2,1:T(8,128)(2,1)S(1)} %copy-done.7, f32[512,4]{0,1:T(4,128)S(1)} %add_bitcast_fusion), kind=kOutput, calls=%fused_computation.81 | convolution fusion | flops 277217280 | bytes 10240000 | tf_op jit(solution)/shard_map/hqk,khd->qhd/dot_general | solution.py:562
  85.7 2.1 convolution_convert_fusion.5
  88.6 3.3 %convolution_convert_fusion.1 = bf16[512,768]{1,0:T(8,128)(2,1)} fusion(bf16[1024,768]{0,1:T(8,128)(2,1)} %all-gather.4.cloned.1.call-done, bf16[1,512,1024]{2,1,0:T(8,128)(2,1)S(1)} %copy-done.5), kind=kOutput, calls=%fused_computation.30 | convolution fusion | flops 805699584 | bytes 3407872 | tf_op jit(solution)/shard_map/dot_general | solution.py:494
  91.9 1.4 copy.41
  96.9 19.1 %shard_map.141 = f32[16,128]{1,0:T(8,128)} custom-call(f32[32,16,128]{2,1,0:T(8,128)} %bitcast.93), custom_call_target="tpu_custom_call" | custom-call | tf_op jit(solution)/shard_map/pallas_call | solution.py:225
  118.1 1.4 fusion.137
  120.4 55.2 %shard_map.142 = bf16[4,128,1024]{2,1,0:T(8,128)(2,1)} custom-call(bf16[4,128,1024]{2,1,0:T(8,128)(2,1)} %bitcast.90, f32[128,1024]{1,0:T(8,128)} %convert_add_fusion.1.own_ref, f32[1,1024]{1,0:T(1,128)} %bitcast.107, f32[1,1024]{1,0:T(1,128)} %bitcast.108), custom_call_target="tpu_custom_call" | custom-call | tf_op jit(solution)/shard_map/pallas_call | solution.py:382
  175.6 10.5 %fusion.138 = (bf16[512,1024]{1,0:T(8,128)(2,1)}, f32[512,1024]{1,0:T(8,128)}) fusion(bf16[1024,1024]{1,0:T(8,128)(2,1)} %all-gather.8.cloned.1.call-done, bf16[512,1024]{1,0:T(8,128)(2,1)} %bitcast.91, bf16[1024,1024]{1,0:T(8,128)(2,1)} %all-gather.6.cloned.1.call-done), kind=kOutput, calls=%fused_computation.180 | convolution fusion | flops 2182086656 | bytes 8388608 | tf_op jit(solution)/shard_map/dot_general | solution.py:593
  186.1 2.0 convert_add_fusion.own_ref
  188.0 37.9 %shard_map.143 = f32[128,1024]{1,0:T(8,128)} custom-call(bf16[4,128,1024]{2,1,0:T(8,128)(2,1)} %bitcast.92, f32[128,1024]{1,0:T(8,128)} %convert_add_fusion.own_ref), custom_call_target="tpu_custom_call" | custom-call | tf_op jit(solution)/shard_map/pallas_call | solution.py:318
  228.4 1.9 fusion.80
  230.3 2.8 %copy.59 = bf16[1,1,32,2,16,4,128]{6,5,4,3,2,1,0:T(4,128)(2,1)} copy(bf16[1,1,32,2,16,4,128]{6,5,4,3,2,1,0:T(4,128)(2,1)} %bitcast.36) | data formatting | bytes 2097152
  (83 shorter events, 23.5 us)
Async XLA Ops:
  7.2 1.5 copy-start
  7.2 78.5 %all-gather.4.cloned.1.call-start = ((), (), s32[]{:S(2)}) async-start(), calls=%async_computation.1 | async-start | bytes 1966080 | tf_op jit(solution)/shard_map/all_gather | solution.py:443
  7.9 88.9 %all-gather.6.cloned.1.call-start = ((), (), s32[]{:S(2)}) async-start(), calls=%async_computation.2 | async-start | bytes 2621440 | tf_op jit(solution)/shard_map/all_gather | solution.py:446
  10.9 2.8 %copy-start.12 = (s32[1,32,1]{1,2,0:T(1,128)S(1)}, s32[1,32,1]{1,2,0:T(1,128)}, u32[]{:S(2)}) copy-start(s32[1,32,1]{1,2,0:T(1,128)} %param.25) | copy-start | bytes 388
  17.9 16.6 %copy-start.11 = (s32[1,128]{1,0:T(1,128)S(1)}, s32[1,128]{1,0:T(1,128)}, u32[]{:S(2)}) copy-start(s32[1,128]{1,0:T(1,128)} %param.24) | copy-start | bytes 1540
  17.9 18.2 %copy-start.2 = (s32[1,16384]{1,0:T(1,128)S(1)}, s32[1,16384]{1,0:T(1,128)}, u32[]{:S(2)}) copy-start(s32[1,16384]{1,0:T(1,128)} %param.23) | copy-start | bytes 196612
  17.9 55.4 %all-to-all-start = ((bf16[32,2,16,4,128]{4,3,2,1,0:T(4,128)(2,1)}), bf16[32,2,16,4,128]{4,3,2,1,0:T(4,128)(2,1)}, u32[]{:S(2)}, u32[]{:S(2)}) async-start(bf16[32,2,16,4,128]{4,3,2,1,0:T(4,128)(2,1)} %reshape.178), calls=%async_computation | async-start | bytes 2097152 | tf_op jit(solution)/shard_map/all_to_all | solution.py:476
  28.3 147.3 %all-gather.8.cloned.1.call-start = ((), (), s32[]{:S(2)}) async-start(), calls=%async_computation.3 | async-start | bytes 2621440 | tf_op jit(solution)/shard_map/all_gather | solution.py:447
  29.2 37.0 %collective-permute-start = (bf16[256,4,128]{0,2,1:T(8,128)(2,1)}, bf16[256,4,128]{0,2,1:T(8,128)(2,1)}, u32[]{:S(2)}, u32[]{:S(2)}) collective-permute-start(bf16[256,4,128]{0,2,1:T(8,128)(2,1)} %get-tuple-element.10), channel_id=1, source_target_pairs={{0,16},{16,32},{32,48},{48,64},{64,80},{80,96},{96,112},{112,128},... | collective-permute-start | bytes 786440 | tf_op jit(solution)/shard_map/ppermute | solution.py:21
  32.6 33.6 %collective-permute-start.1 = (bf16[256,4,128]{0,2,1:T(8,128)(2,1)}, bf16[256,4,128]{0,2,1:T(8,128)(2,1)}, u32[]{:S(2)}, u32[]{:S(2)}) collective-permute-start(bf16[256,4,128]{0,2,1:T(8,128)(2,1)} %get-tuple-element.11), channel_id=1, source_target_pairs={{16,0},{32,16},{48,32},{64,48},{80,64},{96,80},{112,96},{128,112},... | collective-permute-start | bytes 786440 | tf_op jit(solution)/shard_map/ppermute | solution.py:24
  66.1 1.4 copy-start.3
  67.5 1.0 copy-start.6
  73.3 2.9 %copy-start.4 = (pred[512,1024]{1,0:T(8,128)(4,1)S(1)}, pred[512,1024]{1,0:T(8,128)(4,1)}, u32[]{:S(2)}) copy-start(pred[512,1024]{1,0:T(8,128)(4,1)} %copy-done.3) | copy-start | bytes 1572868
  76.3 6.5 %copy-start.1 = (f32[4,512,1024]{2,1,0:T(8,128)S(1)}, f32[4,512,1024]{2,1,0:T(8,128)}, u32[]{:S(2)}) copy-start(f32[4,512,1024]{2,1,0:T(8,128)} %get-tuple-element.13) | copy-start | bytes 25165828
  76.3 6.5 %copy-start.7 = (bf16[1024,4,128]{0,2,1:T(8,128)(2,1)S(1)}, bf16[1024,4,128]{0,2,1:T(8,128)(2,1)}, u32[]{:S(2)}) copy-start(bf16[1024,4,128]{0,2,1:T(8,128)(2,1)} %copy-done.6) | copy-start | bytes 3145732
  85.7 3.0 %copy-start.5 = (bf16[1,512,1024]{2,1,0:T(8,128)(2,1)S(1)}, bf16[1,512,1024]{2,1,0:T(8,128)(2,1)}, u32[]{:S(2)}) copy-start(bf16[1,512,1024]{2,1,0:T(8,128)(2,1)} %param.13) | copy-start | bytes 3145732
  96.0 22.2 %copy-start.8 = (bf16[256,1024]{1,0:T(8,128)(2,1)S(1)}, bf16[256,1024]{1,0:T(8,128)(2,1)}, u32[]{:S(2)}) copy-start(bf16[256,1024]{1,0:T(8,128)(2,1)} %param.16) | copy-start | bytes 1572868
  186.1 42.3 %copy-start.9 = (f32[1024]{0:T(1024)S(1)}, f32[1024]{0:T(1024)}, u32[]{:S(2)}) copy-start(f32[1024]{0:T(1024)} %param.22) | copy-start | bytes 12292
  186.1 42.3 %copy-start.10 = (f32[1024]{0:T(1024)S(1)}, f32[1024]{0:T(1024)}, u32[]{:S(2)}) copy-start(f32[1024]{0:T(1024)} %param.21) | copy-start | bytes 12292
Sparse Core Ops, SparseCore 0:
  10.1 38.9 all-gather.3
  51.2 38.2 all-gather.5
  91.6 39.2 all-gather.7

commit v9 on v8

--- a/solution.py
+++ b/solution.py
@@ -233,6 +233,138 @@
             pltpu.SemaphoreType.DMA((n - 1,)),
         ],
         compiler_params=pltpu.CompilerParams(collective_id=5, has_side_effects=True),
+    )(parts)
+
+
+def seq_two_level_peers(group):
+    me, n = lax.axis_index("seq"), lax.axis_size("seq")
+    row, col = lax.axis_index("row"), lax.axis_index("col")
+    first = (me // group) * group
+    near = [first + lax.rem(me - first + j, group) for j in range(1, group)]
+    far = [lax.rem(me + group * j, n) for j in range(1, n // group)]
+    barrier = pltpu.get_barrier_semaphore()
+    for peer in near + far:
+        pl.semaphore_signal(barrier, inc=1, device_id=(peer, row, col), device_id_type=MESH)
+    pl.semaphore_wait(barrier, len(near) + len(far))
+    return me, first, [(p, row, col) for p in near], [(p, row, col) for p in far]
+
+
+def seq_gather2_kernel(group, x_ref, out_ref, self_sem, near_send, near_recv, far_send, far_recv):
+    me, first, near, far = seq_two_level_peers(group)
+    own = pltpu.make_async_copy(x_ref, out_ref.at[me], self_sem)
+    own.start()
+    copies = []
+    for j, peer in enumerate(near):
+        copy = pltpu.make_async_remote_copy(
+            src_ref=x_ref,
+            dst_ref=out_ref.at[me],
+            send_sem=near_send.at[j],
+            recv_sem=near_recv.at[j],
+            device_id=peer,
+            device_id_type=MESH,
+        )
+        copy.start()
+        copies.append(copy)
+    own.wait()
+    for copy in copies:
+        copy.wait()
+    block = out_ref.at[pl.ds(first, group)]
+    copies = []
+    for j, peer in enumerate(far):
+        copy = pltpu.make_async_remote_copy(
+            src_ref=block,
+            dst_ref=block,
+            send_sem=far_send.at[j],
+            recv_sem=far_recv.at[j],
+            device_id=peer,
+            device_id_type=MESH,
+        )
+        copy.start()
+        copies.append(copy)
+    for copy in copies:
+        copy.wait()
+
+
+def seq_gather2(block, group):
+    n = lax.axis_size("seq")
+    return pl.pallas_call(
+        functools.partial(seq_gather2_kernel, group),
+        out_shape=jax.ShapeDtypeStruct((n,) + block.shape, block.dtype),
+        in_specs=[pl.BlockSpec(memory_space=pltpu.VMEM)],
+        out_specs=pl.BlockSpec(memory_space=pltpu.VMEM),
+        scratch_shapes=[
+            pltpu.SemaphoreType.DMA(()),
+            pltpu.SemaphoreType.DMA((group - 1,)),
+            pltpu.SemaphoreType.DMA((group - 1,)),
+            pltpu.SemaphoreType.DMA((n // group - 1,)),
+            pltpu.SemaphoreType.DMA((n // group - 1,)),
+        ],
+        compiler_params=pltpu.CompilerParams(collective_id=8, has_side_effects=True),
+    )(block)
+
+
+def seq_merge2_kernel(
+    group, top_lane, x_ref, out_ref, got_far, partial, got_near, far_send, far_recv, near_send, near_recv
+):
+    me, first, near, far = seq_two_level_peers(group)
+    copies = []
+    for j, peer in enumerate(far):
+        start = pl.multiple_of((peer[0] // group) * group, group)
+        copy = pltpu.make_async_remote_copy(
+            src_ref=x_ref.at[pl.ds(start, group)],
+            dst_ref=got_far.at[j],
+            send_sem=far_send.at[j],
+            recv_sem=far_recv.at[j],
+            device_id=peer,
+            device_id_type=MESH,
+        )
+        copy.start()
+        copies.append(copy)
+    for copy in copies:
+        copy.wait()
+    for k in range(group):
+        value = x_ref[first + k]
+        for j in range(len(far)):
+            value = merge_parts(value, got_far[j, k], top_lane)
+        partial[k] = value
+    copies = []
+    for j, peer in enumerate(near):
+        copy = pltpu.make_async_remote_copy(
+            src_ref=partial.at[peer[0] - first],
+            dst_ref=got_near.at[j],
+            send_sem=near_send.at[j],
+            recv_sem=near_recv.at[j],
+            device_id=peer,
+            device_id_type=MESH,
+        )
+        copy.start()
+        copies.append(copy)
+    for copy in copies:
+        copy.wait()
+    value = partial[me - first]
+    for j in range(len(near)):
+        value = merge_parts(value, got_near[j], top_lane)
+    out_ref[...] = value
+
+
+def seq_merge2(parts, top_lane, group):
+    n = parts.shape[0]
+    blk = parts.shape[1:]
+    return pl.pallas_call(
+        functools.partial(seq_merge2_kernel, group, top_lane),
+        out_shape=jax.ShapeDtypeStruct(blk, parts.dtype),
+        in_specs=[pl.BlockSpec(memory_space=pltpu.VMEM)],
+        out_specs=pl.BlockSpec(memory_space=pltpu.VMEM),
+        scratch_shapes=[
+            pltpu.VMEM((n // group - 1, group) + blk, parts.dtype),
+            pltpu.VMEM((group,) + blk, parts.dtype),
+            pltpu.VMEM((group - 1,) + blk, parts.dtype),
+            pltpu.SemaphoreType.DMA((n // group - 1,)),
+            pltpu.SemaphoreType.DMA((n // group - 1,)),
+            pltpu.SemaphoreType.DMA((group - 1,)),
+            pltpu.SemaphoreType.DMA((group - 1,)),
+        ],
+        compiler_params=pltpu.CompilerParams(collective_id=9, has_side_effects=True),
     )(parts)
 
 
@@ -438,7 +570,11 @@
     own_match = (own_pos - base)[:, None] == local_order[None, :]
     picker = own_match.astype(jnp.bfloat16)
     own_rows = jnp.dot(picker, tokens, preferred_element_type=jnp.float32).astype(jnp.bfloat16)
-    glob_rows = seq_direct_gather(own_rows.reshape(-1, 128)).reshape(n_glob, width)
+    group = 4 if n_seq % 4 == 0 and n_seq > 4 else 1
+    if group > 1:
+        glob_rows = seq_gather2(own_rows.reshape(-1, 128), group).reshape(n_glob, width)
+    else:
+        glob_rows = seq_direct_gather(own_rows.reshape(-1, 128)).reshape(n_glob, width)
 
     w_global = lax.all_gather(
         qkv_global_weight.reshape(qkv_global_weight.shape[0], -1), "row", axis=0, tiled=True
@@ -534,7 +670,11 @@
     )
     packed = jnp.transpose(packed, (1, 0, 2)).reshape(n_glob * heads_here, 128)
     packed, f_in = lax.optimization_barrier((packed, f_in))
-    merged = seq_direct_merge(packed.reshape(n_seq, -1, 128), head_dim + 1).reshape(
+    if group > 1:
+        merged = seq_merge2(packed.reshape(n_seq, -1, 128), head_dim + 1, group)
+    else:
+        merged = seq_direct_merge(packed.reshape(n_seq, -1, 128), head_dim + 1)
+    merged = merged.reshape(
         per_shard, heads_here, 128
     )
     own_out = jnp.transpose(

time: 241 us -> 237 us (0.983)
  the two profiles are of different devices: /device:TPU:25 before, /device:TPU:43 now
where the time goes in v9:
time: 237 us; the launch traced here: 235 us
  Pallas kernels  134 us (57%)
  matrix products  37.1 us (16%)
  local copies, waits for them, and re-layouts  17.7 us (7%)
  other arithmetic  15.9 us (7%)
  starting transfers between devices  15.1 us (6%)
  between operations  14.2 us (6%)
    pallas_call x1, Pallas kernels, col_sum_norm_gather(): pl.pallas_call(col_mid_kernel, out_shape=jax.ShapeDtypeStruct((m, rows, w...  57.9 us
    pallas_call x1, Pallas kernels, col_reduce_scatter(): pl.pallas_call(col_sum_kernel, out_shape=jax.ShapeDtypeStruct(own.shape,...  36.6 us
    pallas_call x1, Pallas kernels, seq_gather2(): pl.pallas_call(functools.partial(seq_gather2_kernel, group), out_shape=ja...  20.1 us
    pallas_call x1, Pallas kernels, seq_merge2(): pl.pallas_call(functools.partial(seq_merge2_kernel, group, top_lane), out...  19.5 us
    dot_general x1, matrix products, per_device(): ffn_full = jnp.dot(ffn_hidden, f_out, preferred_element_type=jnp.float32)  10.5 us
    all_to_all x1, starting transfers between devices, per_device(): lax.all_to_all(outgoing, 'seq', split_axis=0, concat_axis=0, tiled=True)  9.58 us
    reduce_sum x2, other arithmetic, per_device(): total = jnp.sum(e_win, axis=2) + jnp.sum(e_glob, axis=2)  5.17 us
    dot_general x1, matrix products, per_device(): jnp.einsum('qhd,khd->hqk', queries, k_blk, preferred_element_type=jnp.flo...  4.83 us
  transfers between devices with their start and end apart: 6, of which 0 were waited for; matrix products, arithmetic and copies ran while one was open for 21% of the time, Pallas kernels for 41%

profile of v9, /device:TPU:43, one launch (start us, length us, event | category | flops | bytes accessed | tf_op | source)
XLA Modules:
  0.0 235.5 jit_solution(10364835946754316511)
XLA Ops:
  8.7 2.2 convolution_convert_fusion.2
  12.3 1.4 reshape.177
  14.0 1.4 convolution_convert_fusion
  15.3 2.6 %reshape.178 = bf16[32,2,16,4,128]{4,3,2,1,0:T(4,128)(2,1)} reshape(bf16[64,8192]{1,0:T(8,128)(2,1)} %convolution_convert_fusion) | data formatting | bytes 2097152 | tf_op jit(solution)/shard_map/reshape | solution.py:611
  17.9 9.6 %all-to-all-start = ((bf16[32,2,16,4,128]{4,3,2,1,0:T(4,128)(2,1)}), bf16[32,2,16,4,128]{4,3,2,1,0:T(4,128)(2,1)}, u32[]{:S(2)}, u32[]{:S(2)}) async-start(bf16[32,2,16,4,128]{4,3,2,1,0:T(4,128)(2,1)} %reshape.178), calls=%async_computation | async-start | bytes 2097152 | tf_op jit(solution)/shard_map/all_to_all | solution.py:612
  28.4 3.3 %collective-permute-start = (bf16[256,4,128]{0,2,1:T(8,128)(2,1)}, bf16[256,4,128]{0,2,1:T(8,128)(2,1)}, u32[]{:S(2)}, u32[]{:S(2)}) collective-permute-start(bf16[256,4,128]{0,2,1:T(8,128)(2,1)} %get-tuple-element.10), channel_id=1, source_target_pairs={{0,16},{16,32},{32,48},{48,64},{64,80},{80,96},{96,112},{112,128},... | collective-permute-start | bytes 786440 | tf_op jit(solution)/shard_map/ppermute | solution.py:21
  31.7 2.1 collective-permute-start.1
  34.0 1.5 convolution_convert_fusion.6
  37.7 20.1 %shard_map.140 = bf16[32,32,128]{2,1,0:T(8,128)(2,1)} custom-call(bf16[32,128]{1,0:T(8,128)(2,1)} %reshape.179.x_ref), custom_call_target="tpu_custom_call" | custom-call | tf_op jit(solution)/shard_map/pallas_call | solution.py:290
  62.5 4.8 %select_reduce_fusion = (f32[4,512]{1,0:T(4,128)S(1)}, f32[4,512,1024]{2,1,0:T(8,128)}) fusion(pred[512,1024]{1,0:T(8,128)(4,1)S(1)} %fusion.15, bf16[1024,4,128]{0,2,1:T(8,128)(2,1)S(1)} %pad_maximum_fusion, bf16[512,4,192]{0,2,1:T(8,128)(2,1)S(1)} %bitcast.88), kind=kOutput, calls=%fused_computation.3 | convolution fusion | flops 274724864 | bytes 9707520 | tf_op jit(solution)/shard_map/qhd,khd->hqk/dot_general | solution.py:688
  70.3 5.0 %fusion = f32[4,512]{1,0:T(4,128)S(1)} fusion(f32[4,512,1024]{2,1,0:T(8,128)} %get-tuple-element.13, f32[4,512]{1,0:T(4,128)S(1)} %max.7, pred[512,1024]{1,0:T(8,128)(4,1)S(1)} %copy-done.4), kind=kLoop, calls=%fused_computation.4 | loop fusion | flops 8386560 | bytes 8929280 | tf_op jit(solution)/shard_map/reduce_sum | solution.py:701
  75.2 1.4 fusion.69
  76.7 2.9 %fusion.62 = bf16[512,4,64]{0,2,1:T(8,128)(2,1)} fusion(f32[4,64,512]{2,1,0:T(8,128)S(1)} %fusion.69, f32[4,512,1024]{2,1,0:T(8,128)S(1)} %copy-done.1, f32[4,512]{1,0:T(4,128)S(1)} %max.7, pred[512,1024]{1,0:T(8,128)(4,1)S(1)} %copy-done.4, bf16[1024,4,128]{0,2,1:T(8,128)(2,1)S(1)} %copy-done.7, f32[512,4]{0,1:T(4,128)S(1)} %add_bitcast_fusion), kind=kOutput, calls=%fused_computation.81 | convolution fusion | flops 277217280 | bytes 10240000 | tf_op jit(solution)/shard_map/hqk,khd->qhd/dot_general | solution.py:702
  79.6 2.2 convolution_convert_fusion.5
  82.5 3.3 %convolution_convert_fusion.1 = bf16[512,768]{1,0:T(8,128)(2,1)} fusion(bf16[1024,768]{0,1:T(8,128)(2,1)} %all-gather.4.cloned.1.call-done, bf16[1,512,1024]{2,1,0:T(8,128)(2,1)S(1)} %copy-done.5), kind=kOutput, calls=%fused_computation.30 | convolution fusion | flops 805699584 | bytes 3407872 | tf_op jit(solution)/shard_map/dot_general | solution.py:630
  85.9 1.4 copy.41
  90.8 19.5 %shard_map.141 = f32[16,128]{1,0:T(8,128)} custom-call(f32[32,16,128]{2,1,0:T(8,128)} %bitcast.93), custom_call_target="tpu_custom_call" | custom-call | tf_op jit(solution)/shard_map/pallas_call | solution.py:353
  112.5 1.4 fusion.137
  114.8 57.9 %shard_map.142 = bf16[4,128,1024]{2,1,0:T(8,128)(2,1)} custom-call(bf16[4,128,1024]{2,1,0:T(8,128)(2,1)} %bitcast.90, f32[128,1024]{1,0:T(8,128)} %convert_add_fusion.1.own_ref, f32[1,1024]{1,0:T(1,128)} %bitcast.107, f32[1,1024]{1,0:T(1,128)} %bitcast.108), custom_call_target="tpu_custom_call" | custom-call | tf_op jit(solution)/shard_map/pallas_call | solution.py:514
  172.7 10.5 %fusion.138 = (bf16[512,1024]{1,0:T(8,128)(2,1)}, f32[512,1024]{1,0:T(8,128)}) fusion(bf16[1024,1024]{1,0:T(8,128)(2,1)} %all-gather.8.cloned.1.call-done, bf16[512,1024]{1,0:T(8,128)(2,1)} %bitcast.91, bf16[1024,1024]{1,0:T(8,128)(2,1)} %all-gather.6.cloned.1.call-done), kind=kOutput, calls=%fused_computation.180 | convolution fusion | flops 2182086656 | bytes 8388608 | tf_op jit(solution)/shard_map/dot_general | solution.py:733
  183.2 2.0 convert_add_fusion.own_ref
  185.1 36.6 %shard_map.143 = f32[128,1024]{1,0:T(8,128)} custom-call(bf16[4,128,1024]{2,1,0:T(8,128)(2,1)} %bitcast.92, f32[128,1024]{1,0:T(8,128)} %convert_add_fusion.own_ref), custom_call_target="tpu_custom_call" | custom-call | tf_op jit(solution)/shard_map/pallas_call | solution.py:450
  224.2 1.9 fusion.80
  226.1 2.8 %copy.59 = bf16[1,1,32,2,16,4,128]{6,5,4,3,2,1,0:T(4,128)(2,1)} copy(bf16[1,1,32,2,16,4,128]{6,5,4,3,2,1,0:T(4,128)(2,1)} %bitcast.36) | data formatting | bytes 2097152
  (83 shorter events, 23.5 us)
Async XLA Ops:
  7.2 1.5 copy-start
  7.2 72.4 %all-gather.4.cloned.1.call-start = ((), (), s32[]{:S(2)}) async-start(), calls=%async_computation.1 | async-start | bytes 1966080 | tf_op jit(solution)/shard_map/all_gather | solution.py:579
  7.9 82.9 %all-gather.6.cloned.1.call-start = ((), (), s32[]{:S(2)}) async-start(), calls=%async_computation.2 | async-start | bytes 2621440 | tf_op jit(solution)/shard_map/all_gather | solution.py:582
  10.9 2.8 %copy-start.12 = (s32[1,32,1]{1,2,0:T(1,128)S(1)}, s32[1,32,1]{1,2,0:T(1,128)}, u32[]{:S(2)}) copy-start(s32[1,32,1]{1,2,0:T(1,128)} %param.25) | copy-start | bytes 388
  17.9 16.0 %copy-start.11 = (s32[1,128]{1,0:T(1,128)S(1)}, s32[1,128]{1,0:T(1,128)}, u32[]{:S(2)}) copy-start(s32[1,128]{1,0:T(1,128)} %param.24) | copy-start | bytes 1540
  17.9 17.6 %copy-start.2 = (s32[1,16384]{1,0:T(1,128)S(1)}, s32[1,16384]{1,0:T(1,128)}, u32[]{:S(2)}) copy-start(s32[1,16384]{1,0:T(1,128)} %param.23) | copy-start | bytes 196612
  17.9 49.4 %all-to-all-start = ((bf16[32,2,16,4,128]{4,3,2,1,0:T(4,128)(2,1)}), bf16[32,2,16,4,128]{4,3,2,1,0:T(4,128)(2,1)}, u32[]{:S(2)}, u32[]{:S(2)}) async-start(bf16[32,2,16,4,128]{4,3,2,1,0:T(4,128)(2,1)} %reshape.178), calls=%async_computation | async-start | bytes 2097152 | tf_op jit(solution)/shard_map/all_to_all | solution.py:612
  27.5 145.2 %all-gather.8.cloned.1.call-start = ((), (), s32[]{:S(2)}) async-start(), calls=%async_computation.3 | async-start | bytes 2621440 | tf_op jit(solution)/shard_map/all_gather | solution.py:583
  28.4 31.7 %collective-permute-start = (bf16[256,4,128]{0,2,1:T(8,128)(2,1)}, bf16[256,4,128]{0,2,1:T(8,128)(2,1)}, u32[]{:S(2)}, u32[]{:S(2)}) collective-permute-start(bf16[256,4,128]{0,2,1:T(8,128)(2,1)} %get-tuple-element.10), channel_id=1, source_target_pairs={{0,16},{16,32},{32,48},{48,64},{64,80},{80,96},{96,112},{112,128},... | collective-permute-start | bytes 786440 | tf_op jit(solution)/shard_map/ppermute | solution.py:21
  31.7 28.4 %collective-permute-start.1 = (bf16[256,4,128]{0,2,1:T(8,128)(2,1)}, bf16[256,4,128]{0,2,1:T(8,128)(2,1)}, u32[]{:S(2)}, u32[]{:S(2)}) collective-permute-start(bf16[256,4,128]{0,2,1:T(8,128)(2,1)} %get-tuple-element.11), channel_id=1, source_target_pairs={{16,0},{32,16},{48,32},{64,48},{80,64},{96,80},{112,96},{128,112},... | collective-permute-start | bytes 786440 | tf_op jit(solution)/shard_map/ppermute | solution.py:24
  60.1 1.4 copy-start.3
  61.5 1.0 copy-start.6
  67.3 2.9 %copy-start.4 = (pred[512,1024]{1,0:T(8,128)(4,1)S(1)}, pred[512,1024]{1,0:T(8,128)(4,1)}, u32[]{:S(2)}) copy-start(pred[512,1024]{1,0:T(8,128)(4,1)} %copy-done.3) | copy-start | bytes 1572868
  70.2 6.4 %copy-start.1 = (f32[4,512,1024]{2,1,0:T(8,128)S(1)}, f32[4,512,1024]{2,1,0:T(8,128)}, u32[]{:S(2)}) copy-start(f32[4,512,1024]{2,1,0:T(8,128)} %get-tuple-element.13) | copy-start | bytes 25165828
  70.2 6.4 %copy-start.7 = (bf16[1024,4,128]{0,2,1:T(8,128)(2,1)S(1)}, bf16[1024,4,128]{0,2,1:T(8,128)(2,1)}, u32[]{:S(2)}) copy-start(bf16[1024,4,128]{0,2,1:T(8,128)(2,1)} %copy-done.6) | copy-start | bytes 3145732
  79.6 3.0 %copy-start.5 = (bf16[1,512,1024]{2,1,0:T(8,128)(2,1)S(1)}, bf16[1,512,1024]{2,1,0:T(8,128)(2,1)}, u32[]{:S(2)}) copy-start(bf16[1,512,1024]{2,1,0:T(8,128)(2,1)} %param.13) | copy-start | bytes 3145732
  89.9 22.6 %copy-start.8 = (bf16[256,1024]{1,0:T(8,128)(2,1)S(1)}, bf16[256,1024]{1,0:T(8,128)(2,1)}, u32[]{:S(2)}) copy-start(bf16[256,1024]{1,0:T(8,128)(2,1)} %param.16) | copy-start | bytes 1572868
  183.1 41.0 %copy-start.9 = (f32[1024]{0:T(1024)S(1)}, f32[1024]{0:T(1024)}, u32[]{:S(2)}) copy-start(f32[1024]{0:T(1024)} %param.22) | copy-start | bytes 12292
  183.1 41.0 %copy-start.10 = (f32[1024]{0:T(1024)S(1)}, f32[1024]{0:T(1024)}, u32[]{:S(2)}) copy-start(f32[1024]{0:T(1024)} %param.21) | copy-start | bytes 12292
Sparse Core Ops, SparseCore 0:
  10.1 38.2 all-gather.3
  50.5 37.7 all-gather.5
  90.4 39.5 all-gather.7

commit v10 on v9

--- a/solution.py
+++ b/solution.py
@@ -525,6 +525,78 @@
         ],
         compiler_params=pltpu.CompilerParams(collective_id=7, has_side_effects=True),
     )(parts, own, gain.reshape(1, width), bias.reshape(1, width))
+
+
+def col_proj_kernel(x_ref, own_ref, w_ref, gain_ref, bias_ref, out_ref, got, rs_send, rs_recv, g_send, g_recv):
+    me, peers = col_peers()
+    m = len(peers) + 1
+    heads_width = x_ref.shape[2]
+    copies = []
+    for j, peer in enumerate(peers):
+        copy = pltpu.make_async_remote_copy(
+            src_ref=x_ref.at[peer[2]],
+            dst_ref=got.at[j],
+            send_sem=rs_send.at[j],
+            recv_sem=rs_recv.at[j],
+            device_id=peer,
+            device_id_type=MESH,
+        )
+        copy.start()
+        copies.append(copy)
+    for copy in copies:
+        copy.wait()
+    chunk = 32
+    width = out_ref.shape[2]
+
+    def body(i, carry):
+        rows = pl.ds(pl.multiple_of(i * chunk, chunk), chunk)
+        total = own_ref[rows, :]
+        for j in range(len(copies)):
+            source = lax.rem(me + m - 1 - j, m)
+            weights = w_ref[pl.ds(pl.multiple_of(source * heads_width, heads_width), heads_width), :]
+            total = total + jnp.dot(got[j, rows, :], weights, preferred_element_type=jnp.float32)
+        center = total - jnp.sum(total, axis=1, keepdims=True) / width
+        spread = jnp.sum(center * center, axis=1, keepdims=True) / width
+        normed = center / jnp.sqrt(spread + 1e-05) * gain_ref[...] + bias_ref[...]
+        out_ref[me, rows, :] = normed.astype(out_ref.dtype)
+        return carry
+
+    lax.fori_loop(0, out_ref.shape[1] // chunk, body, 0)
+    sends = []
+    for j, peer in enumerate(peers):
+        copy = pltpu.make_async_remote_copy(
+            src_ref=out_ref.at[me],
+            dst_ref=out_ref.at[me],
+            send_sem=g_send.at[j],
+            recv_sem=g_recv.at[j],
+            device_id=peer,
+            device_id_type=MESH,
+        )
+        copy.start()
+        sends.append(copy)
+    for copy in sends:
+        copy.wait()
+
+
+def col_proj_norm_gather(attn_parts, own, w_full, gain, bias):
+    m = lax.axis_size("col")
+    rows, width = own.shape
+    return pl.pallas_call(
+        col_proj_kernel,
+        out_shape=jax.ShapeDtypeStruct((m, rows, width), jnp.bfloat16),
+        in_specs=[pl.BlockSpec(memory_space=pltpu.VMEM)] * 5,
+        out_specs=pl.BlockSpec(memory_space=pltpu.VMEM),
+        scratch_shapes=[
+            pltpu.VMEM((m - 1,) + attn_parts.shape[1:], attn_parts.dtype),
+            pltpu.SemaphoreType.DMA((m - 1,)),
+            pltpu.SemaphoreType.DMA((m - 1,)),
+            pltpu.SemaphoreType.DMA((m - 1,)),
+            pltpu.SemaphoreType.DMA((m - 1,)),
+        ],
+        compiler_params=pltpu.CompilerParams(
+            collective_id=10, has_side_effects=True, vmem_limit_bytes=48 * 1024 * 1024
+        ),
+    )(attn_parts, own, w_full, gain.reshape(1, width), bias.reshape(1, width))
 
 
 def layer_norm(values, gain, bias):
@@ -581,6 +653,7 @@
     )
     f_in = lax.all_gather(ffn_in, "row", axis=0, tiled=True)
     f_out = lax.all_gather(ffn_out, "row", axis=1, tiled=True)
+    w_out = lax.all_gather(out_weight, "col", axis=0, tiled=True)
 
     flat_weight = qkv_weight.reshape(width, heads_here * triple)
     qkv = jnp.dot(tokens, flat_weight, preferred_element_type=jnp.float32).astype(jnp.bfloat16)
@@ -669,7 +742,7 @@
         axis=2,
     )
     packed = jnp.transpose(packed, (1, 0, 2)).reshape(n_glob * heads_here, 128)
-    packed, f_in = lax.optimization_barrier((packed, f_in))
+    packed, w_out = lax.optimization_barrier((packed, w_out))
     if group > 1:
         merged = seq_merge2(packed.reshape(n_seq, -1, 128), head_dim + 1, group)
     else:
@@ -717,12 +790,13 @@
 
 
     out_rows = shard_len // n_col
-    proj = jnp.dot(attention, out_weight, preferred_element_type=jnp.float32)
-    proj_own = lax.dynamic_slice_in_dim(proj, col_index * out_rows, out_rows, 0)
+    attn_own = lax.dynamic_slice_in_dim(attention, col_index * out_rows, out_rows, 0)
     token_own = lax.dynamic_slice_in_dim(tokens, col_index * out_rows, out_rows, 0)
-    middle_all = col_sum_norm_gather(
-        proj.astype(jnp.bfloat16).reshape(n_col, out_rows, width),
+    proj_own = jnp.dot(attn_own, out_weight, preferred_element_type=jnp.float32)
+    middle_all = col_proj_norm_gather(
+        attention.reshape(n_col, out_rows, heads_here * head_dim),
         token_own.astype(jnp.float32) + proj_own,
+        w_out,
         ln_gain,
         ln_bias,
     )

time: 237 us -> 246 us (1.038)
  the two profiles are of different devices: /device:TPU:43 before, /device:TPU:1 now
where the time goes in v10:
time: 246 us; the launch traced here: 242 us
  Pallas kernels  112 us (46%)
  matrix products  35.3 us (14%)
  waiting for transfers between devices  29.6 us (12%)
  local copies, waits for them, and re-layouts  18.9 us (8%)
  starting transfers between devices  17.1 us (7%)
  other arithmetic  15 us (6%)
  between operations  14.3 us (6%)
    pallas_call x1, Pallas kernels, col_proj_norm_gather(): pl.pallas_call(col_proj_kernel, out_shape=jax.ShapeDtypeStruct((m, rows,...  41 us
    pallas_call x1, Pallas kernels, col_reduce_scatter(): pl.pallas_call(col_sum_kernel, out_shape=jax.ShapeDtypeStruct(own.shape,...  27.9 us
    pallas_call x1, Pallas kernels, seq_gather2(): pl.pallas_call(functools.partial(seq_gather2_kernel, group), out_shape=ja...  23.7 us
    pallas_call x1, Pallas kernels, seq_merge2(): pl.pallas_call(functools.partial(seq_merge2_kernel, group, top_lane), out...  19.4 us
    all_gather x1, waiting for transfers between devices, per_device(): f_in = lax.all_gather(ffn_in, 'row', axis=0, tiled=True)  15 us
    all_gather x1, waiting for transfers between devices, per_device(): w_out = lax.all_gather(out_weight, 'col', axis=0, tiled=True)  12.5 us
    all_to_all x1, starting transfers between devices, per_device(): lax.all_to_all(outgoing, 'seq', split_axis=0, concat_axis=0, tiled=True)  11.3 us
    dot_general x1, matrix products, per_device(): ffn_full = jnp.dot(ffn_hidden, f_out, preferred_element_type=jnp.float32)  10.1 us
  transfers between devices with their start and end apart: 7, of which 2 were waited for; matrix products, arithmetic and copies ran while one was open for 20% of the time, Pallas kernels for 35%

profile of v10, /device:TPU:1, one launch (start us, length us, event | category | flops | bytes accessed | tf_op | source)
XLA Modules:
  0.0 242.0 jit_solution(13375061723983701061)
XLA Ops:
  9.4 2.2 convolution_convert_fusion.2
  13.1 1.4 reshape.174
  16.1 2.6 %reshape.175 = bf16[32,2,16,4,128]{4,3,2,1,0:T(4,128)(2,1)} reshape(bf16[64,8192]{1,0:T(8,128)(2,1)} %convolution_convert_fusion) | data formatting | bytes 2097152 | tf_op jit(solution)/shard_map/reshape | solution.py:684
  18.7 11.3 %all-to-all-start = ((bf16[32,2,16,4,128]{4,3,2,1,0:T(4,128)(2,1)}), bf16[32,2,16,4,128]{4,3,2,1,0:T(4,128)(2,1)}, u32[]{:S(2)}, u32[]{:S(2)}) async-start(bf16[32,2,16,4,128]{4,3,2,1,0:T(4,128)(2,1)} %reshape.175), calls=%async_computation | async-start | bytes 2097152 | tf_op jit(solution)/shard_map/all_to_all | solution.py:685
  30.8 3.5 %collective-permute-start = (bf16[256,4,128]{0,2,1:T(8,128)(2,1)}, bf16[256,4,128]{0,2,1:T(8,128)(2,1)}, u32[]{:S(2)}, u32[]{:S(2)}) collective-permute-start(bf16[256,4,128]{0,2,1:T(8,128)(2,1)} %get-tuple-element.10), channel_id=1, source_target_pairs={{0,16},{16,32},{32,48},{48,64},{64,80},{80,96},{96,112},{112,128},... | collective-permute-start | bytes 786440 | tf_op jit(solution)/shard_map/ppermute | solution.py:21
  34.4 2.1 collective-permute-start.1
  36.6 1.5 convolution_convert_fusion.6
  40.3 23.7 %shard_map.140 = bf16[32,32,128]{2,1,0:T(8,128)(2,1)} custom-call(bf16[32,128]{1,0:T(8,128)(2,1)} %reshape.176.x_ref), custom_call_target="tpu_custom_call" | custom-call | tf_op jit(solution)/shard_map/pallas_call | solution.py:290
  68.7 4.8 %select_reduce_fusion = (f32[4,512]{1,0:T(4,128)S(1)}, f32[4,512,1024]{2,1,0:T(8,128)}) fusion(pred[512,1024]{1,0:T(8,128)(4,1)S(1)} %fusion.15, bf16[1024,4,128]{0,2,1:T(8,128)(2,1)S(1)} %pad_maximum_fusion, bf16[512,4,192]{0,2,1:T(8,128)(2,1)S(1)} %bitcast.91), kind=kOutput, calls=%fused_computation.3 | convolution fusion | flops 274724864 | bytes 9707520 | tf_op jit(solution)/shard_map/qhd,khd->hqk/dot_general | solution.py:761
  76.3 5.0 %fusion = f32[4,512]{1,0:T(4,128)S(1)} fusion(f32[4,512,1024]{2,1,0:T(8,128)} %get-tuple-element.13, f32[4,512]{1,0:T(4,128)S(1)} %max.7, pred[512,1024]{1,0:T(8,128)(4,1)S(1)} %copy-done.7), kind=kLoop, calls=%fused_computation.4 | loop fusion | flops 8386560 | bytes 8929280 | tf_op jit(solution)/shard_map/reduce_sum | solution.py:774
  82.7 2.9 %fusion.62 = bf16[512,4,64]{0,2,1:T(8,128)(2,1)} fusion(f32[4,64,512]{2,1,0:T(8,128)S(1)} %fusion.69, f32[4,512,1024]{2,1,0:T(8,128)S(1)} %copy-done.4, f32[4,512]{1,0:T(4,128)S(1)} %max.7, pred[512,1024]{1,0:T(8,128)(4,1)S(1)} %copy-done.7, bf16[1024,4,128]{0,2,1:T(8,128)(2,1)S(1)} %copy-done.11, f32[512,4]{0,1:T(4,128)S(1)} %add_bitcast_fusion), kind=kOutput, calls=%fused_computation.82 | convolution fusion | flops 277217280 | bytes 10240000 | tf_op jit(solution)/shard_map/hqk,khd->qhd/dot_general | solution.py:775
  85.6 2.2 convolution_convert_fusion.5
  87.9 3.3 %convolution_convert_fusion.1 = bf16[512,768]{1,0:T(8,128)(2,1)} fusion(bf16[1024,768]{0,1:T(8,128)(2,1)} %all-gather.5.cloned.1.call-done, bf16[1,512,1024]{2,1,0:T(8,128)(2,1)S(1)} %copy-done.9), kind=kOutput, calls=%fused_computation.30 | convolution fusion | flops 805699584 | bytes 3407872 | tf_op jit(solution)/shard_map/dot_general | solution.py:703
  91.3 1.4 copy.43
  95.4 12.5 %all-gather.7.cloned.1.call-done.w_ref = bf16[1024,1024]{1,0:T(8,128)(2,1)} async-done(((bf16[256,1024]{1,0:T(8,128)(2,1)}), bf16[1024,1024]{1,0:T(8,128)(2,1)}) %all-gather.7.cloned.1.call-update) | async-done | bytes 2097168 | tf_op jit(solution)/shard_map/all_gather | solution.py:656
  107.9 19.4 %shard_map.141 = f32[16,128]{1,0:T(8,128)} custom-call(f32[32,16,128]{2,1,0:T(8,128)} %bitcast.94), custom_call_target="tpu_custom_call" | custom-call | tf_op jit(solution)/shard_map/pallas_call | solution.py:353
  130.8 1.6 copy-done.1
  132.3 41.0 %shard_map.142 = bf16[4,128,1024]{2,1,0:T(8,128)(2,1)S(1)} custom-call(bf16[4,128,256]{2,1,0:T(8,128)(2,1)S(1)} %copy.50.x_ref, f32[128,1024]{1,0:T(8,128)S(1)} %convolution_add_fusion.own_ref, bf16[1024,1024]{1,0:T(8,128)(2,1)S(1)} %copy-done.1, f32[1,1024]{1,0:T(1,128)S(1)} %bitcast.85, f32[1,1024]{1,0:T(1,128)S(1)} %bitcast.86), custom_call_target="tpu_custom_call" | custom-call | tf_op jit(solution)/shard_map/pallas_call | solution.py:584
  173.4 15.0 %all-gather.9.cloned.1.call-done = bf16[1024,1024]{1,0:T(8,128)(2,1)} async-done(((bf16[256,1024]{1,0:T(8,128)(2,1)}), bf16[1024,1024]{1,0:T(8,128)(2,1)}) %all-gather.9.cloned.1.call-update) | async-done | bytes 2097168 | tf_op jit(solution)/shard_map/all_gather | solution.py:654
  188.3 10.1 %fusion.139 = (bf16[512,1024]{1,0:T(8,128)(2,1)}, f32[512,1024]{1,0:T(8,128)}) fusion(bf16[1024,1024]{1,0:T(8,128)(2,1)} %all-gather.11.cloned.1.call-done, bf16[512,1024]{1,0:T(8,128)(2,1)S(1)} %bitcast.84, bf16[1024,1024]{1,0:T(8,128)(2,1)} %all-gather.9.cloned.1.call-done), kind=kOutput, calls=%fused_computation.181 | convolution fusion | flops 2182086656 | bytes 8388608 | tf_op jit(solution)/shard_map/dot_general | solution.py:807
  198.5 2.0 convert_add_fusion.own_ref
  200.4 27.9 %shard_map.143 = f32[128,1024]{1,0:T(8,128)} custom-call(bf16[4,128,1024]{2,1,0:T(8,128)(2,1)} %bitcast.93, f32[128,1024]{1,0:T(8,128)} %convert_add_fusion.own_ref), custom_call_target="tpu_custom_call" | custom-call | tf_op jit(solution)/shard_map/pallas_call | solution.py:450
  230.7 1.9 fusion.80
  232.6 2.8 %copy.62 = bf16[1,1,32,2,16,4,128]{6,5,4,3,2,1,0:T(4,128)(2,1)} copy(bf16[1,1,32,2,16,4,128]{6,5,4,3,2,1,0:T(4,128)(2,1)} %bitcast.35) | data formatting | bytes 2097152
  (95 shorter events, 25.7 us)
Async XLA Ops:
  7.2 2.2 copy-start
  7.2 78.4 %all-gather.5.cloned.1.call-start = ((), (), s32[]{:S(2)}) async-start(), calls=%async_computation.1 | async-start | bytes 1966080 | tf_op jit(solution)/shard_map/all_gather | solution.py:651
  7.9 100.0 %all-gather.7.cloned.1.call-start = ((), (), s32[]{:S(2)}) async-start(), calls=%async_computation.2 | async-start | bytes 2621440 | tf_op jit(solution)/shard_map/all_gather | solution.py:656
  8.7 164.7 %all-gather.11.cloned.1.call-start = ((), (), s32[]{:S(2)}) async-start(), calls=%async_computation.4 | async-start | bytes 2621440 | tf_op jit(solution)/shard_map/all_gather | solution.py:655
  11.7 2.8 %copy-start.15 = (s32[1,32,1]{1,2,0:T(1,128)S(1)}, s32[1,32,1]{1,2,0:T(1,128)}, u32[]{:S(2)}) copy-start(s32[1,32,1]{1,2,0:T(1,128)} %param.25) | copy-start | bytes 388
  18.7 17.8 %copy-start.14 = (s32[1,128]{1,0:T(1,128)S(1)}, s32[1,128]{1,0:T(1,128)}, u32[]{:S(2)}) copy-start(s32[1,128]{1,0:T(1,128)} %param.24) | copy-start | bytes 1540
  18.7 19.5 %copy-start.5 = (s32[1,16384]{1,0:T(1,128)S(1)}, s32[1,16384]{1,0:T(1,128)}, u32[]{:S(2)}) copy-start(s32[1,16384]{1,0:T(1,128)} %param.23) | copy-start | bytes 196612
  18.7 54.8 %all-to-all-start = ((bf16[32,2,16,4,128]{4,3,2,1,0:T(4,128)(2,1)}), bf16[32,2,16,4,128]{4,3,2,1,0:T(4,128)(2,1)}, u32[]{:S(2)}, u32[]{:S(2)}) async-start(bf16[32,2,16,4,128]{4,3,2,1,0:T(4,128)(2,1)} %reshape.175), calls=%async_computation | async-start | bytes 2097152 | tf_op jit(solution)/shard_map/all_to_all | solution.py:685
  29.9 158.4 %all-gather.9.cloned.1.call-start = ((), (), s32[]{:S(2)}) async-start(), calls=%async_computation.3 | async-start | bytes 2621440 | tf_op jit(solution)/shard_map/all_gather | solution.py:654
  30.8 35.5 %collective-permute-start = (bf16[256,4,128]{0,2,1:T(8,128)(2,1)}, bf16[256,4,128]{0,2,1:T(8,128)(2,1)}, u32[]{:S(2)}, u32[]{:S(2)}) collective-permute-start(bf16[256,4,128]{0,2,1:T(8,128)(2,1)} %get-tuple-element.10), channel_id=1, source_target_pairs={{0,16},{16,32},{32,48},{48,64},{64,80},{80,96},{96,112},{112,128},... | collective-permute-start | bytes 786440 | tf_op jit(solution)/shard_map/ppermute | solution.py:21
  34.4 32.0 %collective-permute-start.1 = (bf16[256,4,128]{0,2,1:T(8,128)(2,1)}, bf16[256,4,128]{0,2,1:T(8,128)(2,1)}, u32[]{:S(2)}, u32[]{:S(2)}) collective-permute-start(bf16[256,4,128]{0,2,1:T(8,128)(2,1)} %get-tuple-element.11), channel_id=1, source_target_pairs={{16,0},{32,16},{48,32},{64,48},{80,64},{96,80},{112,96},{128,112},... | collective-permute-start | bytes 786440 | tf_op jit(solution)/shard_map/ppermute | solution.py:24
  66.3 1.4 copy-start.6
  67.7 1.0 copy-start.10
  73.5 2.7 %copy-start.7 = (pred[512,1024]{1,0:T(8,128)(4,1)S(1)}, pred[512,1024]{1,0:T(8,128)(4,1)}, u32[]{:S(2)}) copy-start(pred[512,1024]{1,0:T(8,128)(4,1)} %copy-done.6) | copy-start | bytes 1572868
  76.2 6.4 %copy-start.4 = (f32[4,512,1024]{2,1,0:T(8,128)S(1)}, f32[4,512,1024]{2,1,0:T(8,128)}, u32[]{:S(2)}) copy-start(f32[4,512,1024]{2,1,0:T(8,128)} %get-tuple-element.13) | copy-start | bytes 25165828
  81.2 1.5 copy-start.11
  85.6 2.3 copy-start.9
  93.1 35.1 %copy-start.16 = (bf16[512,4,64]{0,2,1:T(8,128)(2,1)S(1)}, bf16[512,4,64]{0,2,1:T(8,128)(2,1)}, u32[]{:S(2)}) copy-start(bf16[512,4,64]{0,2,1:T(8,128)(2,1)} %fusion.62) | copy-start | bytes 786436
  93.5 36.0 %copy-start.8 = (bf16[256,1024]{1,0:T(8,128)(2,1)S(1)}, bf16[256,1024]{1,0:T(8,128)(2,1)}, u32[]{:S(2)}) copy-start(bf16[256,1024]{1,0:T(8,128)(2,1)} %param.16) | copy-start | bytes 1572868
  94.5 36.2 %copy-start.2 = (f32[1024]{0:T(1024)S(1)}, f32[1024]{0:T(1024)}, u32[]{:S(2)}) copy-start(f32[1024]{0:T(1024)} %param.17) | copy-start | bytes 12292
  94.5 36.2 %copy-start.3 = (f32[1024]{0:T(1024)S(1)}, f32[1024]{0:T(1024)}, u32[]{:S(2)}) copy-start(f32[1024]{0:T(1024)} %param.18) | copy-start | bytes 12292
  130.7 1.6 copy-start.1
  198.5 32.2 %copy-start.12 = (f32[1024]{0:T(1024)S(1)}, f32[1024]{0:T(1024)}, u32[]{:S(2)}) copy-start(f32[1024]{0:T(1024)} %param.22) | copy-start | bytes 12292
  198.5 32.3 %copy-start.13 = (f32[1024]{0:T(1024)S(1)}, f32[1024]{0:T(1024)}, u32[]{:S(2)}) copy-start(f32[1024]{0:T(1024)} %param.21) | copy-start | bytes 12292
Sparse Core Ops, SparseCore 0:
  10.1 40.1 all-gather.4
  52.4 55.4 all-gather.6
  110.0 38.2 all-gather.10
  150.2 38.0 all-gather.8

commit v11 on v10

--- a/solution.py
+++ b/solution.py
@@ -648,10 +648,17 @@
     else:
         glob_rows = seq_direct_gather(own_rows.reshape(-1, 128)).reshape(n_glob, width)
 
-    w_global = lax.all_gather(
-        qkv_global_weight.reshape(qkv_global_weight.shape[0], -1), "row", axis=0, tiled=True
-    )
-    f_in = lax.all_gather(ffn_in, "row", axis=0, tiled=True)
+    wg_cols = qkv_global_weight.shape[1] * qkv_global_weight.shape[2]
+    wg_fin = lax.all_gather(
+        jnp.concatenate(
+            [qkv_global_weight.reshape(qkv_global_weight.shape[0], wg_cols), ffn_in], axis=1
+        ),
+        "row",
+        axis=0,
+        tiled=True,
+    )
+    w_global = wg_fin[:, :wg_cols]
+    f_in = wg_fin[:, wg_cols:]
     f_out = lax.all_gather(ffn_out, "row", axis=1, tiled=True)
     w_out = lax.all_gather(out_weight, "col", axis=0, tiled=True)
 
@@ -742,7 +749,6 @@
         axis=2,
     )
     packed = jnp.transpose(packed, (1, 0, 2)).reshape(n_glob * heads_here, 128)
-    packed, w_out = lax.optimization_barrier((packed, w_out))
     if group > 1:
         merged = seq_merge2(packed.reshape(n_seq, -1, 128), head_dim + 1, group)
     else:
@@ -790,6 +796,7 @@
 
 
     out_rows = shard_len // n_col
+    attention, w_out = lax.optimization_barrier((attention, w_out))
     attn_own = lax.dynamic_slice_in_dim(attention, col_index * out_rows, out_rows, 0)
     token_own = lax.dynamic_slice_in_dim(tokens, col_index * out_rows, out_rows, 0)
     proj_own = jnp.dot(attn_own, out_weight, preferred_element_type=jnp.float32)

time: 246 us -> 222 us (0.902); the launches traced: 242 us -> 221 us
  waiting for transfers between devices: 29.6 us -> 7.22 us
    all_gather x2 -> x1, waiting for transfers between devices: 15 us -> 0.01 us  [per_device(): lax.all_gather(jnp.concatenate([qkv_global_weight.reshape(qkv_global_weig...]
    all_gather x1, waiting for transfers between devices: 12.5 us -> 6.46 us  [per_device(): w_out = lax.all_gather(out_weight, 'col', axis=0, tiled=True)]
    pallas_call x1, Pallas kernels: 27.9 us -> 32.6 us  [col_reduce_scatter(): pl.pallas_call(col_sum_kernel, out_shape=jax.ShapeDtypeStruct(own.shape,...]
    pallas_call x1, Pallas kernels: 41 us -> 36.4 us  [col_proj_norm_gather(): pl.pallas_call(col_proj_kernel, out_shape=jax.ShapeDtypeStruct((m, rows,...]
    unnamed x35 -> x41, local copies, waits for them, and re-layouts: 5.47 us -> 5.49 us
  transfers between devices with their start and end apart: 7 -> 6, of which waited for: 2 -> 1; matrix products, arithmetic and copies ran while one was open for 20% -> 20% of each run, Pallas kernels for 35% -> 36%
where the time goes in v11:
time: 222 us; the launch traced here: 221 us
  Pallas kernels  113 us (51%)
  matrix products  33.1 us (15%)
  local copies, waits for them, and re-layouts  19.4 us (9%)
  other arithmetic  17.4 us (8%)
  starting transfers between devices  17.1 us (8%)
  between operations  14.3 us (6%)
  waiting for transfers between devices  7.22 us (3%)
    pallas_call x1, Pallas kernels, col_proj_norm_gather(): pl.pallas_call(col_proj_kernel, out_shape=jax.ShapeDtypeStruct((m, rows,...  36.4 us
    pallas_call x1, Pallas kernels, col_reduce_scatter(): pl.pallas_call(col_sum_kernel, out_shape=jax.ShapeDtypeStruct(own.shape,...  32.6 us
    pallas_call x1, Pallas kernels, seq_gather2(): pl.pallas_call(functools.partial(seq_gather2_kernel, group), out_shape=ja...  23.5 us
    pallas_call x1, Pallas kernels, seq_merge2(): pl.pallas_call(functools.partial(seq_merge2_kernel, group, top_lane), out...  20.1 us
    all_to_all x1, starting transfers between devices, per_device(): lax.all_to_all(outgoing, 'seq', split_axis=0, concat_axis=0, tiled=True)  11.3 us
    dot_general x1, matrix products, per_device(): ffn_full = jnp.dot(ffn_hidden, f_out, preferred_element_type=jnp.float32)  10.1 us
    all_gather x1, waiting for transfers between devices, per_device(): w_out = lax.all_gather(out_weight, 'col', axis=0, tiled=True)  6.46 us
    unnamed x41, local copies, waits for them, and re-layouts  5.49 us
  transfers between devices with their start and end apart: 6, of which 1 were waited for; matrix products, arithmetic and copies ran while one was open for 20% of the time, Pallas kernels for 36%

profile of v11, /device:TPU:1, one launch (start us, length us, event | category | flops | bytes accessed | tf_op | source)
XLA Modules:
  0.0 221.0 jit_solution(14514107216116561544)
XLA Ops:
  8.6 2.0 pad_maximum_fusion.1
  13.8 1.4 reshape.171
  16.8 2.6 %reshape.172 = bf16[32,2,16,4,128]{4,3,2,1,0:T(4,128)(2,1)} reshape(bf16[64,8192]{1,0:T(8,128)(2,1)} %convolution_convert_fusion) | data formatting | bytes 2097152 | tf_op jit(solution)/shard_map/reshape | solution.py:691
  19.4 11.3 %all-to-all-start = ((bf16[32,2,16,4,128]{4,3,2,1,0:T(4,128)(2,1)}), bf16[32,2,16,4,128]{4,3,2,1,0:T(4,128)(2,1)}, u32[]{:S(2)}, u32[]{:S(2)}) async-start(bf16[32,2,16,4,128]{4,3,2,1,0:T(4,128)(2,1)} %reshape.172), calls=%async_computation | async-start | bytes 2097152 | tf_op jit(solution)/shard_map/all_to_all | solution.py:692
  31.6 2.3 %collective-permute-start.1 = (bf16[256,4,128]{0,2,1:T(8,128)(2,1)}, bf16[256,4,128]{0,2,1:T(8,128)(2,1)}, u32[]{:S(2)}, u32[]{:S(2)}) collective-permute-start(bf16[256,4,128]{0,2,1:T(8,128)(2,1)} %get-tuple-element.11), channel_id=1, source_target_pairs={{16,0},{32,16},{48,32},{64,48},{80,64},{96,80},{112,96},{128,112},... | collective-permute-start | bytes 786440 | tf_op jit(solution)/shard_map/ppermute | solution.py:24
  33.9 3.4 %collective-permute-start = (bf16[256,4,128]{0,2,1:T(8,128)(2,1)}, bf16[256,4,128]{0,2,1:T(8,128)(2,1)}, u32[]{:S(2)}, u32[]{:S(2)}) collective-permute-start(bf16[256,4,128]{0,2,1:T(8,128)(2,1)} %get-tuple-element.10), channel_id=1, source_target_pairs={{0,16},{16,32},{32,48},{48,64},{64,80},{80,96},{96,112},{112,128},... | collective-permute-start | bytes 786440 | tf_op jit(solution)/shard_map/ppermute | solution.py:21
  37.5 1.5 convolution_convert_fusion.5
  41.2 23.5 %shard_map.140 = bf16[32,32,128]{2,1,0:T(8,128)(2,1)} custom-call(bf16[32,128]{1,0:T(8,128)(2,1)} %reshape.173.x_ref), custom_call_target="tpu_custom_call" | custom-call | tf_op jit(solution)/shard_map/pallas_call | solution.py:290
  64.8 1.8 reshape.174
  70.5 4.8 %select_reduce_fusion = (f32[4,512]{1,0:T(4,128)S(1)}, f32[4,512,1024]{2,1,0:T(8,128)}) fusion(pred[512,1024]{1,0:T(8,128)(4,1)S(1)} %fusion.17, bf16[1024,4,128]{0,2,1:T(8,128)(2,1)S(1)} %pad_maximum_fusion, bf16[512,4,192]{0,2,1:T(8,128)(2,1)S(1)} %bitcast.89), kind=kOutput, calls=%fused_computation.3 | convolution fusion | flops 274724864 | bytes 9707520 | tf_op jit(solution)/shard_map/qhd,khd->hqk/dot_general | solution.py:767
  78.0 5.0 %fusion = f32[4,512]{1,0:T(4,128)S(1)} fusion(f32[4,512,1024]{2,1,0:T(8,128)} %get-tuple-element.13, f32[4,512]{1,0:T(4,128)S(1)} %max.7, pred[512,1024]{1,0:T(8,128)(4,1)S(1)} %fusion.17), kind=kLoop, calls=%fused_computation.4 | loop fusion | flops 8386560 | bytes 8929280 | tf_op jit(solution)/shard_map/reduce_sum | solution.py:780
  83.2 1.5 fusion.81
  84.7 2.9 %fusion.70 = bf16[512,4,64]{0,2,1:T(8,128)(2,1)} fusion(f32[4,64,512]{2,1,0:T(8,128)S(1)} %fusion.81, f32[4,512,1024]{2,1,0:T(8,128)S(1)} %copy-done.4, f32[4,512]{1,0:T(4,128)S(1)} %max.7, pred[512,1024]{1,0:T(8,128)(4,1)S(1)} %fusion.17, bf16[1024,4,128]{0,2,1:T(8,128)(2,1)S(1)} %copy-done.10, f32[512,4]{0,1:T(4,128)S(1)} %add_bitcast_fusion), kind=kOutput, calls=%fused_computation.87 | convolution fusion | flops 277217280 | bytes 10240000 | tf_op jit(solution)/shard_map/hqk,khd->qhd/dot_general | solution.py:781
  87.6 1.9 fusion.28
  89.7 2.4 %convolution_convert_fusion.1 = bf16[768,512]{1,0:T(8,128)(2,1)S(1)} fusion(bf16[1024,1792]{1,0:T(8,128)(2,1)} %all-gather.4.cloned.1.call-done, bf16[1,512,1024]{2,1,0:T(8,128)(2,1)S(1)} %copy-done.8), kind=kOutput, calls=%fused_computation.32 | convolution fusion | flops 805699584 | bytes 3407872 | tf_op jit(solution)/shard_map/dot_general | solution.py:710
  94.8 20.1 %shard_map.141 = f32[16,128]{1,0:T(8,128)} custom-call(f32[32,16,128]{2,1,0:T(8,128)} %bitcast.92), custom_call_target="tpu_custom_call" | custom-call | tf_op jit(solution)/shard_map/pallas_call | solution.py:353
  116.8 6.5 %all-gather.6.cloned.1.call-done.w_ref = bf16[1024,1024]{1,0:T(8,128)(2,1)} async-done(((bf16[256,1024]{1,0:T(8,128)(2,1)}), bf16[1024,1024]{1,0:T(8,128)(2,1)}) %all-gather.6.cloned.1.call-update) | async-done | bytes 2097168 | tf_op jit(solution)/shard_map/all_gather | solution.py:663
  124.7 1.6 copy-done.1
  126.3 36.4 %shard_map.142 = bf16[4,128,1024]{2,1,0:T(8,128)(2,1)S(1)} custom-call(bf16[4,128,256]{2,1,0:T(8,128)(2,1)S(1)} %bitcast.82, f32[128,1024]{1,0:T(8,128)S(1)} %convolution_add_fusion.own_ref, bf16[1024,1024]{1,0:T(8,128)(2,1)S(1)} %copy-done.1, f32[1,1024]{1,0:T(1,128)S(1)} %bitcast.83, f32[1,1024]{1,0:T(1,128)S(1)} %bitcast.84), custom_call_target="tpu_custom_call" | custom-call | tf_op jit(solution)/shard_map/pallas_call | solution.py:584
  162.6 10.1 %fusion.151 = (bf16[512,1024]{1,0:T(8,128)(2,1)}, f32[512,1024]{1,0:T(8,128)}) fusion(bf16[1024,1024]{1,0:T(8,128)(2,1)} %all-gather.8.cloned.1.call-done, bf16[512,1024]{1,0:T(8,128)(2,1)S(1)} %bitcast.81, bf16[1024,1792]{1,0:T(8,128)(2,1)} %all-gather.4.cloned.1.call-done), kind=kOutput, calls=%fused_computation.187 | convolution fusion | flops 2182086656 | bytes 8388608 | tf_op jit(solution)/shard_map/dot_general | solution.py:814
  172.8 1.9 convert_add_fusion.own_ref
  174.7 32.6 %shard_map.143 = f32[128,1024]{1,0:T(8,128)} custom-call(bf16[4,128,1024]{2,1,0:T(8,128)(2,1)} %bitcast.91, f32[128,1024]{1,0:T(8,128)} %convert_add_fusion.own_ref), custom_call_target="tpu_custom_call" | custom-call | tf_op jit(solution)/shard_map/pallas_call | solution.py:450
  209.7 1.9 fusion.92
  211.6 2.8 %copy.62 = bf16[1,1,32,2,16,4,128]{6,5,4,3,2,1,0:T(4,128)(2,1)} copy(bf16[1,1,32,2,16,4,128]{6,5,4,3,2,1,0:T(4,128)(2,1)} %bitcast.37) | data formatting | bytes 2097152
  (98 shorter events, 24.6 us)
Async XLA Ops:
  7.2 4.2 %copy-start = (bf16[1024,4,192]{0,2,1:T(8,128)(2,1)S(1)}, bf16[1024,4,192]{0,2,1:T(8,128)(2,1)}, u32[]{:S(2)}) copy-start(bf16[1024,4,192]{0,2,1:T(8,128)(2,1)} %param.14) | copy-start | bytes 4718596
  7.2 4.2 %copy-start.7 = (bf16[1,512,1024]{2,1,0:T(8,128)(2,1)S(1)}, bf16[1,512,1024]{2,1,0:T(8,128)(2,1)}, u32[]{:S(2)}) copy-start(bf16[1,512,1024]{2,1,0:T(8,128)(2,1)} %param.13) | copy-start | bytes 3145732
  7.2 80.4 %all-gather.4.cloned.1.call-start = ((), (), s32[]{:S(2)}) async-start(), calls=%async_computation.1 | async-start | bytes 4587520 | tf_op jit(solution)/shard_map/all_gather | solution.py:652
  10.6 112.7 %all-gather.6.cloned.1.call-start = ((), (), s32[]{:S(2)}) async-start(), calls=%async_computation.2 | async-start | bytes 2621440 | tf_op jit(solution)/shard_map/all_gather | solution.py:663
  12.4 2.8 %copy-start.17 = (s32[1,32,1]{1,2,0:T(1,128)S(1)}, s32[1,32,1]{1,2,0:T(1,128)}, u32[]{:S(2)}) copy-start(s32[1,32,1]{1,2,0:T(1,128)} %param.25) | copy-start | bytes 388
  19.4 17.9 %copy-start.16 = (s32[1,128]{1,0:T(1,128)S(1)}, s32[1,128]{1,0:T(1,128)}, u32[]{:S(2)}) copy-start(s32[1,128]{1,0:T(1,128)} %param.24) | copy-start | bytes 1540
  19.4 19.6 %copy-start.5 = (s32[1,16384]{1,0:T(1,128)S(1)}, s32[1,16384]{1,0:T(1,128)}, u32[]{:S(2)}) copy-start(s32[1,16384]{1,0:T(1,128)} %param.23) | copy-start | bytes 196612
  19.4 55.9 %all-to-all-start = ((bf16[32,2,16,4,128]{4,3,2,1,0:T(4,128)(2,1)}), bf16[32,2,16,4,128]{4,3,2,1,0:T(4,128)(2,1)}, u32[]{:S(2)}, u32[]{:S(2)}) async-start(bf16[32,2,16,4,128]{4,3,2,1,0:T(4,128)(2,1)} %reshape.172), calls=%async_computation | async-start | bytes 2097152 | tf_op jit(solution)/shard_map/all_to_all | solution.py:692
  30.7 131.9 %all-gather.8.cloned.1.call-start = ((), (), s32[]{:S(2)}) async-start(), calls=%async_computation.3 | async-start | bytes 2621440 | tf_op jit(solution)/shard_map/all_gather | solution.py:662
  31.6 36.7 %collective-permute-start.1 = (bf16[256,4,128]{0,2,1:T(8,128)(2,1)}, bf16[256,4,128]{0,2,1:T(8,128)(2,1)}, u32[]{:S(2)}, u32[]{:S(2)}) collective-permute-start(bf16[256,4,128]{0,2,1:T(8,128)(2,1)} %get-tuple-element.11), channel_id=1, source_target_pairs={{16,0},{32,16},{48,32},{64,48},{80,64},{96,80},{112,96},{128,112},... | collective-permute-start | bytes 786440 | tf_op jit(solution)/shard_map/ppermute | solution.py:24
  33.9 34.4 %collective-permute-start = (bf16[256,4,128]{0,2,1:T(8,128)(2,1)}, bf16[256,4,128]{0,2,1:T(8,128)(2,1)}, u32[]{:S(2)}, u32[]{:S(2)}) collective-permute-start(bf16[256,4,128]{0,2,1:T(8,128)(2,1)} %get-tuple-element.10), channel_id=1, source_target_pairs={{0,16},{16,32},{32,48},{48,64},{64,80},{80,96},{96,112},{112,128},... | collective-permute-start | bytes 786440 | tf_op jit(solution)/shard_map/ppermute | solution.py:21
  37.5 30.0 %copy-start.14 = (s32[4]{0:T(128)}, s32[4]{0:T(128)S(1)}, u32[]{:S(2)}) copy-start(s32[4]{0:T(128)S(1)} %fusion.113) | copy-start | bytes 52
  70.5 4.8 %copy-start.11 = (bf16[128,1024]{1,0:T(8,128)(2,1)S(1)}, bf16[128,1024]{1,0:T(8,128)(2,1)}, u32[]{:S(2)}) copy-start(bf16[128,1024]{1,0:T(8,128)(2,1)} %reshape.174) | copy-start | bytes 786436
  78.0 6.7 %copy-start.4 = (f32[4,512,1024]{2,1,0:T(8,128)S(1)}, f32[4,512,1024]{2,1,0:T(8,128)}, u32[]{:S(2)}) copy-start(f32[4,512,1024]{2,1,0:T(8,128)} %get-tuple-element.13) | copy-start | bytes 25165828
  83.0 1.7 copy-start.10
  87.6 2.0 copy-start.8
  92.5 23.2 %copy-start.15 = (s32[4]{0:T(128)S(1)}, s32[4]{0:T(128)}, u32[]{:S(2)}) copy-start(s32[4]{0:T(128)} %copy-done.14) | copy-start | bytes 52
  92.6 23.2 %copy-start.18 = (pred[512]{0:T(512)(128)(4,1)S(1)}, pred[512]{0:T(512)(128)(4,1)}, u32[]{:S(2)}) copy-start(pred[512]{0:T(512)(128)(4,1)} %fusion.104) | copy-start | bytes 1540
  92.6 23.2 %copy-start.19 = (bf16[512,4,64]{0,2,1:T(8,128)(2,1)S(1)}, bf16[512,4,64]{0,2,1:T(8,128)(2,1)}, u32[]{:S(2)}) copy-start(bf16[512,4,64]{0,2,1:T(8,128)(2,1)} %fusion.70) | copy-start | bytes 786436
  92.9 30.5 %copy-start.6 = (bf16[256,1024]{1,0:T(8,128)(2,1)S(1)}, bf16[256,1024]{1,0:T(8,128)(2,1)}, u32[]{:S(2)}) copy-start(bf16[256,1024]{1,0:T(8,128)(2,1)} %param.16) | copy-start | bytes 1572868
  93.9 30.7 %copy-start.2 = (f32[1024]{0:T(1024)S(1)}, f32[1024]{0:T(1024)}, u32[]{:S(2)}) copy-start(f32[1024]{0:T(1024)} %param.17) | copy-start | bytes 12292
  93.9 30.7 %copy-start.3 = (f32[1024]{0:T(1024)S(1)}, f32[1024]{0:T(1024)}, u32[]{:S(2)}) copy-start(f32[1024]{0:T(1024)} %param.18) | copy-start | bytes 12292
  172.8 36.9 %copy-start.12 = (f32[1024]{0:T(1024)S(1)}, f32[1024]{0:T(1024)}, u32[]{:S(2)}) copy-start(f32[1024]{0:T(1024)} %param.22) | copy-start | bytes 12292
  172.8 36.9 %copy-start.13 = (f32[1024]{0:T(1024)S(1)}, f32[1024]{0:T(1024)}, u32[]{:S(2)}) copy-start(f32[1024]{0:T(1024)} %param.21) | copy-start | bytes 12292
  (2 other events, 2.6 us)
Sparse Core Ops, SparseCore 0:
  10.7 54.7 all-gather.3
  67.6 55.6 all-gather.5
  125.4 36.7 all-gather.7

commit v12 on v11

--- a/solution.py
+++ b/solution.py
@@ -796,13 +796,13 @@
 
 
     out_rows = shard_len // n_col
-    attention, w_out = lax.optimization_barrier((attention, w_out))
     attn_own = lax.dynamic_slice_in_dim(attention, col_index * out_rows, out_rows, 0)
     token_own = lax.dynamic_slice_in_dim(tokens, col_index * out_rows, out_rows, 0)
     proj_own = jnp.dot(attn_own, out_weight, preferred_element_type=jnp.float32)
+    own_sum, w_out = lax.optimization_barrier((token_own.astype(jnp.float32) + proj_own, w_out))
     middle_all = col_proj_norm_gather(
         attention.reshape(n_col, out_rows, heads_here * head_dim),
-        token_own.astype(jnp.float32) + proj_own,
+        own_sum,
         w_out,
         ln_gain,
         ln_bias,

time: 222 us -> 221 us (level)
  the two profiles are of different devices: /device:TPU:1 before, /device:TPU:12 now
where the time goes in v12:
time: 221 us; the launch traced here: 219 us
  Pallas kernels  111 us (50%)
  matrix products  33.1 us (15%)
  local copies, waits for them, and re-layouts  19.5 us (9%)
  other arithmetic  17.6 us (8%)
  starting transfers between devices  15 us (7%)
  between operations  14.2 us (6%)
  waiting for transfers between devices  8.73 us (4%)
    pallas_call x1, Pallas kernels, col_proj_norm_gather(): pl.pallas_call(col_proj_kernel, out_shape=jax.ShapeDtypeStruct((m, rows,...  36.6 us
    pallas_call x1, Pallas kernels, col_reduce_scatter(): pl.pallas_call(col_sum_kernel, out_shape=jax.ShapeDtypeStruct(own.shape,...  32.1 us
    pallas_call x1, Pallas kernels, seq_gather2(): pl.pallas_call(functools.partial(seq_gather2_kernel, group), out_shape=ja...  26.1 us
    pallas_call x1, Pallas kernels, seq_merge2(): pl.pallas_call(functools.partial(seq_merge2_kernel, group, top_lane), out...  16.5 us
    dot_general x1, matrix products, per_device(): ffn_full = jnp.dot(ffn_hidden, f_out, preferred_element_type=jnp.float32)  10.1 us
    all_to_all x1, starting transfers between devices, per_device(): lax.all_to_all(outgoing, 'seq', split_axis=0, concat_axis=0, tiled=True)  9.7 us
    all_gather x1, waiting for transfers between devices, per_device(): w_out = lax.all_gather(out_weight, 'col', axis=0, tiled=True)  6.85 us
    unnamed x41, local copies, waits for them, and re-layouts  5.5 us
  transfers between devices with their start and end apart: 6, of which 2 were waited for; matrix products, arithmetic and copies ran while one was open for 20% of the time, Pallas kernels for 36%

profile of v12, /device:TPU:12, one launch (start us, length us, event | category | flops | bytes accessed | tf_op | source)
XLA Modules:
  0.0 219.5 jit_solution(6043801771046387683)
XLA Ops:
  8.6 2.0 pad_maximum_fusion.1
  13.8 1.4 reshape.168
  16.8 2.6 %reshape.169 = bf16[32,2,16,4,128]{4,3,2,1,0:T(4,128)(2,1)} reshape(bf16[64,8192]{1,0:T(8,128)(2,1)} %convolution_convert_fusion) | data formatting | bytes 2097152 | tf_op jit(solution)/shard_map/reshape | solution.py:691
  19.4 9.7 %all-to-all-start = ((bf16[32,2,16,4,128]{4,3,2,1,0:T(4,128)(2,1)}), bf16[32,2,16,4,128]{4,3,2,1,0:T(4,128)(2,1)}, u32[]{:S(2)}, u32[]{:S(2)}) async-start(bf16[32,2,16,4,128]{4,3,2,1,0:T(4,128)(2,1)} %reshape.169), calls=%async_computation | async-start | bytes 2097152 | tf_op jit(solution)/shard_map/all_to_all | solution.py:692
  30.0 3.1 %collective-permute-start.1 = (bf16[256,4,128]{0,2,1:T(8,128)(2,1)}, bf16[256,4,128]{0,2,1:T(8,128)(2,1)}, u32[]{:S(2)}, u32[]{:S(2)}) collective-permute-start(bf16[256,4,128]{0,2,1:T(8,128)(2,1)} %get-tuple-element.11), channel_id=1, source_target_pairs={{16,0},{32,16},{48,32},{64,48},{80,64},{96,80},{112,96},{128,112},... | collective-permute-start | bytes 786440 | tf_op jit(solution)/shard_map/ppermute | solution.py:24
  33.1 2.1 collective-permute-start
  35.4 1.5 convolution_convert_fusion.5
  39.1 26.1 %shard_map.140 = bf16[32,32,128]{2,1,0:T(8,128)(2,1)} custom-call(bf16[32,128]{1,0:T(8,128)(2,1)} %reshape.170.x_ref), custom_call_target="tpu_custom_call" | custom-call | tf_op jit(solution)/shard_map/pallas_call | solution.py:290
  65.3 1.8 reshape.171
  71.0 4.8 %select_reduce_fusion = (f32[4,512]{1,0:T(4,128)S(1)}, f32[4,512,1024]{2,1,0:T(8,128)}) fusion(pred[512,1024]{1,0:T(8,128)(4,1)S(1)} %fusion.17, bf16[1024,4,128]{0,2,1:T(8,128)(2,1)S(1)} %pad_maximum_fusion, bf16[512,4,192]{0,2,1:T(8,128)(2,1)S(1)} %bitcast.89), kind=kOutput, calls=%fused_computation.3 | convolution fusion | flops 274724864 | bytes 9707520 | tf_op jit(solution)/shard_map/qhd,khd->hqk/dot_general | solution.py:767
  78.5 5.1 %fusion = f32[4,512]{1,0:T(4,128)S(1)} fusion(f32[4,512,1024]{2,1,0:T(8,128)} %get-tuple-element.13, f32[4,512]{1,0:T(4,128)S(1)} %max.7, pred[512,1024]{1,0:T(8,128)(4,1)S(1)} %fusion.17), kind=kLoop, calls=%fused_computation.4 | loop fusion | flops 8386560 | bytes 8929280 | tf_op jit(solution)/shard_map/reduce_sum | solution.py:780
  83.9 1.4 fusion.81
  85.4 2.9 %fusion.70 = bf16[512,4,64]{0,2,1:T(8,128)(2,1)} fusion(f32[4,64,512]{2,1,0:T(8,128)S(1)} %fusion.81, f32[4,512,1024]{2,1,0:T(8,128)S(1)} %copy-done.4, f32[4,512]{1,0:T(4,128)S(1)} %max.7, pred[512,1024]{1,0:T(8,128)(4,1)S(1)} %fusion.17, bf16[1024,4,128]{0,2,1:T(8,128)(2,1)S(1)} %copy-done.10, f32[512,4]{0,1:T(4,128)S(1)} %add_bitcast_fusion), kind=kOutput, calls=%fused_computation.87 | convolution fusion | flops 277217280 | bytes 10240000 | tf_op jit(solution)/shard_map/hqk,khd->qhd/dot_general | solution.py:781
  88.3 1.9 fusion.28
  90.4 2.4 %convolution_convert_fusion.1 = bf16[768,512]{1,0:T(8,128)(2,1)S(1)} fusion(bf16[1024,1792]{1,0:T(8,128)(2,1)} %all-gather.4.cloned.1.call-done, bf16[1,512,1024]{2,1,0:T(8,128)(2,1)S(1)} %copy-done.8), kind=kOutput, calls=%fused_computation.32 | convolution fusion | flops 805699584 | bytes 3407872 | tf_op jit(solution)/shard_map/dot_general | solution.py:710
  95.5 16.5 %shard_map.141 = f32[16,128]{1,0:T(8,128)} custom-call(f32[32,16,128]{2,1,0:T(8,128)} %bitcast.92), custom_call_target="tpu_custom_call" | custom-call | tf_op jit(solution)/shard_map/pallas_call | solution.py:353
  115.5 6.8 %all-gather.6.cloned.1.call-done.w_ref = bf16[1024,1024]{1,0:T(8,128)(2,1)} async-done(((bf16[256,1024]{1,0:T(8,128)(2,1)}), bf16[1024,1024]{1,0:T(8,128)(2,1)}) %all-gather.6.cloned.1.call-update) | async-done | bytes 2097168 | tf_op jit(solution)/shard_map/all_gather | solution.py:663
  122.3 1.6 copy-done.1
  123.9 36.6 %shard_map.142 = bf16[4,128,1024]{2,1,0:T(8,128)(2,1)S(1)} custom-call(bf16[4,128,256]{2,1,0:T(8,128)(2,1)S(1)} %copy.50.x_ref, f32[128,1024]{1,0:T(8,128)S(1)} %convolution_add_fusion.own_ref, bf16[1024,1024]{1,0:T(8,128)(2,1)S(1)} %copy-done.1, f32[1,1024]{1,0:T(1,128)S(1)} %bitcast.83, f32[1,1024]{1,0:T(1,128)S(1)} %bitcast.84), custom_call_target="tpu_custom_call" | custom-call | tf_op jit(solution)/shard_map/pallas_call | solution.py:584
  161.6 10.1 %fusion.151 = (bf16[512,1024]{1,0:T(8,128)(2,1)}, f32[512,1024]{1,0:T(8,128)}) fusion(bf16[1024,1024]{1,0:T(8,128)(2,1)} %all-gather.8.cloned.1.call-done, bf16[512,1024]{1,0:T(8,128)(2,1)S(1)} %bitcast.82, bf16[1024,1792]{1,0:T(8,128)(2,1)} %all-gather.4.cloned.1.call-done), kind=kOutput, calls=%fused_computation.187 | convolution fusion | flops 2182086656 | bytes 8388608 | tf_op jit(solution)/shard_map/dot_general | solution.py:814
  171.8 1.9 convert_add_fusion.own_ref
  173.7 32.1 %shard_map.143 = f32[128,1024]{1,0:T(8,128)} custom-call(bf16[4,128,1024]{2,1,0:T(8,128)(2,1)} %bitcast.91, f32[128,1024]{1,0:T(8,128)} %convert_add_fusion.own_ref), custom_call_target="tpu_custom_call" | custom-call | tf_op jit(solution)/shard_map/pallas_call | solution.py:450
  208.2 1.9 fusion.92
  210.1 2.8 %copy.62 = bf16[1,1,32,2,16,4,128]{6,5,4,3,2,1,0:T(4,128)(2,1)} copy(bf16[1,1,32,2,16,4,128]{6,5,4,3,2,1,0:T(4,128)(2,1)} %bitcast.36) | data formatting | bytes 2097152
  (99 shorter events, 25.9 us)
Async XLA Ops:
  7.2 4.2 %copy-start = (bf16[1024,4,192]{0,2,1:T(8,128)(2,1)S(1)}, bf16[1024,4,192]{0,2,1:T(8,128)(2,1)}, u32[]{:S(2)}) copy-start(bf16[1024,4,192]{0,2,1:T(8,128)(2,1)} %param.14) | copy-start | bytes 4718596
  7.2 4.2 %copy-start.7 = (bf16[1,512,1024]{2,1,0:T(8,128)(2,1)S(1)}, bf16[1,512,1024]{2,1,0:T(8,128)(2,1)}, u32[]{:S(2)}) copy-start(bf16[1,512,1024]{2,1,0:T(8,128)(2,1)} %param.13) | copy-start | bytes 3145732
  7.2 81.1 %all-gather.4.cloned.1.call-start = ((), (), s32[]{:S(2)}) async-start(), calls=%async_computation.1 | async-start | bytes 4587520 | tf_op jit(solution)/shard_map/all_gather | solution.py:652
  10.6 111.7 %all-gather.6.cloned.1.call-start = ((), (), s32[]{:S(2)}) async-start(), calls=%async_computation.2 | async-start | bytes 2621440 | tf_op jit(solution)/shard_map/all_gather | solution.py:663
  12.4 2.8 %copy-start.17 = (s32[1,32,1]{1,2,0:T(1,128)S(1)}, s32[1,32,1]{1,2,0:T(1,128)}, u32[]{:S(2)}) copy-start(s32[1,32,1]{1,2,0:T(1,128)} %param.25) | copy-start | bytes 388
  19.4 15.9 %copy-start.16 = (s32[1,128]{1,0:T(1,128)S(1)}, s32[1,128]{1,0:T(1,128)}, u32[]{:S(2)}) copy-start(s32[1,128]{1,0:T(1,128)} %param.24) | copy-start | bytes 1540
  19.4 17.5 %copy-start.5 = (s32[1,16384]{1,0:T(1,128)S(1)}, s32[1,16384]{1,0:T(1,128)}, u32[]{:S(2)}) copy-start(s32[1,16384]{1,0:T(1,128)} %param.23) | copy-start | bytes 196612
  19.4 56.4 %all-to-all-start = ((bf16[32,2,16,4,128]{4,3,2,1,0:T(4,128)(2,1)}), bf16[32,2,16,4,128]{4,3,2,1,0:T(4,128)(2,1)}, u32[]{:S(2)}, u32[]{:S(2)}) async-start(bf16[32,2,16,4,128]{4,3,2,1,0:T(4,128)(2,1)} %reshape.169), calls=%async_computation | async-start | bytes 2097152 | tf_op jit(solution)/shard_map/all_to_all | solution.py:692
  29.1 132.5 %all-gather.8.cloned.1.call-start = ((), (), s32[]{:S(2)}) async-start(), calls=%async_computation.3 | async-start | bytes 2621440 | tf_op jit(solution)/shard_map/all_gather | solution.py:662
  30.0 38.8 %collective-permute-start.1 = (bf16[256,4,128]{0,2,1:T(8,128)(2,1)}, bf16[256,4,128]{0,2,1:T(8,128)(2,1)}, u32[]{:S(2)}, u32[]{:S(2)}) collective-permute-start(bf16[256,4,128]{0,2,1:T(8,128)(2,1)} %get-tuple-element.11), channel_id=1, source_target_pairs={{16,0},{32,16},{48,32},{64,48},{80,64},{96,80},{112,96},{128,112},... | collective-permute-start | bytes 786440 | tf_op jit(solution)/shard_map/ppermute | solution.py:24
  33.1 35.7 %collective-permute-start = (bf16[256,4,128]{0,2,1:T(8,128)(2,1)}, bf16[256,4,128]{0,2,1:T(8,128)(2,1)}, u32[]{:S(2)}, u32[]{:S(2)}) collective-permute-start(bf16[256,4,128]{0,2,1:T(8,128)(2,1)} %get-tuple-element.10), channel_id=1, source_target_pairs={{0,16},{16,32},{32,48},{48,64},{64,80},{80,96},{96,112},{112,128},... | collective-permute-start | bytes 786440 | tf_op jit(solution)/shard_map/ppermute | solution.py:21
  35.4 32.6 %copy-start.14 = (s32[4]{0:T(128)}, s32[4]{0:T(128)S(1)}, u32[]{:S(2)}) copy-start(s32[4]{0:T(128)S(1)} %fusion.113) | copy-start | bytes 52
  71.0 4.8 %copy-start.11 = (bf16[128,1024]{1,0:T(8,128)(2,1)S(1)}, bf16[128,1024]{1,0:T(8,128)(2,1)}, u32[]{:S(2)}) copy-start(bf16[128,1024]{1,0:T(8,128)(2,1)} %reshape.171) | copy-start | bytes 786436
  78.5 6.8 %copy-start.4 = (f32[4,512,1024]{2,1,0:T(8,128)S(1)}, f32[4,512,1024]{2,1,0:T(8,128)}, u32[]{:S(2)}) copy-start(f32[4,512,1024]{2,1,0:T(8,128)} %get-tuple-element.13) | copy-start | bytes 25165828
  83.7 1.7 copy-start.10
  88.3 2.0 copy-start.8
  93.2 19.7 %copy-start.15 = (s32[4]{0:T(128)S(1)}, s32[4]{0:T(128)}, u32[]{:S(2)}) copy-start(s32[4]{0:T(128)} %copy-done.14) | copy-start | bytes 52
  93.2 19.7 %copy-start.18 = (pred[512]{0:T(512)(128)(4,1)S(1)}, pred[512]{0:T(512)(128)(4,1)}, u32[]{:S(2)}) copy-start(pred[512]{0:T(512)(128)(4,1)} %fusion.104) | copy-start | bytes 1540
  93.3 19.7 %copy-start.19 = (bf16[512,4,64]{0,2,1:T(8,128)(2,1)S(1)}, bf16[512,4,64]{0,2,1:T(8,128)(2,1)}, u32[]{:S(2)}) copy-start(bf16[512,4,64]{0,2,1:T(8,128)(2,1)} %fusion.70) | copy-start | bytes 786436
  93.6 20.6 %copy-start.6 = (bf16[256,1024]{1,0:T(8,128)(2,1)S(1)}, bf16[256,1024]{1,0:T(8,128)(2,1)}, u32[]{:S(2)}) copy-start(bf16[256,1024]{1,0:T(8,128)(2,1)} %param.16) | copy-start | bytes 1572868
  94.6 27.7 %copy-start.2 = (f32[1024]{0:T(1024)S(1)}, f32[1024]{0:T(1024)}, u32[]{:S(2)}) copy-start(f32[1024]{0:T(1024)} %param.17) | copy-start | bytes 12292
  94.6 27.7 %copy-start.3 = (f32[1024]{0:T(1024)S(1)}, f32[1024]{0:T(1024)}, u32[]{:S(2)}) copy-start(f32[1024]{0:T(1024)} %param.18) | copy-start | bytes 12292
  171.8 36.4 %copy-start.12 = (f32[1024]{0:T(1024)S(1)}, f32[1024]{0:T(1024)}, u32[]{:S(2)}) copy-start(f32[1024]{0:T(1024)} %param.22) | copy-start | bytes 12292
  171.8 36.4 %copy-start.13 = (f32[1024]{0:T(1024)S(1)}, f32[1024]{0:T(1024)}, u32[]{:S(2)}) copy-start(f32[1024]{0:T(1024)} %param.21) | copy-start | bytes 12292
  (2 other events, 2.6 us)
Sparse Core Ops, SparseCore 0:
  10.7 52.7 all-gather.3
  65.6 56.6 all-gather.5
  124.4 37.1 all-gather.7

commit v13 on v12

--- a/solution.py
+++ b/solution.py
@@ -547,9 +547,10 @@
         copy.wait()
     chunk = 32
     width = out_ref.shape[2]
-
-    def body(i, carry):
-        rows = pl.ds(pl.multiple_of(i * chunk, chunk), chunk)
+    n_chunks = out_ref.shape[1] // chunk
+    sends = []
+    for i in range(n_chunks):
+        rows = pl.ds(i * chunk, chunk)
         total = own_ref[rows, :]
         for j in range(len(copies)):
             source = lax.rem(me + m - 1 - j, m)
@@ -559,21 +560,17 @@
         spread = jnp.sum(center * center, axis=1, keepdims=True) / width
         normed = center / jnp.sqrt(spread + 1e-05) * gain_ref[...] + bias_ref[...]
         out_ref[me, rows, :] = normed.astype(out_ref.dtype)
-        return carry
-
-    lax.fori_loop(0, out_ref.shape[1] // chunk, body, 0)
-    sends = []
-    for j, peer in enumerate(peers):
-        copy = pltpu.make_async_remote_copy(
-            src_ref=out_ref.at[me],
-            dst_ref=out_ref.at[me],
-            send_sem=g_send.at[j],
-            recv_sem=g_recv.at[j],
-            device_id=peer,
-            device_id_type=MESH,
-        )
-        copy.start()
-        sends.append(copy)
+        for j, peer in enumerate(peers):
+            copy = pltpu.make_async_remote_copy(
+                src_ref=out_ref.at[me, rows],
+                dst_ref=out_ref.at[me, rows],
+                send_sem=g_send.at[j * n_chunks + i],
+                recv_sem=g_recv.at[j * n_chunks + i],
+                device_id=peer,
+                device_id_type=MESH,
+            )
+            copy.start()
+            sends.append(copy)
     for copy in sends:
         copy.wait()
 
@@ -590,8 +587,8 @@
             pltpu.VMEM((m - 1,) + attn_parts.shape[1:], attn_parts.dtype),
             pltpu.SemaphoreType.DMA((m - 1,)),
             pltpu.SemaphoreType.DMA((m - 1,)),
-            pltpu.SemaphoreType.DMA((m - 1,)),
-            pltpu.SemaphoreType.DMA((m - 1,)),
+            pltpu.SemaphoreType.DMA(((m - 1) * (rows // 32),)),
+            pltpu.SemaphoreType.DMA(((m - 1) * (rows // 32),)),
         ],
         compiler_params=pltpu.CompilerParams(
             collective_id=10, has_side_effects=True, vmem_limit_bytes=48 * 1024 * 1024

time: 221 us -> 220 us (level)
  the two profiles are of different devices: /device:TPU:12 before, /device:TPU:2 now
where the time goes in v13:
time: 220 us; the launch traced here: 219 us
  Pallas kernels  114 us (52%)
  matrix products  33.1 us (15%)
  local copies, waits for them, and re-layouts  19.5 us (9%)
  other arithmetic  17.4 us (8%)
  starting transfers between devices  14.7 us (7%)
  between operations  14.2 us (6%)
  waiting for transfers between devices  6.54 us (3%)
    pallas_call x1, Pallas kernels, col_proj_norm_gather(): pl.pallas_call(col_proj_kernel, out_shape=jax.ShapeDtypeStruct((m, rows,...  37.5 us
    pallas_call x1, Pallas kernels, col_reduce_scatter(): pl.pallas_call(col_sum_kernel, out_shape=jax.ShapeDtypeStruct(own.shape,...  31.9 us
    pallas_call x1, Pallas kernels, seq_gather2(): pl.pallas_call(functools.partial(seq_gather2_kernel, group), out_shape=ja...  24.7 us
    pallas_call x1, Pallas kernels, seq_merge2(): pl.pallas_call(functools.partial(seq_merge2_kernel, group, top_lane), out...  19.6 us
    dot_general x1, matrix products, per_device(): ffn_full = jnp.dot(ffn_hidden, f_out, preferred_element_type=jnp.float32)  10.1 us
    all_to_all x1, starting transfers between devices, per_device(): lax.all_to_all(outgoing, 'seq', split_axis=0, concat_axis=0, tiled=True)  9.56 us
    all_gather x1, waiting for transfers between devices, per_device(): w_out = lax.all_gather(out_weight, 'col', axis=0, tiled=True)  5.78 us
    unnamed x41, local copies, waits for them, and re-layouts  5.5 us
  transfers between devices with their start and end apart: 6, of which 1 were waited for; matrix products, arithmetic and copies ran while one was open for 20% of the time, Pallas kernels for 37%

profile of v13, /device:TPU:2, one launch (start us, length us, event | category | flops | bytes accessed | tf_op | source)
XLA Modules:
  0.0 219.3 jit_solution(16451294672326910849)
XLA Ops:
  8.6 2.0 pad_maximum_fusion.1
  13.8 1.4 reshape.168
  15.4 1.4 convolution_convert_fusion
  16.8 2.6 %reshape.169 = bf16[32,2,16,4,128]{4,3,2,1,0:T(4,128)(2,1)} reshape(bf16[64,8192]{1,0:T(8,128)(2,1)} %convolution_convert_fusion) | data formatting | bytes 2097152 | tf_op jit(solution)/shard_map/reshape | solution.py:688
  19.4 9.6 %all-to-all-start = ((bf16[32,2,16,4,128]{4,3,2,1,0:T(4,128)(2,1)}), bf16[32,2,16,4,128]{4,3,2,1,0:T(4,128)(2,1)}, u32[]{:S(2)}, u32[]{:S(2)}) async-start(bf16[32,2,16,4,128]{4,3,2,1,0:T(4,128)(2,1)} %reshape.169), calls=%async_computation | async-start | bytes 2097152 | tf_op jit(solution)/shard_map/all_to_all | solution.py:689
  31.1 3.7 %collective-permute-start = (bf16[256,4,128]{0,2,1:T(8,128)(2,1)}, bf16[256,4,128]{0,2,1:T(8,128)(2,1)}, u32[]{:S(2)}, u32[]{:S(2)}) collective-permute-start(bf16[256,4,128]{0,2,1:T(8,128)(2,1)} %get-tuple-element.10), channel_id=1, source_target_pairs={{0,16},{16,32},{32,48},{48,64},{64,80},{80,96},{96,112},{112,128},... | collective-permute-start | bytes 786440 | tf_op jit(solution)/shard_map/ppermute | solution.py:21
  35.0 1.5 convolution_convert_fusion.5
  38.8 24.7 %shard_map.140 = bf16[32,32,128]{2,1,0:T(8,128)(2,1)} custom-call(bf16[32,128]{1,0:T(8,128)(2,1)} %reshape.170.x_ref), custom_call_target="tpu_custom_call" | custom-call | tf_op jit(solution)/shard_map/pallas_call | solution.py:290
  63.5 1.8 reshape.171
  69.2 4.8 %select_reduce_fusion = (f32[4,512]{1,0:T(4,128)S(1)}, f32[4,512,1024]{2,1,0:T(8,128)}) fusion(pred[512,1024]{1,0:T(8,128)(4,1)S(1)} %fusion.17, bf16[1024,4,128]{0,2,1:T(8,128)(2,1)S(1)} %pad_maximum_fusion, bf16[512,4,192]{0,2,1:T(8,128)(2,1)S(1)} %bitcast.89), kind=kOutput, calls=%fused_computation.3 | convolution fusion | flops 274724864 | bytes 9707520 | tf_op jit(solution)/shard_map/qhd,khd->hqk/dot_general | solution.py:764
  76.8 5.0 %fusion = f32[4,512]{1,0:T(4,128)S(1)} fusion(f32[4,512,1024]{2,1,0:T(8,128)} %get-tuple-element.13, f32[4,512]{1,0:T(4,128)S(1)} %max.7, pred[512,1024]{1,0:T(8,128)(4,1)S(1)} %fusion.17), kind=kLoop, calls=%fused_computation.4 | loop fusion | flops 8386560 | bytes 8929280 | tf_op jit(solution)/shard_map/reduce_sum | solution.py:777
  82.0 1.5 fusion.81
  83.5 2.9 %fusion.70 = bf16[512,4,64]{0,2,1:T(8,128)(2,1)} fusion(f32[4,64,512]{2,1,0:T(8,128)S(1)} %fusion.81, f32[4,512,1024]{2,1,0:T(8,128)S(1)} %copy-done.4, f32[4,512]{1,0:T(4,128)S(1)} %max.7, pred[512,1024]{1,0:T(8,128)(4,1)S(1)} %fusion.17, bf16[1024,4,128]{0,2,1:T(8,128)(2,1)S(1)} %copy-done.10, f32[512,4]{0,1:T(4,128)S(1)} %add_bitcast_fusion), kind=kOutput, calls=%fused_computation.87 | convolution fusion | flops 277217280 | bytes 10240000 | tf_op jit(solution)/shard_map/hqk,khd->qhd/dot_general | solution.py:778
  86.4 1.9 fusion.28
  88.4 2.4 %convolution_convert_fusion.1 = bf16[768,512]{1,0:T(8,128)(2,1)S(1)} fusion(bf16[1024,1792]{1,0:T(8,128)(2,1)} %all-gather.4.cloned.1.call-done, bf16[1,512,1024]{2,1,0:T(8,128)(2,1)S(1)} %copy-done.8), kind=kOutput, calls=%fused_computation.32 | convolution fusion | flops 805699584 | bytes 3407872 | tf_op jit(solution)/shard_map/dot_general | solution.py:707
  93.6 19.6 %shard_map.141 = f32[16,128]{1,0:T(8,128)} custom-call(f32[32,16,128]{2,1,0:T(8,128)} %bitcast.92), custom_call_target="tpu_custom_call" | custom-call | tf_op jit(solution)/shard_map/pallas_call | solution.py:353
  116.6 5.8 %all-gather.6.cloned.1.call-done.w_ref = bf16[1024,1024]{1,0:T(8,128)(2,1)} async-done(((bf16[256,1024]{1,0:T(8,128)(2,1)}), bf16[1024,1024]{1,0:T(8,128)(2,1)}) %all-gather.6.cloned.1.call-update) | async-done | bytes 2097168 | tf_op jit(solution)/shard_map/all_gather | solution.py:660
  122.4 1.6 copy-done.1
  124.0 37.5 %shard_map.142 = bf16[4,128,1024]{2,1,0:T(8,128)(2,1)S(1)} custom-call(bf16[4,128,256]{2,1,0:T(8,128)(2,1)S(1)} %copy.50.x_ref, f32[128,1024]{1,0:T(8,128)S(1)} %convolution_add_fusion.own_ref, bf16[1024,1024]{1,0:T(8,128)(2,1)S(1)} %copy-done.1, f32[1,1024]{1,0:T(1,128)S(1)} %bitcast.83, f32[1,1024]{1,0:T(1,128)S(1)} %bitcast.84), custom_call_target="tpu_custom_call" | custom-call | tf_op jit(solution)/shard_map/pallas_call | solution.py:581
  161.6 10.1 %fusion.151 = (bf16[512,1024]{1,0:T(8,128)(2,1)}, f32[512,1024]{1,0:T(8,128)}) fusion(bf16[1024,1024]{1,0:T(8,128)(2,1)} %all-gather.8.cloned.1.call-done, bf16[512,1024]{1,0:T(8,128)(2,1)S(1)} %bitcast.82, bf16[1024,1792]{1,0:T(8,128)(2,1)} %all-gather.4.cloned.1.call-done), kind=kOutput, calls=%fused_computation.187 | convolution fusion | flops 2182086656 | bytes 8388608 | tf_op jit(solution)/shard_map/dot_general | solution.py:811
  171.8 1.9 convert_add_fusion.own_ref
  173.7 31.9 %shard_map.143 = f32[128,1024]{1,0:T(8,128)} custom-call(bf16[4,128,1024]{2,1,0:T(8,128)(2,1)} %bitcast.91, f32[128,1024]{1,0:T(8,128)} %convert_add_fusion.own_ref), custom_call_target="tpu_custom_call" | custom-call | tf_op jit(solution)/shard_map/pallas_call | solution.py:450
  208.1 1.9 fusion.92
  210.0 2.8 %copy.62 = bf16[1,1,32,2,16,4,128]{6,5,4,3,2,1,0:T(4,128)(2,1)} copy(bf16[1,1,32,2,16,4,128]{6,5,4,3,2,1,0:T(4,128)(2,1)} %bitcast.36) | data formatting | bytes 2097152
  (99 shorter events, 24.6 us)
Async XLA Ops:
  7.2 4.2 %copy-start = (bf16[1024,4,192]{0,2,1:T(8,128)(2,1)S(1)}, bf16[1024,4,192]{0,2,1:T(8,128)(2,1)}, u32[]{:S(2)}) copy-start(bf16[1024,4,192]{0,2,1:T(8,128)(2,1)} %param.14) | copy-start | bytes 4718596
  7.2 4.2 %copy-start.7 = (bf16[1,512,1024]{2,1,0:T(8,128)(2,1)S(1)}, bf16[1,512,1024]{2,1,0:T(8,128)(2,1)}, u32[]{:S(2)}) copy-start(bf16[1,512,1024]{2,1,0:T(8,128)(2,1)} %param.13) | copy-start | bytes 3145732
  7.2 79.2 %all-gather.4.cloned.1.call-start = ((), (), s32[]{:S(2)}) async-start(), calls=%async_computation.1 | async-start | bytes 4587520 | tf_op jit(solution)/shard_map/all_gather | solution.py:649
  10.6 111.8 %all-gather.6.cloned.1.call-start = ((), (), s32[]{:S(2)}) async-start(), calls=%async_computation.2 | async-start | bytes 2621440 | tf_op jit(solution)/shard_map/all_gather | solution.py:660
  12.4 2.8 %copy-start.17 = (s32[1,32,1]{1,2,0:T(1,128)S(1)}, s32[1,32,1]{1,2,0:T(1,128)}, u32[]{:S(2)}) copy-start(s32[1,32,1]{1,2,0:T(1,128)} %param.25) | copy-start | bytes 388
  19.4 15.5 %copy-start.16 = (s32[1,128]{1,0:T(1,128)S(1)}, s32[1,128]{1,0:T(1,128)}, u32[]{:S(2)}) copy-start(s32[1,128]{1,0:T(1,128)} %param.24) | copy-start | bytes 1540
  19.4 17.1 %copy-start.5 = (s32[1,16384]{1,0:T(1,128)S(1)}, s32[1,16384]{1,0:T(1,128)}, u32[]{:S(2)}) copy-start(s32[1,16384]{1,0:T(1,128)} %param.23) | copy-start | bytes 196612
  19.4 54.6 %all-to-all-start = ((bf16[32,2,16,4,128]{4,3,2,1,0:T(4,128)(2,1)}), bf16[32,2,16,4,128]{4,3,2,1,0:T(4,128)(2,1)}, u32[]{:S(2)}, u32[]{:S(2)}) async-start(bf16[32,2,16,4,128]{4,3,2,1,0:T(4,128)(2,1)} %reshape.169), calls=%async_computation | async-start | bytes 2097152 | tf_op jit(solution)/shard_map/all_to_all | solution.py:689
  29.0 132.6 %all-gather.8.cloned.1.call-start = ((), (), s32[]{:S(2)}) async-start(), calls=%async_computation.3 | async-start | bytes 2621440 | tf_op jit(solution)/shard_map/all_gather | solution.py:659
  29.9 37.2 %collective-permute-start.1 = (bf16[256,4,128]{0,2,1:T(8,128)(2,1)}, bf16[256,4,128]{0,2,1:T(8,128)(2,1)}, u32[]{:S(2)}, u32[]{:S(2)}) collective-permute-start(bf16[256,4,128]{0,2,1:T(8,128)(2,1)} %get-tuple-element.11), channel_id=1, source_target_pairs={{16,0},{32,16},{48,32},{64,48},{80,64},{96,80},{112,96},{128,112},... | collective-permute-start | bytes 786440 | tf_op jit(solution)/shard_map/ppermute | solution.py:24
  31.1 35.9 %collective-permute-start = (bf16[256,4,128]{0,2,1:T(8,128)(2,1)}, bf16[256,4,128]{0,2,1:T(8,128)(2,1)}, u32[]{:S(2)}, u32[]{:S(2)}) collective-permute-start(bf16[256,4,128]{0,2,1:T(8,128)(2,1)} %get-tuple-element.10), channel_id=1, source_target_pairs={{0,16},{16,32},{32,48},{48,64},{64,80},{80,96},{96,112},{112,128},... | collective-permute-start | bytes 786440 | tf_op jit(solution)/shard_map/ppermute | solution.py:21
  35.0 31.2 %copy-start.14 = (s32[4]{0:T(128)}, s32[4]{0:T(128)S(1)}, u32[]{:S(2)}) copy-start(s32[4]{0:T(128)S(1)} %fusion.113) | copy-start | bytes 52
  69.2 4.8 %copy-start.11 = (bf16[128,1024]{1,0:T(8,128)(2,1)S(1)}, bf16[128,1024]{1,0:T(8,128)(2,1)}, u32[]{:S(2)}) copy-start(bf16[128,1024]{1,0:T(8,128)(2,1)} %reshape.171) | copy-start | bytes 786436
  76.8 6.7 %copy-start.4 = (f32[4,512,1024]{2,1,0:T(8,128)S(1)}, f32[4,512,1024]{2,1,0:T(8,128)}, u32[]{:S(2)}) copy-start(f32[4,512,1024]{2,1,0:T(8,128)} %get-tuple-element.13) | copy-start | bytes 25165828
  81.7 1.7 copy-start.10
  86.4 2.0 copy-start.8
  91.3 22.8 %copy-start.15 = (s32[4]{0:T(128)S(1)}, s32[4]{0:T(128)}, u32[]{:S(2)}) copy-start(s32[4]{0:T(128)} %copy-done.14) | copy-start | bytes 52
  91.3 22.8 %copy-start.18 = (pred[512]{0:T(512)(128)(4,1)S(1)}, pred[512]{0:T(512)(128)(4,1)}, u32[]{:S(2)}) copy-start(pred[512]{0:T(512)(128)(4,1)} %fusion.104) | copy-start | bytes 1540
  91.3 22.8 %copy-start.19 = (bf16[512,4,64]{0,2,1:T(8,128)(2,1)S(1)}, bf16[512,4,64]{0,2,1:T(8,128)(2,1)}, u32[]{:S(2)}) copy-start(bf16[512,4,64]{0,2,1:T(8,128)(2,1)} %fusion.70) | copy-start | bytes 786436
  91.7 23.7 %copy-start.6 = (bf16[256,1024]{1,0:T(8,128)(2,1)S(1)}, bf16[256,1024]{1,0:T(8,128)(2,1)}, u32[]{:S(2)}) copy-start(bf16[256,1024]{1,0:T(8,128)(2,1)} %param.16) | copy-start | bytes 1572868
  92.7 29.7 %copy-start.2 = (f32[1024]{0:T(1024)S(1)}, f32[1024]{0:T(1024)}, u32[]{:S(2)}) copy-start(f32[1024]{0:T(1024)} %param.17) | copy-start | bytes 12292
  92.7 29.7 %copy-start.3 = (f32[1024]{0:T(1024)S(1)}, f32[1024]{0:T(1024)}, u32[]{:S(2)}) copy-start(f32[1024]{0:T(1024)} %param.18) | copy-start | bytes 12292
  171.7 36.3 %copy-start.12 = (f32[1024]{0:T(1024)S(1)}, f32[1024]{0:T(1024)}, u32[]{:S(2)}) copy-start(f32[1024]{0:T(1024)} %param.22) | copy-start | bytes 12292
  171.8 36.3 %copy-start.13 = (f32[1024]{0:T(1024)S(1)}, f32[1024]{0:T(1024)}, u32[]{:S(2)}) copy-start(f32[1024]{0:T(1024)} %param.21) | copy-start | bytes 12292
  (2 other events, 2.6 us)
Sparse Core Ops, SparseCore 0:
  10.7 53.1 all-gather.3
  66.0 56.3 all-gather.5
  124.5 36.8 all-gather.7

commit v14 on v13

--- a/solution.py
+++ b/solution.py
@@ -594,6 +594,56 @@
             collective_id=10, has_side_effects=True, vmem_limit_bytes=48 * 1024 * 1024
         ),
     )(attn_parts, own, w_full, gain.reshape(1, width), bias.reshape(1, width))
+
+
+def col_sum_ln_kernel(x_ref, own_ref, gain_ref, bias_ref, out_ref, got, send_sem, recv_sem):
+    me, peers = col_peers()
+    copies = []
+    for j, peer in enumerate(peers):
+        copy = pltpu.make_async_remote_copy(
+            src_ref=x_ref.at[peer[2]],
+            dst_ref=got.at[j],
+            send_sem=send_sem.at[j],
+            recv_sem=recv_sem.at[j],
+            device_id=peer,
+            device_id_type=MESH,
+        )
+        copy.start()
+        copies.append(copy)
+    for copy in copies:
+        copy.wait()
+    chunk = 32
+    width = out_ref.shape[1]
+
+    def body(i, carry):
+        rows = pl.ds(pl.multiple_of(i * chunk, chunk), chunk)
+        total = own_ref[rows, :]
+        for j in range(len(copies)):
+            total = total + got[j, rows, :].astype(jnp.float32)
+        center = total - jnp.sum(total, axis=1, keepdims=True) / width
+        spread = jnp.sum(center * center, axis=1, keepdims=True) / width
+        normed = center / jnp.sqrt(spread + 1e-05) * gain_ref[...] + bias_ref[...]
+        out_ref[rows, :] = normed.astype(out_ref.dtype)
+        return carry
+
+    lax.fori_loop(0, out_ref.shape[0] // chunk, body, 0)
+
+
+def col_sum_norm(parts, own, gain, bias):
+    m = lax.axis_size("col")
+    rows, width = own.shape
+    return pl.pallas_call(
+        col_sum_ln_kernel,
+        out_shape=jax.ShapeDtypeStruct(own.shape, jnp.bfloat16),
+        in_specs=[pl.BlockSpec(memory_space=pltpu.VMEM)] * 4,
+        out_specs=pl.BlockSpec(memory_space=pltpu.VMEM),
+        scratch_shapes=[
+            pltpu.VMEM((m - 1,) + parts.shape[1:], parts.dtype),
+            pltpu.SemaphoreType.DMA((m - 1,)),
+            pltpu.SemaphoreType.DMA((m - 1,)),
+        ],
+        compiler_params=pltpu.CompilerParams(collective_id=11, has_side_effects=True),
+    )(parts, own, gain.reshape(1, width), bias.reshape(1, width))
 
 
 def layer_norm(values, gain, bias):
@@ -810,13 +860,13 @@
     ffn_hidden = jax.nn.gelu(ffn_pre, approximate=False).astype(jnp.bfloat16)
     ffn_full = jnp.dot(ffn_hidden, f_out, preferred_element_type=jnp.float32)
     ffn_own = lax.dynamic_slice_in_dim(ffn_full, col_index * out_rows, out_rows, 0)
-    second = col_reduce_scatter(
+    normed = col_sum_norm(
         ffn_full.astype(jnp.bfloat16).reshape(n_col, out_rows, width),
         mine.astype(jnp.float32) + ffn_own,
-        6,
-    )
-    normed = layer_norm(second, ln2_gain, ln2_bias)
-    return (normed.astype(jnp.bfloat16)[None], page_pool)
+        ln2_gain,
+        ln2_bias,
+    )
+    return (normed[None], page_pool)
 
 
 def solution(mesh):

time: 220 us -> 219 us (level)
  the two profiles are of different devices: /device:TPU:2 before, /device:TPU:8 now
where the time goes in v14:
time: 219 us; the launch traced here: 218 us
  Pallas kernels  110 us (50%)
  matrix products  33 us (15%)
  local copies, waits for them, and re-layouts  21.2 us (10%)
  starting transfers between devices  15.4 us (7%)
  between operations  14.2 us (6%)
  other arithmetic  13.4 us (6%)
  waiting for transfers between devices  10.6 us (5%)
    pallas_call x1, Pallas kernels, col_proj_norm_gather(): pl.pallas_call(col_proj_kernel, out_shape=jax.ShapeDtypeStruct((m, rows,...  35 us
    pallas_call x1, Pallas kernels, col_sum_norm(): pl.pallas_call(col_sum_ln_kernel, out_shape=jax.ShapeDtypeStruct(own.shap...  32.7 us
    pallas_call x1, Pallas kernels, seq_gather2(): pl.pallas_call(functools.partial(seq_gather2_kernel, group), out_shape=ja...  26.4 us
    pallas_call x1, Pallas kernels, seq_merge2(): pl.pallas_call(functools.partial(seq_merge2_kernel, group, top_lane), out...  16 us
    all_to_all x1, starting transfers between devices, per_device(): lax.all_to_all(outgoing, 'seq', split_axis=0, concat_axis=0, tiled=True)  10.2 us
    dot_general x1, matrix products, per_device(): ffn_full = jnp.dot(ffn_hidden, f_out, preferred_element_type=jnp.float32)  10.1 us
    unnamed x38, local copies, waits for them, and re-layouts  7.16 us
    all_gather x1, waiting for transfers between devices, per_device(): w_out = lax.all_gather(out_weight, 'col', axis=0, tiled=True)  6.86 us
  transfers between devices with their start and end apart: 6, of which 2 were waited for; matrix products, arithmetic and copies ran while one was open for 21% of the time, Pallas kernels for 36%

profile of v14, /device:TPU:8, one launch (start us, length us, event | category | flops | bytes accessed | tf_op | source)
XLA Modules:
  0.0 217.9 jit_solution(3638590907284166547)
XLA Ops:
  8.6 2.0 pad_maximum_fusion.1
  13.8 1.4 reshape.160
  16.8 2.6 %reshape.161 = bf16[32,2,16,4,128]{4,3,2,1,0:T(4,128)(2,1)} reshape(bf16[64,8192]{1,0:T(8,128)(2,1)} %convolution_convert_fusion) | data formatting | bytes 2097152 | tf_op jit(solution)/shard_map/reshape | solution.py:738
  19.4 10.2 %all-to-all-start = ((bf16[32,2,16,4,128]{4,3,2,1,0:T(4,128)(2,1)}), bf16[32,2,16,4,128]{4,3,2,1,0:T(4,128)(2,1)}, u32[]{:S(2)}, u32[]{:S(2)}) async-start(bf16[32,2,16,4,128]{4,3,2,1,0:T(4,128)(2,1)} %reshape.161), calls=%async_computation | async-start | bytes 2097152 | tf_op jit(solution)/shard_map/all_to_all | solution.py:739
  30.6 3.1 %collective-permute-start.1 = (bf16[256,4,128]{0,2,1:T(8,128)(2,1)}, bf16[256,4,128]{0,2,1:T(8,128)(2,1)}, u32[]{:S(2)}, u32[]{:S(2)}) collective-permute-start(bf16[256,4,128]{0,2,1:T(8,128)(2,1)} %get-tuple-element.11), channel_id=1, source_target_pairs={{16,0},{32,16},{48,32},{64,48},{80,64},{96,80},{112,96},{128,112},... | collective-permute-start | bytes 786440 | tf_op jit(solution)/shard_map/ppermute | solution.py:24
  33.7 1.9 collective-permute-start
  35.8 1.5 convolution_convert_fusion.5
  39.5 26.4 %shard_map.140 = bf16[32,32,128]{2,1,0:T(8,128)(2,1)} custom-call(bf16[32,128]{1,0:T(8,128)(2,1)} %reshape.162.x_ref), custom_call_target="tpu_custom_call" | custom-call | tf_op jit(solution)/shard_map/pallas_call | solution.py:290
  65.9 1.8 reshape.163
  71.6 4.8 %select_reduce_fusion = (f32[4,512]{1,0:T(4,128)S(1)}, f32[4,512,1024]{2,1,0:T(8,128)}) fusion(pred[512,1024]{1,0:T(8,128)(4,1)S(1)} %fusion.17, bf16[1024,4,128]{0,2,1:T(8,128)(2,1)S(1)} %pad_maximum_fusion, bf16[512,4,192]{0,2,1:T(8,128)(2,1)S(1)} %bitcast.90), kind=kOutput, calls=%fused_computation.3 | convolution fusion | flops 274724864 | bytes 9707520 | tf_op jit(solution)/shard_map/qhd,khd->hqk/dot_general | solution.py:814
  79.1 5.3 %fusion = f32[4,512]{1,0:T(4,128)S(1)} fusion(f32[4,512,1024]{2,1,0:T(8,128)} %get-tuple-element.13, f32[4,512]{1,0:T(4,128)S(1)} %max.7, pred[512,1024]{1,0:T(8,128)(4,1)S(1)} %fusion.17), kind=kLoop, calls=%fused_computation.4 | loop fusion | flops 8386560 | bytes 8929280 | tf_op jit(solution)/shard_map/reduce_sum | solution.py:827
  86.0 2.9 %fusion.70 = bf16[512,4,64]{0,2,1:T(8,128)(2,1)} fusion(f32[4,64,512]{2,1,0:T(8,128)S(1)} %fusion.81, f32[4,512,1024]{2,1,0:T(8,128)S(1)} %copy-done.4, f32[4,512]{1,0:T(4,128)S(1)} %max.7, pred[512,1024]{1,0:T(8,128)(4,1)S(1)} %fusion.17, bf16[1024,4,128]{0,2,1:T(8,128)(2,1)S(1)} %copy-done.10, f32[512,4]{0,1:T(4,128)S(1)} %add_bitcast_fusion), kind=kOutput, calls=%fused_computation.87 | convolution fusion | flops 277217280 | bytes 10240000 | tf_op jit(solution)/shard_map/hqk,khd->qhd/dot_general | solution.py:828
  88.9 1.9 fusion.28
  90.9 2.4 %convolution_convert_fusion.1 = bf16[768,512]{1,0:T(8,128)(2,1)S(1)} fusion(bf16[1024,1792]{1,0:T(8,128)(2,1)} %all-gather.4.cloned.1.call-done, bf16[1,512,1024]{2,1,0:T(8,128)(2,1)S(1)} %copy-done.8), kind=kOutput, calls=%fused_computation.32 | convolution fusion | flops 805699584 | bytes 3407872 | tf_op jit(solution)/shard_map/dot_general | solution.py:757
  96.1 16.0 %shard_map.141 = f32[16,128]{1,0:T(8,128)} custom-call(f32[32,16,128]{2,1,0:T(8,128)} %bitcast.94), custom_call_target="tpu_custom_call" | custom-call | tf_op jit(solution)/shard_map/pallas_call | solution.py:353
  115.5 6.9 %all-gather.6.cloned.1.call-done.w_ref = bf16[1024,1024]{1,0:T(8,128)(2,1)} async-done(((bf16[256,1024]{1,0:T(8,128)(2,1)}), bf16[1024,1024]{1,0:T(8,128)(2,1)}) %all-gather.6.cloned.1.call-update) | async-done | bytes 2097168 | tf_op jit(solution)/shard_map/all_gather | solution.py:710
  122.4 1.6 copy-done.1
  124.0 35.0 %shard_map.142 = bf16[4,128,1024]{2,1,0:T(8,128)(2,1)S(1)} custom-call(bf16[4,128,256]{2,1,0:T(8,128)(2,1)S(1)} %copy.50.x_ref, f32[128,1024]{1,0:T(8,128)S(1)} %convolution_add_fusion.own_ref, bf16[1024,1024]{1,0:T(8,128)(2,1)S(1)} %copy-done.1, f32[1,1024]{1,0:T(1,128)S(1)} %bitcast.84, f32[1,1024]{1,0:T(1,128)S(1)} %bitcast.85), custom_call_target="tpu_custom_call" | custom-call | tf_op jit(solution)/shard_map/pallas_call | solution.py:581
  159.0 3.0 %all-gather.8.cloned.1.call-done = bf16[1024,1024]{1,0:T(8,128)(2,1)} async-done(((bf16[1024,256]{1,0:T(8,128)(2,1)}), bf16[1024,1024]{1,0:T(8,128)(2,1)}) %all-gather.8.cloned.1.call-update) | async-done | bytes 2097168 | tf_op jit(solution)/shard_map/all_gather | solution.py:709
  162.1 10.1 %fusion.150 = (bf16[512,1024]{1,0:T(8,128)(2,1)}, f32[512,1024]{1,0:T(8,128)}) fusion(bf16[1024,1024]{1,0:T(8,128)(2,1)} %all-gather.8.cloned.1.call-done, bf16[512,1024]{1,0:T(8,128)(2,1)S(1)} %bitcast.83, bf16[1024,1792]{1,0:T(8,128)(2,1)} %all-gather.4.cloned.1.call-done), kind=kOutput, calls=%fused_computation.182 | convolution fusion | flops 2182086656 | bytes 8388608 | tf_op jit(solution)/shard_map/dot_general | solution.py:861
  172.2 1.9 convert_add_fusion.own_ref
  174.1 32.7 %shard_map.143 = bf16[128,1024]{1,0:T(8,128)(2,1)} custom-call(bf16[4,128,1024]{2,1,0:T(8,128)(2,1)} %bitcast.92, f32[128,1024]{1,0:T(8,128)} %convert_add_fusion.own_ref, f32[1,1024]{1,0:T(1,128)} %bitcast.106, f32[1,1024]{1,0:T(1,128)} %bitcast.107), custom_call_target="tpu_custom_call" | custom-call | tf_op jit(solution)/shard_map/pallas_call | solution.py:635
  206.8 1.7 copy.63
  208.5 2.8 %copy.64 = bf16[1,1,32,2,16,4,128]{6,5,4,3,2,1,0:T(4,128)(2,1)} copy(bf16[1,1,32,2,16,4,128]{6,5,4,3,2,1,0:T(4,128)(2,1)} %bitcast.38) | data formatting | bytes 2097152
  (91 shorter events, 23.7 us)
Async XLA Ops:
  7.2 4.2 %copy-start = (bf16[1024,4,192]{0,2,1:T(8,128)(2,1)S(1)}, bf16[1024,4,192]{0,2,1:T(8,128)(2,1)}, u32[]{:S(2)}) copy-start(bf16[1024,4,192]{0,2,1:T(8,128)(2,1)} %param.14) | copy-start | bytes 4718596
  7.2 4.2 %copy-start.7 = (bf16[1,512,1024]{2,1,0:T(8,128)(2,1)S(1)}, bf16[1,512,1024]{2,1,0:T(8,128)(2,1)}, u32[]{:S(2)}) copy-start(bf16[1,512,1024]{2,1,0:T(8,128)(2,1)} %param.13) | copy-start | bytes 3145732
  7.2 81.7 %all-gather.4.cloned.1.call-start = ((), (), s32[]{:S(2)}) async-start(), calls=%async_computation.1 | async-start | bytes 4587520 | tf_op jit(solution)/shard_map/all_gather | solution.py:699
  10.6 111.8 %all-gather.6.cloned.1.call-start = ((), (), s32[]{:S(2)}) async-start(), calls=%async_computation.2 | async-start | bytes 2621440 | tf_op jit(solution)/shard_map/all_gather | solution.py:710
  12.4 2.8 %copy-start.15 = (s32[1,32,1]{1,2,0:T(1,128)S(1)}, s32[1,32,1]{1,2,0:T(1,128)}, u32[]{:S(2)}) copy-start(s32[1,32,1]{1,2,0:T(1,128)} %param.25) | copy-start | bytes 388
  19.4 16.2 %copy-start.14 = (s32[1,128]{1,0:T(1,128)S(1)}, s32[1,128]{1,0:T(1,128)}, u32[]{:S(2)}) copy-start(s32[1,128]{1,0:T(1,128)} %param.24) | copy-start | bytes 1540
  19.4 17.8 %copy-start.5 = (s32[1,16384]{1,0:T(1,128)S(1)}, s32[1,16384]{1,0:T(1,128)}, u32[]{:S(2)}) copy-start(s32[1,16384]{1,0:T(1,128)} %param.23) | copy-start | bytes 196612
  19.4 57.0 %all-to-all-start = ((bf16[32,2,16,4,128]{4,3,2,1,0:T(4,128)(2,1)}), bf16[32,2,16,4,128]{4,3,2,1,0:T(4,128)(2,1)}, u32[]{:S(2)}, u32[]{:S(2)}) async-start(bf16[32,2,16,4,128]{4,3,2,1,0:T(4,128)(2,1)} %reshape.161), calls=%async_computation | async-start | bytes 2097152 | tf_op jit(solution)/shard_map/all_to_all | solution.py:739
  29.7 132.4 %all-gather.8.cloned.1.call-start = ((), (), s32[]{:S(2)}) async-start(), calls=%async_computation.3 | async-start | bytes 2621440 | tf_op jit(solution)/shard_map/all_gather | solution.py:709
  30.6 38.8 %collective-permute-start.1 = (bf16[256,4,128]{0,2,1:T(8,128)(2,1)}, bf16[256,4,128]{0,2,1:T(8,128)(2,1)}, u32[]{:S(2)}, u32[]{:S(2)}) collective-permute-start(bf16[256,4,128]{0,2,1:T(8,128)(2,1)} %get-tuple-element.11), channel_id=1, source_target_pairs={{16,0},{32,16},{48,32},{64,48},{80,64},{96,80},{112,96},{128,112},... | collective-permute-start | bytes 786440 | tf_op jit(solution)/shard_map/ppermute | solution.py:24
  33.7 35.7 %collective-permute-start = (bf16[256,4,128]{0,2,1:T(8,128)(2,1)}, bf16[256,4,128]{0,2,1:T(8,128)(2,1)}, u32[]{:S(2)}, u32[]{:S(2)}) collective-permute-start(bf16[256,4,128]{0,2,1:T(8,128)(2,1)} %get-tuple-element.10), channel_id=1, source_target_pairs={{0,16},{16,32},{32,48},{48,64},{64,80},{80,96},{96,112},{112,128},... | collective-permute-start | bytes 786440 | tf_op jit(solution)/shard_map/ppermute | solution.py:21
  35.8 32.8 %copy-start.12 = (s32[4]{0:T(128)}, s32[4]{0:T(128)S(1)}, u32[]{:S(2)}) copy-start(s32[4]{0:T(128)S(1)} %fusion.112) | copy-start | bytes 52
  70.6 1.0 copy-start.9
  71.6 4.8 %copy-start.11 = (bf16[128,1024]{1,0:T(8,128)(2,1)S(1)}, bf16[128,1024]{1,0:T(8,128)(2,1)}, u32[]{:S(2)}) copy-start(bf16[128,1024]{1,0:T(8,128)(2,1)} %reshape.163) | copy-start | bytes 786436
  79.1 6.9 %copy-start.4 = (f32[4,512,1024]{2,1,0:T(8,128)S(1)}, f32[4,512,1024]{2,1,0:T(8,128)}, u32[]{:S(2)}) copy-start(f32[4,512,1024]{2,1,0:T(8,128)} %get-tuple-element.13) | copy-start | bytes 25165828
  84.4 1.6 copy-start.10
  88.9 2.0 copy-start.8
  93.8 19.1 %copy-start.13 = (s32[4]{0:T(128)S(1)}, s32[4]{0:T(128)}, u32[]{:S(2)}) copy-start(s32[4]{0:T(128)} %copy-done.12) | copy-start | bytes 52
  93.8 19.1 %copy-start.16 = (pred[512]{0:T(512)(128)(4,1)S(1)}, pred[512]{0:T(512)(128)(4,1)}, u32[]{:S(2)}) copy-start(pred[512]{0:T(512)(128)(4,1)} %fusion.103) | copy-start | bytes 1540
  93.9 19.1 %copy-start.17 = (bf16[512,4,64]{0,2,1:T(8,128)(2,1)S(1)}, bf16[512,4,64]{0,2,1:T(8,128)(2,1)}, u32[]{:S(2)}) copy-start(bf16[512,4,64]{0,2,1:T(8,128)(2,1)} %fusion.70) | copy-start | bytes 786436
  94.2 20.1 %copy-start.6 = (bf16[256,1024]{1,0:T(8,128)(2,1)S(1)}, bf16[256,1024]{1,0:T(8,128)(2,1)}, u32[]{:S(2)}) copy-start(bf16[256,1024]{1,0:T(8,128)(2,1)} %param.16) | copy-start | bytes 1572868
  95.2 27.1 %copy-start.2 = (f32[1024]{0:T(1024)S(1)}, f32[1024]{0:T(1024)}, u32[]{:S(2)}) copy-start(f32[1024]{0:T(1024)} %param.17) | copy-start | bytes 12292
  95.2 27.1 %copy-start.3 = (f32[1024]{0:T(1024)S(1)}, f32[1024]{0:T(1024)}, u32[]{:S(2)}) copy-start(f32[1024]{0:T(1024)} %param.18) | copy-start | bytes 12292
  122.4 1.6 copy-start.1
Sparse Core Ops, SparseCore 0:
  10.7 53.7 all-gather.3
  66.7 55.6 all-gather.5
  124.5 37.5 all-gather.7

commit v15 on v14

--- a/solution.py
+++ b/solution.py
@@ -527,8 +527,12 @@
     )(parts, own, gain.reshape(1, width), bias.reshape(1, width))
 
 
-def col_proj_kernel(x_ref, own_ref, w_ref, gain_ref, bias_ref, out_ref, got, rs_send, rs_recv, g_send, g_recv):
+def col_proj_kernel(
+    x_ref, own_ref, w_hbm, gain_ref, bias_ref, out_ref, got, w_ref, w_sem, rs_send, rs_recv, g_send, g_recv
+):
     me, peers = col_peers()
+    w_copy = pltpu.make_async_copy(w_hbm, w_ref, w_sem)
+    w_copy.start()
     m = len(peers) + 1
     heads_width = x_ref.shape[2]
     copies = []
@@ -545,6 +549,7 @@
         copies.append(copy)
     for copy in copies:
         copy.wait()
+    w_copy.wait()
     chunk = 32
     width = out_ref.shape[2]
     n_chunks = out_ref.shape[1] // chunk
@@ -581,10 +586,14 @@
     return pl.pallas_call(
         col_proj_kernel,
         out_shape=jax.ShapeDtypeStruct((m, rows, width), jnp.bfloat16),
-        in_specs=[pl.BlockSpec(memory_space=pltpu.VMEM)] * 5,
+        in_specs=[pl.BlockSpec(memory_space=pltpu.VMEM)] * 2
+        + [pl.BlockSpec(memory_space=pl.ANY)]
+        + [pl.BlockSpec(memory_space=pltpu.VMEM)] * 2,
         out_specs=pl.BlockSpec(memory_space=pltpu.VMEM),
         scratch_shapes=[
             pltpu.VMEM((m - 1,) + attn_parts.shape[1:], attn_parts.dtype),
+            pltpu.VMEM(w_full.shape, w_full.dtype),
+            pltpu.SemaphoreType.DMA(()),
             pltpu.SemaphoreType.DMA((m - 1,)),
             pltpu.SemaphoreType.DMA((m - 1,)),
             pltpu.SemaphoreType.DMA(((m - 1) * (rows // 32),)),

time: 219 us -> 218 us (level)
  the two profiles are of different devices: /device:TPU:8 before, /device:TPU:1 now
where the time goes in v15:
time: 218 us; the launch traced here: 214 us
  Pallas kernels  108 us (50%)
  matrix products  33.1 us (15%)
  local copies, waits for them, and re-layouts  21.2 us (10%)
  starting transfers between devices  17.1 us (8%)
  between operations  14.2 us (7%)
  other arithmetic  13.1 us (6%)
  waiting for transfers between devices  6.96 us (3%)
    pallas_call x1, Pallas kernels, col_proj_norm_gather(): pl.pallas_call(col_proj_kernel, out_shape=jax.ShapeDtypeStruct((m, rows,...  35.9 us
    pallas_call x1, Pallas kernels, col_sum_norm(): pl.pallas_call(col_sum_ln_kernel, out_shape=jax.ShapeDtypeStruct(own.shap...  28.6 us
    pallas_call x1, Pallas kernels, seq_gather2(): pl.pallas_call(functools.partial(seq_gather2_kernel, group), out_shape=ja...  23.5 us
    pallas_call x1, Pallas kernels, seq_merge2(): pl.pallas_call(functools.partial(seq_merge2_kernel, group, top_lane), out...  20.1 us
    all_to_all x1, starting transfers between devices, per_device(): lax.all_to_all(outgoing, 'seq', split_axis=0, concat_axis=0, tiled=True)  11.3 us
    dot_general x1, matrix products, per_device(): ffn_full = jnp.dot(ffn_hidden, f_out, preferred_element_type=jnp.float32)  10.1 us
    unnamed x38, local copies, waits for them, and re-layouts  7.16 us
    reduce_sum x2, other arithmetic, per_device(): total = jnp.sum(e_win, axis=2) + jnp.sum(e_glob, axis=2)  5.17 us
  transfers between devices with their start and end apart: 6, of which 2 were waited for; matrix products, arithmetic and copies ran while one was open for 21% of the time, Pallas kernels for 37%

profile of v15, /device:TPU:1, one launch (start us, length us, event | category | flops | bytes accessed | tf_op | source)
XLA Modules:
  0.0 213.8 jit_solution(13203058611224152229)
XLA Ops:
  8.6 2.0 pad_maximum_fusion.1
  13.8 1.4 reshape.160
  16.8 2.6 %reshape.161 = bf16[32,2,16,4,128]{4,3,2,1,0:T(4,128)(2,1)} reshape(bf16[64,8192]{1,0:T(8,128)(2,1)} %convolution_convert_fusion) | data formatting | bytes 2097152 | tf_op jit(solution)/shard_map/reshape | solution.py:747
  19.4 11.3 %all-to-all-start = ((bf16[32,2,16,4,128]{4,3,2,1,0:T(4,128)(2,1)}), bf16[32,2,16,4,128]{4,3,2,1,0:T(4,128)(2,1)}, u32[]{:S(2)}, u32[]{:S(2)}) async-start(bf16[32,2,16,4,128]{4,3,2,1,0:T(4,128)(2,1)} %reshape.161), calls=%async_computation | async-start | bytes 2097152 | tf_op jit(solution)/shard_map/all_to_all | solution.py:748
  31.6 2.3 %collective-permute-start.1 = (bf16[256,4,128]{0,2,1:T(8,128)(2,1)}, bf16[256,4,128]{0,2,1:T(8,128)(2,1)}, u32[]{:S(2)}, u32[]{:S(2)}) collective-permute-start(bf16[256,4,128]{0,2,1:T(8,128)(2,1)} %get-tuple-element.11), channel_id=1, source_target_pairs={{16,0},{32,16},{48,32},{64,48},{80,64},{96,80},{112,96},{128,112},... | collective-permute-start | bytes 786440 | tf_op jit(solution)/shard_map/ppermute | solution.py:24
  33.9 3.4 %collective-permute-start = (bf16[256,4,128]{0,2,1:T(8,128)(2,1)}, bf16[256,4,128]{0,2,1:T(8,128)(2,1)}, u32[]{:S(2)}, u32[]{:S(2)}) collective-permute-start(bf16[256,4,128]{0,2,1:T(8,128)(2,1)} %get-tuple-element.10), channel_id=1, source_target_pairs={{0,16},{16,32},{32,48},{48,64},{64,80},{80,96},{96,112},{112,128},... | collective-permute-start | bytes 786440 | tf_op jit(solution)/shard_map/ppermute | solution.py:21
  37.5 1.5 convolution_convert_fusion.5
  41.2 23.5 %shard_map.140 = bf16[32,32,128]{2,1,0:T(8,128)(2,1)} custom-call(bf16[32,128]{1,0:T(8,128)(2,1)} %reshape.162.x_ref), custom_call_target="tpu_custom_call" | custom-call | tf_op jit(solution)/shard_map/pallas_call | solution.py:290
  64.8 1.8 reshape.163
  70.5 4.8 %select_reduce_fusion = (f32[4,512]{1,0:T(4,128)S(1)}, f32[4,512,1024]{2,1,0:T(8,128)}) fusion(pred[512,1024]{1,0:T(8,128)(4,1)S(1)} %fusion.17, bf16[1024,4,128]{0,2,1:T(8,128)(2,1)S(1)} %pad_maximum_fusion, bf16[512,4,192]{0,2,1:T(8,128)(2,1)S(1)} %bitcast.90), kind=kOutput, calls=%fused_computation.3 | convolution fusion | flops 274724864 | bytes 9707520 | tf_op jit(solution)/shard_map/qhd,khd->hqk/dot_general | solution.py:823
  78.1 5.0 %fusion = f32[4,512]{1,0:T(4,128)S(1)} fusion(f32[4,512,1024]{2,1,0:T(8,128)} %get-tuple-element.13, f32[4,512]{1,0:T(4,128)S(1)} %max.7, pred[512,1024]{1,0:T(8,128)(4,1)S(1)} %fusion.17), kind=kLoop, calls=%fused_computation.4 | loop fusion | flops 8386560 | bytes 8929280 | tf_op jit(solution)/shard_map/reduce_sum | solution.py:836
  83.3 1.5 fusion.81
  84.7 2.9 %fusion.70 = bf16[512,4,64]{0,2,1:T(8,128)(2,1)} fusion(f32[4,64,512]{2,1,0:T(8,128)S(1)} %fusion.81, f32[4,512,1024]{2,1,0:T(8,128)S(1)} %copy-done.4, f32[4,512]{1,0:T(4,128)S(1)} %max.7, pred[512,1024]{1,0:T(8,128)(4,1)S(1)} %fusion.17, bf16[1024,4,128]{0,2,1:T(8,128)(2,1)S(1)} %copy-done.10, f32[512,4]{0,1:T(4,128)S(1)} %add_bitcast_fusion), kind=kOutput, calls=%fused_computation.87 | convolution fusion | flops 277217280 | bytes 10240000 | tf_op jit(solution)/shard_map/hqk,khd->qhd/dot_general | solution.py:837
  87.6 1.9 fusion.28
  89.7 2.4 %convolution_convert_fusion.1 = bf16[768,512]{1,0:T(8,128)(2,1)S(1)} fusion(bf16[1024,1792]{1,0:T(8,128)(2,1)} %all-gather.4.cloned.1.call-done, bf16[1,512,1024]{2,1,0:T(8,128)(2,1)S(1)} %copy-done.8), kind=kOutput, calls=%fused_computation.32 | convolution fusion | flops 805699584 | bytes 3407872 | tf_op jit(solution)/shard_map/dot_general | solution.py:766
  94.9 20.1 %shard_map.141 = f32[16,128]{1,0:T(8,128)} custom-call(f32[32,16,128]{2,1,0:T(8,128)} %bitcast.94), custom_call_target="tpu_custom_call" | custom-call | tf_op jit(solution)/shard_map/pallas_call | solution.py:353
  118.3 4.9 %all-gather.6.cloned.1.call-done.w_hbm = bf16[1024,1024]{1,0:T(8,128)(2,1)} async-done(((bf16[256,1024]{1,0:T(8,128)(2,1)}), bf16[1024,1024]{1,0:T(8,128)(2,1)}) %all-gather.6.cloned.1.call-update) | async-done | bytes 2097168 | tf_op jit(solution)/shard_map/all_gather | solution.py:719
  123.3 1.6 copy-done.1
  124.9 35.9 %shard_map.142 = bf16[4,128,1024]{2,1,0:T(8,128)(2,1)S(1)} custom-call(bf16[4,128,256]{2,1,0:T(8,128)(2,1)S(1)} %copy.50.x_ref, f32[128,1024]{1,0:T(8,128)S(1)} %convolution_add_fusion.own_ref, bf16[1024,1024]{1,0:T(8,128)(2,1)S(1)} %copy-done.1, f32[1,1024]{1,0:T(1,128)S(1)} %bitcast.84, f32[1,1024]{1,0:T(1,128)S(1)} %bitcast.85), custom_call_target="tpu_custom_call" | custom-call | tf_op jit(solution)/shard_map/pallas_call | solution.py:586
  162.1 10.1 %fusion.150 = (bf16[512,1024]{1,0:T(8,128)(2,1)}, f32[512,1024]{1,0:T(8,128)}) fusion(bf16[1024,1024]{1,0:T(8,128)(2,1)} %all-gather.8.cloned.1.call-done, bf16[512,1024]{1,0:T(8,128)(2,1)S(1)} %bitcast.83, bf16[1024,1792]{1,0:T(8,128)(2,1)} %all-gather.4.cloned.1.call-done), kind=kOutput, calls=%fused_computation.182 | convolution fusion | flops 2182086656 | bytes 8388608 | tf_op jit(solution)/shard_map/dot_general | solution.py:870
  172.2 1.9 convert_add_fusion.own_ref
  174.1 28.6 %shard_map.143 = bf16[128,1024]{1,0:T(8,128)(2,1)} custom-call(bf16[4,128,1024]{2,1,0:T(8,128)(2,1)} %bitcast.92, f32[128,1024]{1,0:T(8,128)} %convert_add_fusion.own_ref, f32[1,1024]{1,0:T(1,128)} %bitcast.106, f32[1,1024]{1,0:T(1,128)} %bitcast.107), custom_call_target="tpu_custom_call" | custom-call | tf_op jit(solution)/shard_map/pallas_call | solution.py:644
  202.7 1.7 copy.63
  204.4 2.8 %copy.64 = bf16[1,1,32,2,16,4,128]{6,5,4,3,2,1,0:T(4,128)(2,1)} copy(bf16[1,1,32,2,16,4,128]{6,5,4,3,2,1,0:T(4,128)(2,1)} %bitcast.38) | data formatting | bytes 2097152
  (91 shorter events, 23.6 us)
Async XLA Ops:
  7.2 4.2 %copy-start = (bf16[1024,4,192]{0,2,1:T(8,128)(2,1)S(1)}, bf16[1024,4,192]{0,2,1:T(8,128)(2,1)}, u32[]{:S(2)}) copy-start(bf16[1024,4,192]{0,2,1:T(8,128)(2,1)} %param.14) | copy-start | bytes 4718596
  7.2 4.2 %copy-start.7 = (bf16[1,512,1024]{2,1,0:T(8,128)(2,1)S(1)}, bf16[1,512,1024]{2,1,0:T(8,128)(2,1)}, u32[]{:S(2)}) copy-start(bf16[1,512,1024]{2,1,0:T(8,128)(2,1)} %param.13) | copy-start | bytes 3145732
  7.2 80.5 %all-gather.4.cloned.1.call-start = ((), (), s32[]{:S(2)}) async-start(), calls=%async_computation.1 | async-start | bytes 4587520 | tf_op jit(solution)/shard_map/all_gather | solution.py:708
  10.6 112.7 %all-gather.6.cloned.1.call-start = ((), (), s32[]{:S(2)}) async-start(), calls=%async_computation.2 | async-start | bytes 2621440 | tf_op jit(solution)/shard_map/all_gather | solution.py:719
  12.4 2.8 %copy-start.15 = (s32[1,32,1]{1,2,0:T(1,128)S(1)}, s32[1,32,1]{1,2,0:T(1,128)}, u32[]{:S(2)}) copy-start(s32[1,32,1]{1,2,0:T(1,128)} %param.25) | copy-start | bytes 388
  19.4 17.9 %copy-start.14 = (s32[1,128]{1,0:T(1,128)S(1)}, s32[1,128]{1,0:T(1,128)}, u32[]{:S(2)}) copy-start(s32[1,128]{1,0:T(1,128)} %param.24) | copy-start | bytes 1540
  19.4 19.6 %copy-start.5 = (s32[1,16384]{1,0:T(1,128)S(1)}, s32[1,16384]{1,0:T(1,128)}, u32[]{:S(2)}) copy-start(s32[1,16384]{1,0:T(1,128)} %param.23) | copy-start | bytes 196612
  19.4 55.9 %all-to-all-start = ((bf16[32,2,16,4,128]{4,3,2,1,0:T(4,128)(2,1)}), bf16[32,2,16,4,128]{4,3,2,1,0:T(4,128)(2,1)}, u32[]{:S(2)}, u32[]{:S(2)}) async-start(bf16[32,2,16,4,128]{4,3,2,1,0:T(4,128)(2,1)} %reshape.161), calls=%async_computation | async-start | bytes 2097152 | tf_op jit(solution)/shard_map/all_to_all | solution.py:748
  30.7 131.4 %all-gather.8.cloned.1.call-start = ((), (), s32[]{:S(2)}) async-start(), calls=%async_computation.3 | async-start | bytes 2621440 | tf_op jit(solution)/shard_map/all_gather | solution.py:718
  31.6 36.7 %collective-permute-start.1 = (bf16[256,4,128]{0,2,1:T(8,128)(2,1)}, bf16[256,4,128]{0,2,1:T(8,128)(2,1)}, u32[]{:S(2)}, u32[]{:S(2)}) collective-permute-start(bf16[256,4,128]{0,2,1:T(8,128)(2,1)} %get-tuple-element.11), channel_id=1, source_target_pairs={{16,0},{32,16},{48,32},{64,48},{80,64},{96,80},{112,96},{128,112},... | collective-permute-start | bytes 786440 | tf_op jit(solution)/shard_map/ppermute | solution.py:24
  33.9 34.4 %collective-permute-start = (bf16[256,4,128]{0,2,1:T(8,128)(2,1)}, bf16[256,4,128]{0,2,1:T(8,128)(2,1)}, u32[]{:S(2)}, u32[]{:S(2)}) collective-permute-start(bf16[256,4,128]{0,2,1:T(8,128)(2,1)} %get-tuple-element.10), channel_id=1, source_target_pairs={{0,16},{16,32},{32,48},{48,64},{64,80},{80,96},{96,112},{112,128},... | collective-permute-start | bytes 786440 | tf_op jit(solution)/shard_map/ppermute | solution.py:21
  37.5 30.0 %copy-start.12 = (s32[4]{0:T(128)}, s32[4]{0:T(128)S(1)}, u32[]{:S(2)}) copy-start(s32[4]{0:T(128)S(1)} %fusion.112) | copy-start | bytes 52
  69.5 1.0 copy-start.9
  70.5 4.8 %copy-start.11 = (bf16[128,1024]{1,0:T(8,128)(2,1)S(1)}, bf16[128,1024]{1,0:T(8,128)(2,1)}, u32[]{:S(2)}) copy-start(bf16[128,1024]{1,0:T(8,128)(2,1)} %reshape.163) | copy-start | bytes 786436
  78.0 6.7 %copy-start.4 = (f32[4,512,1024]{2,1,0:T(8,128)S(1)}, f32[4,512,1024]{2,1,0:T(8,128)}, u32[]{:S(2)}) copy-start(f32[4,512,1024]{2,1,0:T(8,128)} %get-tuple-element.13) | copy-start | bytes 25165828
  83.0 1.7 copy-start.10
  87.6 2.0 copy-start.8
  92.6 23.2 %copy-start.13 = (s32[4]{0:T(128)S(1)}, s32[4]{0:T(128)}, u32[]{:S(2)}) copy-start(s32[4]{0:T(128)} %copy-done.12) | copy-start | bytes 52
  92.6 23.2 %copy-start.16 = (pred[512]{0:T(512)(128)(4,1)S(1)}, pred[512]{0:T(512)(128)(4,1)}, u32[]{:S(2)}) copy-start(pred[512]{0:T(512)(128)(4,1)} %fusion.103) | copy-start | bytes 1540
  92.6 23.2 %copy-start.17 = (bf16[512,4,64]{0,2,1:T(8,128)(2,1)S(1)}, bf16[512,4,64]{0,2,1:T(8,128)(2,1)}, u32[]{:S(2)}) copy-start(bf16[512,4,64]{0,2,1:T(8,128)(2,1)} %fusion.70) | copy-start | bytes 786436
  93.0 24.2 %copy-start.6 = (bf16[256,1024]{1,0:T(8,128)(2,1)S(1)}, bf16[256,1024]{1,0:T(8,128)(2,1)}, u32[]{:S(2)}) copy-start(bf16[256,1024]{1,0:T(8,128)(2,1)} %param.16) | copy-start | bytes 1572868
  94.0 29.3 %copy-start.2 = (f32[1024]{0:T(1024)S(1)}, f32[1024]{0:T(1024)}, u32[]{:S(2)}) copy-start(f32[1024]{0:T(1024)} %param.17) | copy-start | bytes 12292
  94.0 29.3 %copy-start.3 = (f32[1024]{0:T(1024)S(1)}, f32[1024]{0:T(1024)}, u32[]{:S(2)}) copy-start(f32[1024]{0:T(1024)} %param.18) | copy-start | bytes 12292
  123.3 1.6 copy-start.1
Sparse Core Ops, SparseCore 0:
  10.7 54.7 all-gather.3
  67.6 55.6 all-gather.5
  125.4 36.6 all-gather.7

commit v16 on v15

--- a/solution.py
+++ b/solution.py
@@ -643,7 +643,7 @@
     rows, width = own.shape
     return pl.pallas_call(
         col_sum_ln_kernel,
-        out_shape=jax.ShapeDtypeStruct(own.shape, jnp.bfloat16),
+        out_shape=jax.ShapeDtypeStruct(own.shape, jnp.float32),
         in_specs=[pl.BlockSpec(memory_space=pltpu.VMEM)] * 4,
         out_specs=pl.BlockSpec(memory_space=pltpu.VMEM),
         scratch_shapes=[
@@ -875,7 +875,7 @@
         ln2_gain,
         ln2_bias,
     )
-    return (normed[None], page_pool)
+    return (normed.astype(jnp.bfloat16)[None], page_pool)
 
 
 def solution(mesh):

time: 218 us -> 218 us (level)
    unnamed x38 -> x37, local copies, waits for them, and re-layouts: 7.16 us -> 5.49 us
where the time goes in v16:
time: 218 us; the launch traced here: 214 us
  Pallas kernels  108 us (50%)
  matrix products  33.1 us (15%)
  local copies, waits for them, and re-layouts  19.5 us (9%)
  starting transfers between devices  17.1 us (8%)
  other arithmetic  14.9 us (7%)
  between operations  14.2 us (7%)
  waiting for transfers between devices  6.96 us (3%)
    pallas_call x1, Pallas kernels, col_proj_norm_gather(): pl.pallas_call(col_proj_kernel, out_shape=jax.ShapeDtypeStruct((m, rows,...  35.9 us
    pallas_call x1, Pallas kernels, col_sum_norm(): pl.pallas_call(col_sum_ln_kernel, out_shape=jax.ShapeDtypeStruct(own.shap...  28.6 us
    pallas_call x1, Pallas kernels, seq_gather2(): pl.pallas_call(functools.partial(seq_gather2_kernel, group), out_shape=ja...  23.5 us
    pallas_call x1, Pallas kernels, seq_merge2(): pl.pallas_call(functools.partial(seq_merge2_kernel, group, top_lane), out...  20.1 us
    all_to_all x1, starting transfers between devices, per_device(): lax.all_to_all(outgoing, 'seq', split_axis=0, concat_axis=0, tiled=True)  11.3 us
    dot_general x1, matrix products, per_device(): ffn_full = jnp.dot(ffn_hidden, f_out, preferred_element_type=jnp.float32)  10.1 us
    unnamed x37, local copies, waits for them, and re-layouts  5.49 us
    reduce_sum x2, other arithmetic, per_device(): total = jnp.sum(e_win, axis=2) + jnp.sum(e_glob, axis=2)  5.17 us
  transfers between devices with their start and end apart: 6, of which 2 were waited for; matrix products, arithmetic and copies ran while one was open for 21% of the time, Pallas kernels for 37%

profile of v16, /device:TPU:1, one launch (start us, length us, event | category | flops | bytes accessed | tf_op | source)
XLA Modules:
  0.0 213.9 jit_solution(9412687401745643811)
XLA Ops:
  8.6 2.0 pad_maximum_fusion.1
  13.8 1.4 reshape.160
  16.8 2.6 %reshape.161 = bf16[32,2,16,4,128]{4,3,2,1,0:T(4,128)(2,1)} reshape(bf16[64,8192]{1,0:T(8,128)(2,1)} %convolution_convert_fusion) | data formatting | bytes 2097152 | tf_op jit(solution)/shard_map/reshape | solution.py:747
  19.4 11.3 %all-to-all-start = ((bf16[32,2,16,4,128]{4,3,2,1,0:T(4,128)(2,1)}), bf16[32,2,16,4,128]{4,3,2,1,0:T(4,128)(2,1)}, u32[]{:S(2)}, u32[]{:S(2)}) async-start(bf16[32,2,16,4,128]{4,3,2,1,0:T(4,128)(2,1)} %reshape.161), calls=%async_computation | async-start | bytes 2097152 | tf_op jit(solution)/shard_map/all_to_all | solution.py:748
  31.6 2.3 %collective-permute-start.1 = (bf16[256,4,128]{0,2,1:T(8,128)(2,1)}, bf16[256,4,128]{0,2,1:T(8,128)(2,1)}, u32[]{:S(2)}, u32[]{:S(2)}) collective-permute-start(bf16[256,4,128]{0,2,1:T(8,128)(2,1)} %get-tuple-element.11), channel_id=1, source_target_pairs={{16,0},{32,16},{48,32},{64,48},{80,64},{96,80},{112,96},{128,112},... | collective-permute-start | bytes 786440 | tf_op jit(solution)/shard_map/ppermute | solution.py:24
  33.9 3.4 %collective-permute-start = (bf16[256,4,128]{0,2,1:T(8,128)(2,1)}, bf16[256,4,128]{0,2,1:T(8,128)(2,1)}, u32[]{:S(2)}, u32[]{:S(2)}) collective-permute-start(bf16[256,4,128]{0,2,1:T(8,128)(2,1)} %get-tuple-element.10), channel_id=1, source_target_pairs={{0,16},{16,32},{32,48},{48,64},{64,80},{80,96},{96,112},{112,128},... | collective-permute-start | bytes 786440 | tf_op jit(solution)/shard_map/ppermute | solution.py:21
  37.5 1.5 convolution_convert_fusion.5
  41.2 23.5 %shard_map.140 = bf16[32,32,128]{2,1,0:T(8,128)(2,1)} custom-call(bf16[32,128]{1,0:T(8,128)(2,1)} %reshape.162.x_ref), custom_call_target="tpu_custom_call" | custom-call | tf_op jit(solution)/shard_map/pallas_call | solution.py:290
  64.8 1.8 reshape.163
  70.5 4.8 %select_reduce_fusion = (f32[4,512]{1,0:T(4,128)S(1)}, f32[4,512,1024]{2,1,0:T(8,128)}) fusion(pred[512,1024]{1,0:T(8,128)(4,1)S(1)} %fusion.17, bf16[1024,4,128]{0,2,1:T(8,128)(2,1)S(1)} %pad_maximum_fusion, bf16[512,4,192]{0,2,1:T(8,128)(2,1)S(1)} %bitcast.91), kind=kOutput, calls=%fused_computation.3 | convolution fusion | flops 274724864 | bytes 9707520 | tf_op jit(solution)/shard_map/qhd,khd->hqk/dot_general | solution.py:823
  78.1 5.0 %fusion = f32[4,512]{1,0:T(4,128)S(1)} fusion(f32[4,512,1024]{2,1,0:T(8,128)} %get-tuple-element.13, f32[4,512]{1,0:T(4,128)S(1)} %max.7, pred[512,1024]{1,0:T(8,128)(4,1)S(1)} %fusion.17), kind=kLoop, calls=%fused_computation.4 | loop fusion | flops 8386560 | bytes 8929280 | tf_op jit(solution)/shard_map/reduce_sum | solution.py:836
  83.3 1.5 fusion.81
  84.7 2.9 %fusion.70 = bf16[512,4,64]{0,2,1:T(8,128)(2,1)} fusion(f32[4,64,512]{2,1,0:T(8,128)S(1)} %fusion.81, f32[4,512,1024]{2,1,0:T(8,128)S(1)} %copy-done.4, f32[4,512]{1,0:T(4,128)S(1)} %max.7, pred[512,1024]{1,0:T(8,128)(4,1)S(1)} %fusion.17, bf16[1024,4,128]{0,2,1:T(8,128)(2,1)S(1)} %copy-done.10, f32[512,4]{0,1:T(4,128)S(1)} %add_bitcast_fusion), kind=kOutput, calls=%fused_computation.87 | convolution fusion | flops 277217280 | bytes 10240000 | tf_op jit(solution)/shard_map/hqk,khd->qhd/dot_general | solution.py:837
  87.6 1.9 fusion.28
  89.7 2.4 %convolution_convert_fusion.1 = bf16[768,512]{1,0:T(8,128)(2,1)S(1)} fusion(bf16[1024,1792]{1,0:T(8,128)(2,1)} %all-gather.4.cloned.1.call-done, bf16[1,512,1024]{2,1,0:T(8,128)(2,1)S(1)} %copy-done.8), kind=kOutput, calls=%fused_computation.32 | convolution fusion | flops 805699584 | bytes 3407872 | tf_op jit(solution)/shard_map/dot_general | solution.py:766
  94.9 20.1 %shard_map.141 = f32[16,128]{1,0:T(8,128)} custom-call(f32[32,16,128]{2,1,0:T(8,128)} %bitcast.94), custom_call_target="tpu_custom_call" | custom-call | tf_op jit(solution)/shard_map/pallas_call | solution.py:353
  118.3 4.9 %all-gather.6.cloned.1.call-done.w_hbm = bf16[1024,1024]{1,0:T(8,128)(2,1)} async-done(((bf16[256,1024]{1,0:T(8,128)(2,1)}), bf16[1024,1024]{1,0:T(8,128)(2,1)}) %all-gather.6.cloned.1.call-update) | async-done | bytes 2097168 | tf_op jit(solution)/shard_map/all_gather | solution.py:719
  123.3 1.6 copy-done.1
  124.9 35.9 %shard_map.142 = bf16[4,128,1024]{2,1,0:T(8,128)(2,1)S(1)} custom-call(bf16[4,128,256]{2,1,0:T(8,128)(2,1)S(1)} %copy.50.x_ref, f32[128,1024]{1,0:T(8,128)S(1)} %convolution_add_fusion.own_ref, bf16[1024,1024]{1,0:T(8,128)(2,1)S(1)} %copy-done.1, f32[1,1024]{1,0:T(1,128)S(1)} %bitcast.85, f32[1,1024]{1,0:T(1,128)S(1)} %bitcast.86), custom_call_target="tpu_custom_call" | custom-call | tf_op jit(solution)/shard_map/pallas_call | solution.py:586
  162.1 10.1 %fusion.150 = (bf16[512,1024]{1,0:T(8,128)(2,1)}, f32[512,1024]{1,0:T(8,128)}) fusion(bf16[1024,1024]{1,0:T(8,128)(2,1)} %all-gather.8.cloned.1.call-done, bf16[512,1024]{1,0:T(8,128)(2,1)S(1)} %bitcast.84, bf16[1024,1792]{1,0:T(8,128)(2,1)} %all-gather.4.cloned.1.call-done), kind=kOutput, calls=%fused_computation.183 | convolution fusion | flops 2182086656 | bytes 8388608 | tf_op jit(solution)/shard_map/dot_general | solution.py:870
  172.2 1.9 convert_add_fusion.own_ref
  174.1 28.6 %shard_map.143 = f32[128,1024]{1,0:T(8,128)} custom-call(bf16[4,128,1024]{2,1,0:T(8,128)(2,1)} %bitcast.93, f32[128,1024]{1,0:T(8,128)} %convert_add_fusion.own_ref, f32[1,1024]{1,0:T(1,128)} %bitcast.106, f32[1,1024]{1,0:T(1,128)} %bitcast.107), custom_call_target="tpu_custom_call" | custom-call | tf_op jit(solution)/shard_map/pallas_call | solution.py:644
  202.8 1.8 convert_bitcast_fusion
  204.6 2.8 %copy.62 = bf16[1,1,32,2,16,4,128]{6,5,4,3,2,1,0:T(4,128)(2,1)} copy(bf16[1,1,32,2,16,4,128]{6,5,4,3,2,1,0:T(4,128)(2,1)} %bitcast.38) | data formatting | bytes 2097152
  (91 shorter events, 23.6 us)
Async XLA Ops:
  7.2 4.2 %copy-start = (bf16[1024,4,192]{0,2,1:T(8,128)(2,1)S(1)}, bf16[1024,4,192]{0,2,1:T(8,128)(2,1)}, u32[]{:S(2)}) copy-start(bf16[1024,4,192]{0,2,1:T(8,128)(2,1)} %param.14) | copy-start | bytes 4718596
  7.2 4.2 %copy-start.7 = (bf16[1,512,1024]{2,1,0:T(8,128)(2,1)S(1)}, bf16[1,512,1024]{2,1,0:T(8,128)(2,1)}, u32[]{:S(2)}) copy-start(bf16[1,512,1024]{2,1,0:T(8,128)(2,1)} %param.13) | copy-start | bytes 3145732
  7.2 80.5 %all-gather.4.cloned.1.call-start = ((), (), s32[]{:S(2)}) async-start(), calls=%async_computation.1 | async-start | bytes 4587520 | tf_op jit(solution)/shard_map/all_gather | solution.py:708
  10.6 112.7 %all-gather.6.cloned.1.call-start = ((), (), s32[]{:S(2)}) async-start(), calls=%async_computation.2 | async-start | bytes 2621440 | tf_op jit(solution)/shard_map/all_gather | solution.py:719
  12.4 2.8 %copy-start.15 = (s32[1,32,1]{1,2,0:T(1,128)S(1)}, s32[1,32,1]{1,2,0:T(1,128)}, u32[]{:S(2)}) copy-start(s32[1,32,1]{1,2,0:T(1,128)} %param.25) | copy-start | bytes 388
  19.4 17.9 %copy-start.14 = (s32[1,128]{1,0:T(1,128)S(1)}, s32[1,128]{1,0:T(1,128)}, u32[]{:S(2)}) copy-start(s32[1,128]{1,0:T(1,128)} %param.24) | copy-start | bytes 1540
  19.4 19.6 %copy-start.5 = (s32[1,16384]{1,0:T(1,128)S(1)}, s32[1,16384]{1,0:T(1,128)}, u32[]{:S(2)}) copy-start(s32[1,16384]{1,0:T(1,128)} %param.23) | copy-start | bytes 196612
  19.4 55.9 %all-to-all-start = ((bf16[32,2,16,4,128]{4,3,2,1,0:T(4,128)(2,1)}), bf16[32,2,16,4,128]{4,3,2,1,0:T(4,128)(2,1)}, u32[]{:S(2)}, u32[]{:S(2)}) async-start(bf16[32,2,16,4,128]{4,3,2,1,0:T(4,128)(2,1)} %reshape.161), calls=%async_computation | async-start | bytes 2097152 | tf_op jit(solution)/shard_map/all_to_all | solution.py:748
  30.7 131.4 %all-gather.8.cloned.1.call-start = ((), (), s32[]{:S(2)}) async-start(), calls=%async_computation.3 | async-start | bytes 2621440 | tf_op jit(solution)/shard_map/all_gather | solution.py:718
  31.6 36.7 %collective-permute-start.1 = (bf16[256,4,128]{0,2,1:T(8,128)(2,1)}, bf16[256,4,128]{0,2,1:T(8,128)(2,1)}, u32[]{:S(2)}, u32[]{:S(2)}) collective-permute-start(bf16[256,4,128]{0,2,1:T(8,128)(2,1)} %get-tuple-element.11), channel_id=1, source_target_pairs={{16,0},{32,16},{48,32},{64,48},{80,64},{96,80},{112,96},{128,112},... | collective-permute-start | bytes 786440 | tf_op jit(solution)/shard_map/ppermute | solution.py:24
  33.9 34.4 %collective-permute-start = (bf16[256,4,128]{0,2,1:T(8,128)(2,1)}, bf16[256,4,128]{0,2,1:T(8,128)(2,1)}, u32[]{:S(2)}, u32[]{:S(2)}) collective-permute-start(bf16[256,4,128]{0,2,1:T(8,128)(2,1)} %get-tuple-element.10), channel_id=1, source_target_pairs={{0,16},{16,32},{32,48},{48,64},{64,80},{80,96},{96,112},{112,128},... | collective-permute-start | bytes 786440 | tf_op jit(solution)/shard_map/ppermute | solution.py:21
  37.5 30.0 %copy-start.12 = (s32[4]{0:T(128)}, s32[4]{0:T(128)S(1)}, u32[]{:S(2)}) copy-start(s32[4]{0:T(128)S(1)} %fusion.112) | copy-start | bytes 52
  69.5 1.0 copy-start.9
  70.5 4.8 %copy-start.11 = (bf16[128,1024]{1,0:T(8,128)(2,1)S(1)}, bf16[128,1024]{1,0:T(8,128)(2,1)}, u32[]{:S(2)}) copy-start(bf16[128,1024]{1,0:T(8,128)(2,1)} %reshape.163) | copy-start | bytes 786436
  78.0 6.7 %copy-start.4 = (f32[4,512,1024]{2,1,0:T(8,128)S(1)}, f32[4,512,1024]{2,1,0:T(8,128)}, u32[]{:S(2)}) copy-start(f32[4,512,1024]{2,1,0:T(8,128)} %get-tuple-element.13) | copy-start | bytes 25165828
  83.0 1.7 copy-start.10
  87.6 2.0 copy-start.8
  92.6 23.2 %copy-start.13 = (s32[4]{0:T(128)S(1)}, s32[4]{0:T(128)}, u32[]{:S(2)}) copy-start(s32[4]{0:T(128)} %copy-done.12) | copy-start | bytes 52
  92.6 23.2 %copy-start.16 = (pred[512]{0:T(512)(128)(4,1)S(1)}, pred[512]{0:T(512)(128)(4,1)}, u32[]{:S(2)}) copy-start(pred[512]{0:T(512)(128)(4,1)} %fusion.103) | copy-start | bytes 1540
  92.6 23.2 %copy-start.17 = (bf16[512,4,64]{0,2,1:T(8,128)(2,1)S(1)}, bf16[512,4,64]{0,2,1:T(8,128)(2,1)}, u32[]{:S(2)}) copy-start(bf16[512,4,64]{0,2,1:T(8,128)(2,1)} %fusion.70) | copy-start | bytes 786436
  93.0 24.2 %copy-start.6 = (bf16[256,1024]{1,0:T(8,128)(2,1)S(1)}, bf16[256,1024]{1,0:T(8,128)(2,1)}, u32[]{:S(2)}) copy-start(bf16[256,1024]{1,0:T(8,128)(2,1)} %param.16) | copy-start | bytes 1572868
  94.0 29.3 %copy-start.2 = (f32[1024]{0:T(1024)S(1)}, f32[1024]{0:T(1024)}, u32[]{:S(2)}) copy-start(f32[1024]{0:T(1024)} %param.17) | copy-start | bytes 12292
  94.0 29.3 %copy-start.3 = (f32[1024]{0:T(1024)S(1)}, f32[1024]{0:T(1024)}, u32[]{:S(2)}) copy-start(f32[1024]{0:T(1024)} %param.18) | copy-start | bytes 12292
  123.3 1.6 copy-start.1
Sparse Core Ops, SparseCore 0:
  10.7 54.7 all-gather.3
  67.6 55.6 all-gather.5
  125.4 36.6 all-gather.7
